TPU v7x, 32 devices: a whole 2x2x4 slice. The times are simulated.
32 devices in a mesh: seq: 8 (over z, y), slide: 4 (over x, core).
Axes of the slice: x: 2, y: 2, z: 4, core: 2. Of those that a mesh axis runs over, the one named last changes fastest.
Arguments:
- tiles: bfloat16 [40960, 768], P(('seq', 'slide')), may hold values from -6 to 6
- dest_table: int32 [40960], P(('seq', 'slide')), may hold values from -1 to 16383, as said below
- owner_row: int32 [4, 4096], P('slide', 'seq'), may hold values from 0 to 40959, as said below
- w_qkv: bfloat16 [768, 2304], replicated, may hold values from -6 to 6, as said below
- w_out: bfloat16 [768, 768], replicated, may hold values from -0.21875 to 0.21875
- gain_attn: float32 [768], replicated, may hold values from 0.1 to 1.9
- gain_out: float32 [768], replicated, may hold values from 0.1 to 1.9
Outputs:
- predicted: bfloat16 [40960, 768], P(('seq', 'slide'))
Inputs may be any that keep to these rules, and one draw needn't show every extreme that they name: `dest_table`: for each tile row its student position g * 4096 + p, or -1 for a masked row; every position is named by exactly one row. The rows of one device that go to one student device (the positions of group g with the same p // 512) number 0 or exactly 32, and each student device receives rows from exactly half of all devices. `owner_row`: the tile row held at each student position: the inverse of dest_table. `w_qkv`: heads side by side in each projection.
All inputs are finite; a program needn't handle non-finite values.
Results may differ from a plain program's by a relative error of at most 0.0045.
Values may be sent and summed in bfloat16 or wider, within the bound.
No kernel may reach another device: no remote copies, remote signals or barrier semaphores. Data moves between devices by JAX's collectives and lax.ppermute only.
A program may use at most 128 MiB of HBM per device.

v0:
```python
import jax
import jax.numpy as jnp
from jax import lax
from jax.sharding import PartitionSpec as P

HEADS = 12
HDIM = 64
SEG = 2048


EPS = 1e-05


def from_partner(value, axis, apart):
    mask = 2**apart
    pairs = [(source, source ^ mask) for source in range(lax.axis_size(axis))]
    return lax.ppermute(value, axis, pairs)


def layer_norm(inputs, gain):
    average = jnp.mean(inputs, axis=-1, keepdims=True)
    centred = inputs - average
    spread = jnp.mean(centred * centred, axis=-1, keepdims=True)
    return centred * lax.rsqrt(spread + EPS) * gain


def attend_block(queries, keys, values):
    scores = jnp.einsum("...qd,...kd->...qk", queries, keys, preferred_element_type=jnp.float32)
    peak = jnp.max(scores, axis=-1, keepdims=True)
    weights = jnp.exp(scores - peak)
    total = jnp.sum(weights, axis=-1, keepdims=True)
    mixed = jnp.einsum(
        "...qk,...kd->...qd",
        weights.astype(jnp.bfloat16),
        values,
        preferred_element_type=jnp.float32,
    )
    return (mixed / total, peak[..., 0] + jnp.log(total[..., 0]))


def segment_block(keys, values):
    visible, heads, width = keys.shape
    group = SEG // visible
    block = jnp.stack(
        [keys.reshape(visible, heads * width), values.reshape(visible, heads * width)]
    )
    position = lax.axis_index("seq")
    for bit in range(group.bit_length() - 1):
        partner = from_partner(block, "seq", bit)
        upper = position // (1 << bit) % 2 == 1
        block = jnp.where(
            upper,
            jnp.concatenate([partner, block], axis=1),
            jnp.concatenate([block, partner], axis=1),
        )
    return block.reshape(2, SEG, heads, width)


def local_branches(queries, keys, values):
    visible, heads, width = queries.shape
    block = segment_block(keys, values)
    query_heads = queries.transpose(1, 0, 2)
    key_heads = block[0].transpose(1, 0, 2)
    value_heads = block[1].transpose(1, 0, 2)

    def per_head(item):
        query_one, key_one, value_one = item
        mixed_list = []
        total_list = []
        for stride in (1, 2, 4):
            query_cls = query_one.reshape(visible // stride, stride, width).transpose(1, 0, 2)
            key_cls = key_one.reshape(SEG // stride, stride, width).transpose(1, 0, 2)
            value_cls = value_one.reshape(SEG // stride, stride, width).transpose(1, 0, 2)
            mixed, log_total = attend_block(query_cls, key_cls, value_cls)
            mixed_list.append(mixed.transpose(1, 0, 2).reshape(visible, width))
            total_list.append(log_total.transpose(1, 0).reshape(visible))
        return (jnp.stack(mixed_list), jnp.stack(total_list))

    mixed_all, total_all = lax.map(per_head, (query_heads, key_heads, value_heads))
    mixed_all = mixed_all.transpose(1, 2, 0, 3)
    total_all = total_all.transpose(1, 2, 0)
    return ([mixed_all[index] for index in range(3)], [total_all[index] for index in range(3)])


def far_heads(queries, keys, values, n_seq):
    visible, heads, width = queries.shape
    owned = heads * 8 // n_seq
    stacked = jnp.stack([queries, keys, values], axis=2)
    shaped = stacked.reshape(visible // 8, 8, heads, 3, width).transpose(0, 2, 1, 3, 4)
    shaped = shaped.reshape(visible // 8, n_seq, owned, 3, width).transpose(1, 2, 3, 0, 4)
    shaped = shaped.reshape(n_seq, owned, 3, visible // 8 * width)
    arrived = lax.all_to_all(shaped, "seq", split_axis=0, concat_axis=0, tiled=True)
    items = arrived.reshape(n_seq, owned, 3, visible // 8, width).transpose(1, 2, 0, 3, 4)
    items = items.reshape(owned, 3, n_seq * visible // 8, width)

    def solve(item):
        return attend_block(item[0], item[1], item[2])

    mixed, log_total = lax.map(solve, items)
    mixed = mixed.astype(jnp.bfloat16)
    outgoing = mixed.reshape(owned, n_seq, visible // 8, width).transpose(1, 0, 2, 3)
    outgoing = outgoing.reshape(n_seq, owned, visible // 8 * width)
    totals = log_total.reshape(owned, n_seq, visible // 8).transpose(1, 0, 2)
    returned = lax.all_to_all(outgoing, "seq", split_axis=0, concat_axis=0, tiled=True)
    returned_totals = lax.all_to_all(totals, "seq", split_axis=0, concat_axis=0, tiled=True)
    mixed_rows = returned.reshape(n_seq, owned, visible // 8, width).transpose(2, 0, 1, 3)
    mixed_rows = (
        mixed_rows.reshape(visible // 8, heads, 8, width)
        .transpose(0, 2, 1, 3)
        .reshape(visible, heads, width)
    )
    total_rows = returned_totals.transpose(2, 0, 1).reshape(visible // 8, heads, 8)
    total_rows = total_rows.transpose(0, 2, 1).reshape(visible, heads)
    return (mixed_rows.astype(jnp.float32), total_rows)


def encode(rows, w_qkv, w_out, gain_attn, gain_out, n_seq):
    visible, width_model = rows.shape
    normed = layer_norm(rows.astype(jnp.float32), gain_attn).astype(jnp.bfloat16)
    projected = jnp.dot(normed, w_qkv, preferred_element_type=jnp.float32)
    queries = (
        (projected[:, :width_model] * HDIM ** (-0.5))
        .astype(jnp.bfloat16)
        .reshape(visible, HEADS, HDIM)
    )
    keys = (
        projected[:, width_model : 2 * width_model]
        .astype(jnp.bfloat16)
        .reshape(visible, HEADS, HDIM)
    )
    values = projected[:, 2 * width_model :].astype(jnp.bfloat16).reshape(visible, HEADS, HDIM)
    outputs, totals = local_branches(queries, keys, values)
    far_mixed, far_total = far_heads(queries, keys, values, n_seq)
    outputs.append(far_mixed)
    totals.append(far_total)
    stacked = jnp.stack(outputs)
    stacked_totals = jnp.stack(totals)
    top = jnp.max(stacked_totals, axis=0)
    scale = jnp.exp(stacked_totals - top)
    combined = jnp.sum(scale[..., None] * stacked, axis=0) / jnp.sum(scale, axis=0)[..., None]
    attended = combined.reshape(visible, width_model).astype(jnp.bfloat16)
    hidden = rows.astype(jnp.float32) + jnp.dot(attended, w_out, preferred_element_type=jnp.float32)
    return layer_norm(hidden, gain_out).astype(jnp.bfloat16)


def route_rows(block):
    result = lax.all_to_all(block, ("seq", "slide"), split_axis=0, concat_axis=0, tiled=True)
    return result


def on_device(tiles, dest_table, owner_row, w_qkv, w_out, gain_attn, gain_out):
    n_seq = lax.axis_size("seq")
    n_slide = lax.axis_size("slide")
    devices = n_seq * n_slide
    count, width_model = tiles.shape
    visible = owner_row.shape[1]
    capacity = 2 * visible // devices
    seq_length = visible * n_seq
    valid = dest_table >= 0
    target = dest_table % seq_length // visible * n_slide + dest_table // seq_length
    target = jnp.where(valid, target, devices)
    chosen = (target[:, None] == jnp.arange(devices, dtype=jnp.int32)[None, :]).astype(jnp.int32)
    placing = jnp.sum(jnp.cumsum(chosen, axis=0) * chosen, axis=1) - 1
    send_slot = jnp.where(valid, target * capacity + placing, devices * capacity)
    outgoing = (
        jnp.zeros((devices * capacity, width_model), jnp.bfloat16)
        .at[send_slot]
        .set(tiles, mode="drop")
    )
    arrived = route_rows(outgoing.reshape(devices, capacity, width_model))
    arrived = arrived.reshape(devices * capacity, width_model)
    owners = owner_row[0]
    source = owners // count
    same_source = source[:, None] == source[None, :]
    earlier = owners[None, :] < owners[:, None]
    placed = jnp.sum((same_source & earlier).astype(jnp.int32), axis=1)
    slot = source * capacity + placed
    student = arrived[slot]
    predictions = encode(student, w_qkv, w_out, gain_attn, gain_out, n_seq)
    answers = jnp.zeros((devices * capacity, width_model), jnp.bfloat16).at[slot].set(predictions)
    returned = route_rows(answers.reshape(devices, capacity, width_model))
    returned = returned.reshape(devices * capacity, width_model)
    return jnp.take(returned, send_slot, axis=0, mode="fill", fill_value=0)


def solution(mesh):
    in_specs = (
        P(("seq", "slide"), None),
        P(("seq", "slide")),
        P("slide", "seq"),
        P(),
        P(),
        P(),
        P(),
    )
    out_specs = P(("seq", "slide"), None)
    return jax.shard_map(
        on_device, mesh=mesh, in_specs=in_specs, out_specs=out_specs, check_vma=False
    )
```

profile of v0, /device:TPU:0, one launch (start us, length us, event | category | flops | bytes accessed | tf_op | source)
XLA Modules:
  0.0 528.2 jit_solution(5111435874639750884)
XLA Ops:
  2.5 17.7 %reduce-window.6 = s32[32,10,128]{2,1,0:T(8,128)} reduce-window(s32[32,10,128]{2,1,0:T(8,128)} %fusion.63, s32[]{:T(128)} %copy.245), window={size=1x1x128 pad=0_0x0_0x127_0}, to_apply=%region_0.1 | reduce-window | flops 5201920 | bytes 327684 | tf_op jit(solution)/shard_map/reduce-window
  28.1 9.9 %scatter_custom_fusion = bf16[1024,768]{1,0:T(8,128)(2,1)} fusion(s32[1280]{0:T(1024)S(1)} %get-tuple-element.116, bf16[1280,768]{1,0:T(8,128)(2,1)} %param.11, bf16[]{:T(256)} %constant.162.clone.1), kind=kCustom, calls=%fused_computation.91 | custom fusion | bytes 1573376 | tf_op jit(solution)/shard_map/scatter | solution.py:168
  38.1 8.0 %all-to-all-start = ((bf16[32,32,768]{2,1,0:T(8,128)(2,1)}), bf16[32,32,768]{2,1,0:T(8,128)(2,1)}, u32[]{:S(2)}, u32[]{:S(2)}) async-start(bf16[32,32,768]{2,1,0:T(8,128)(2,1)} %bitcast.276), calls=%async_computation | async-start | bytes 3145728 | tf_op jit(solution)/shard_map/all_to_all | solution.py:147
  46.5 37.2 %all-to-all-done = bf16[32,32,768]{2,1,0:T(8,128)(2,1)} async-done(((bf16[32,32,768]{2,1,0:T(8,128)(2,1)}), bf16[32,32,768]{2,1,0:T(8,128)(2,1)}, u32[]{:S(2)}, u32[]{:S(2)}) %all-to-all-start) | async-done | bytes 1572896 | tf_op jit(solution)/shard_map/all_to_all | solution.py:147
  83.7 4.7 gather_fusion
  91.2 5.4 %fusion.84 = (bf16[512,2304]{1,0:T(8,128)(2,1)S(1)}, f32[512,2304]{1,0:T(8,128)}) fusion(bf16[768,2304]{1,0:T(8,128)(2,1)S(1)} %copy-done, bf16[512,768]{1,0:T(8,128)(2,1)} %gather_fusion, f32[768]{0:T(1024)S(1)} %copy-done.14, f32[512]{0:T(512)S(1)} %add_rsqrt_fusion.1, f32[512]{0:T(512)S(1)} %broadcast_multiply_fusion.1), kind=kOutput, calls=%fused_computation.150 | convolution fusion | flops 1815085056 | bytes 11410432 | tf_op jit(solution)/shard_map/dot_general | solution.py:120
  98.1 2.7 stack.32
  106.9 3.9 maximum_bitcast_fusion.2
  110.8 5.2 copy.167
  116.0 9.4 %reshape.393 = bf16[8,12,3,4096]{3,2,1,0:T(4,128)(2,1)} reshape(bf16[8,12,3,64,64]{4,3,2,1,0:T(8,128)(2,1)} %bitcast.269) | data formatting | bytes 4718592 | tf_op jit(solution)/shard_map/reshape | solution.py:91
  125.4 3.8 all-to-all-start.1
  129.2 2.7 pad_maximum_fusion
  133.8 65.3 %collective-permute-done = bf16[2,512,768]{2,1,0:T(8,128)(2,1)} collective-permute-done((bf16[2,512,768]{2,1,0:T(8,128)(2,1)}, bf16[2,512,768]{2,1,0:T(8,128)(2,1)}, u32[]{:S(2)}, u32[]{:S(2)}) %collective-permute-start) | collective-permute-done | bytes 1572896 | tf_op jit(solution)/shard_map/ppermute | solution.py:17
  199.2 4.6 maximum_select_fusion.1
  205.2 3.4 copy.170
  208.6 7.7 %reshape.347 = bf16[8,12,3,64,64]{4,3,0,2,1:T(8,128)(2,1)} reshape(bf16[8,12,3,4096]{3,0,2,1:T(8,128)(2,1)} %copy.170) | data formatting | bytes 4718592 | tf_op jit(solution)/shard_map/reshape | solution.py:93
  216.2 33.4 %while.25 = (s32[]{:T(128)}, bf16[12,512,64]{1,2,0:T(8,128)(2,1)S(1)}, f32[12,512]{1,0:T(8,128)S(1)}, bf16[12,3,512,64]{3,2,1,0:T(8,128)(2,1)}, s32[]{:T(128)}, /*index=5*/s32[]{:T(128)}, s32[]{}, s32[]{}) while((s32[]{:T(128)}, bf16[12,512,64]{1,2,0:T(8,128)(2,1)S(1)}, f32[12,512]{1,0:T(8,128)S(1)}, bf16[12,3,512,64]{3,2,1,0:T(8,128)(2,1)}, ...), condition=%wide.region_18.19_spmd, body=%wide.region_15.18_spmd.sunk | while | flops 68451840 | bytes 3693689 | solution.py:99
  250.4 3.6 all-to-all-start.2
  258.8 17.3 %all-to-all-done.2 = f32[8,1,768]{2,1,0:T(1,128)S(1)} async-done(((f32[8,1,768]{2,1,0:T(1,128)}), f32[8,1,768]{2,1,0:T(1,128)S(1)}, u32[]{:S(2)}, u32[]{:S(2)}) %all-to-all-start.2) | async-done | bytes 24608 | tf_op jit(solution)/shard_map/all_to_all | solution.py:105
  276.1 4.5 all-to-all-start.3
  283.8 6.0 %maximum_select_fusion = bf16[2,2048,768]{2,1,0:T(8,128)(2,1)S(1)} fusion(bf16[2,1024,768]{2,1,0:T(8,128)(2,1)} %maximum_select_fusion.1, bf16[2,1024,768]{2,1,0:T(8,128)(2,1)} %collective-permute-done.1, pred[]{:T(512)S(6)} %eq.60), kind=kLoop, calls=%fused_computation.59 | loop fusion | flops 28311552 | bytes 12582913 | tf_op jit(solution)/shard_map/jit(_where)/select_n | solution.py:51
  292.0 4.7 copy.162
  296.7 3.0 copy.163
  299.7 150.3 %while.24 = (s32[]{:T(128)}, f32[12,3,512,64]{2,3,1,0:T(8,128)}, f32[12,3,512]{2,1,0:T(4,128)}, bf16[12,512,64]{1,2,0:T(8,128)(2,1)}, bf16[12,2048,64]{1,2,0:T(8...) while((s32[]{:T(128)}, f32[12,3,512,64]{2,3,1,0:T(8,128)}, f32[12,3,512]{2,1,0:T(4,128)}, ...), condition=%wide.region_14.15_spmd, body=%wide.region_7.14_spmd.sunk | while | flops 479233536 | bytes 31340672 | solution.py:79
  452.7 2.8 copy_convert_fusion
  455.6 2.7 reshape.390
  462.7 4.0 fusion.44
  469.4 3.9 scatter_custom_fusion.1
  473.3 6.4 %all-to-all-start.4 = ((bf16[32,32,768]{2,1,0:T(8,128)(2,1)}), bf16[32,32,768]{2,1,0:T(8,128)(2,1)}, u32[]{:S(2)}, u32[]{:S(2)}) async-start(bf16[32,32,768]{2,1,0:T(8,128)(2,1)} %bitcast.68), calls=%async_computation.4 | async-start | bytes 3145728 | tf_op jit(solution)/shard_map/all_to_all | solution.py:147
  479.7 37.6 %all-to-all-done.4 = bf16[32,32,768]{2,1,0:T(8,128)(2,1)} async-done(((bf16[32,32,768]{2,1,0:T(8,128)(2,1)}), bf16[32,32,768]{2,1,0:T(8,128)(2,1)}, u32[]{:S(2)}, u32[]{:S(2)}) %all-to-all-start.4) | async-done | bytes 1572896 | tf_op jit(solution)/shard_map/all_to_all | solution.py:147
  517.4 7.5 %gather_fusion.1 = bf16[1280,768]{1,0:T(8,128)(2,1)} fusion(bf16[1024,768]{1,0:T(8,128)(2,1)} %bitcast.69, s32[2048]{0:T(1024)S(1)} %pad_clamp_fusion), kind=kCustom, calls=%fused_computation.1 | custom fusion | bytes 3937280 | tf_op jit(solution)/shard_map/jit(_take)/gather | solution.py:183
  524.9 3.1 broadcast_select_fusion
  (567 shorter events, 227.1 us)
Async XLA Ops:
  0.0 91.2 %copy-start = (bf16[768,2304]{1,0:T(8,128)(2,1)S(1)}, bf16[768,2304]{1,0:T(8,128)(2,1)}, u32[]{:S(2)}) copy-start(bf16[768,2304]{1,0:T(8,128)(2,1)} %param.14) | copy-start | bytes 10616836
  0.0 27.6 %copy-start.7 = (s32[1280]{0:T(1024)S(1)}, s32[1280]{0:T(1024)}, u32[]{:S(2)}) copy-start(s32[1280]{0:T(1024)} %param.12) | copy-start | bytes 15364
  28.1 9.9 %copy-start.9 = (s32[1280]{0:T(1024)}, s32[1280]{0:T(1024)S(1)}, u32[]{:S(2)}) copy-start(s32[1280]{0:T(1024)S(1)} %get-tuple-element.116) | copy-start | bytes 15364
  28.1 17.9 %copy-start.8 = (s32[1,512]{1,0:T(1,128)S(1)}, s32[1,512]{1,0:T(1,128)}, u32[]{:S(2)}) copy-start(s32[1,512]{1,0:T(1,128)} %param.13) | copy-start | bytes 6148
  38.1 45.6 %all-to-all-start = ((bf16[32,32,768]{2,1,0:T(8,128)(2,1)}), bf16[32,32,768]{2,1,0:T(8,128)(2,1)}, u32[]{:S(2)}, u32[]{:S(2)}) async-start(bf16[32,32,768]{2,1,0:T(8,128)(2,1)} %bitcast.276), calls=%async_computation | async-start | bytes 3145728 | tf_op jit(solution)/shard_map/all_to_all | solution.py:147
  83.6 7.5 %copy-start.14 = (f32[768]{0:T(1024)S(1)}, f32[768]{0:T(1024)}, u32[]{:S(2)}) copy-start(f32[768]{0:T(1024)} %param.16) | copy-start | bytes 9220
  104.6 6.2 %copy-start.4 = (bf16[512,768]{1,0:T(8,128)(2,1)}, bf16[512,768]{1,0:T(8,128)(2,1)S(1)}, u32[]{:S(2)}) copy-start(bf16[512,768]{1,0:T(8,128)(2,1)S(1)} %fusion.50) | copy-start | bytes 2359300
  125.4 79.8 %all-to-all-start.1 = ((bf16[8,12,3,4096]{3,2,1,0:T(4,128)(2,1)}), bf16[8,12,3,4096]{3,2,1,0:T(4,128)(2,1)S(1)}, u32[]{:S(2)}, u32[]{:S(2)}) async-start(bf16[8,12,3,4096]{3,2,1,0:T(4,128)(2,1)} %reshape.393), calls=%async_computation.1 | async-start | bytes 6291456 | tf_op jit(solution)/shard_map/all_to_all | solution.py:92
  131.9 67.3 %collective-permute-start = (bf16[2,512,768]{2,1,0:T(8,128)(2,1)}, bf16[2,512,768]{2,1,0:T(8,128)(2,1)}, u32[]{:S(2)}, u32[]{:S(2)}) collective-permute-start(bf16[2,512,768]{2,1,0:T(8,128)(2,1)} %pad_maximum_fusion), channel_id=1, source_target_pairs={{0,4},{4,0},{8,12},{12,8},{16,20},{20,16},{24,28},{28,24},{1,5},{5... | collective-permute-start | bytes 4718600 | tf_op jit(solution)/shard_map/ppermute | solution.py:17
  203.7 80.1 %collective-permute-start.1 = (bf16[2,1024,768]{2,1,0:T(8,128)(2,1)}, bf16[2,1024,768]{2,1,0:T(8,128)(2,1)}, u32[]{:S(2)}, u32[]{:S(2)}) collective-permute-start(bf16[2,1024,768]{2,1,0:T(8,128)(2,1)} %maximum_select_fusion.1), channel_id=1, source_target_pairs={{0,8},{4,12},{8,0},{12,4},{16,24},{20,28},{24,16},{28,20},{1,9},{5... | collective-permute-start | bytes 9437192 | tf_op jit(solution)/shard_map/ppermute | solution.py:17
  208.6 7.7 %copy-start.6 = (bf16[12,512,64]{1,2,0:T(8,128)(2,1)S(1)}, bf16[12,512,64]{1,2,0:T(8,128)(2,1)}, u32[]{:S(2)}) copy-start(bf16[12,512,64]{1,2,0:T(8,128)(2,1)} %custom-call.6) | copy-start | bytes 2359300
  216.2 37.8 %copy-start.5 = (bf16[512,768]{1,0:T(8,128)(2,1)S(1)}, bf16[512,768]{1,0:T(8,128)(2,1)}, u32[]{:S(2)}) copy-start(bf16[512,768]{1,0:T(8,128)(2,1)} %copy-done.4) | copy-start | bytes 2359300
  250.4 25.7 %all-to-all-start.2 = ((f32[8,1,768]{2,1,0:T(1,128)}), f32[8,1,768]{2,1,0:T(1,128)S(1)}, u32[]{:S(2)}, u32[]{:S(2)}) async-start(f32[8,1,768]{2,1,0:T(1,128)} %reshape.398), calls=%async_computation.2 | async-start | bytes 49152 | tf_op jit(solution)/shard_map/all_to_all | solution.py:105
  276.1 176.6 %all-to-all-start.3 = ((bf16[8,12,4096]{2,1,0:T(8,128)(2,1)}), bf16[8,12,4096]{2,1,0:T(8,128)(2,1)}, u32[]{:S(2)}, u32[]{:S(2)}) async-start(bf16[8,12,4096]{2,1,0:T(8,128)(2,1)} %copy.176), calls=%async_computation.3 | async-start | bytes 2097152 | tf_op jit(solution)/shard_map/all_to_all | solution.py:104
  309.4 0.9 copy-start.2
  321.9 0.9 copy-start.2
  334.4 0.9 copy-start.2
  346.9 0.9 copy-start.2
  359.5 0.9 copy-start.2
  372.0 0.9 copy-start.2
  384.5 0.9 copy-start.2
  397.0 0.9 copy-start.2
  409.6 0.9 copy-start.2
  422.1 0.9 copy-start.2
  447.1 0.9 copy-start.2
  466.6 1.1 copy-start.3
  466.7 1.5 copy-start.13
  468.2 1.2 copy-start.12
  473.3 6.4 %copy-start.10 = (s32[1280]{0:T(1024)S(1)}, s32[1280]{0:T(1024)}, u32[]{:S(2)}) copy-start(s32[1280]{0:T(1024)} %copy-done.9) | copy-start | bytes 15364
  473.3 44.0 %all-to-all-start.4 = ((bf16[32,32,768]{2,1,0:T(8,128)(2,1)}), bf16[32,32,768]{2,1,0:T(8,128)(2,1)}, u32[]{:S(2)}, u32[]{:S(2)}) async-start(bf16[32,32,768]{2,1,0:T(8,128)(2,1)} %bitcast.68), calls=%async_computation.4 | async-start | bytes 3145728 | tf_op jit(solution)/shard_map/all_to_all | solution.py:147
  517.4 7.6 %copy-start.11 = (pred[1280]{0:T(1024)(128)(4,1)S(1)}, pred[1280]{0:T(1024)(128)(4,1)}, u32[]{:S(2)}) copy-start(pred[1280]{0:T(1024)(128)(4,1)} %get-tuple-element.115) | copy-start | bytes 3844
  517.4 10.6 %copy-start.1 = (bf16[768,2304]{1,0:T(8,128)(2,1)S(1)}, bf16[768,2304]{1,0:T(8,128)(2,1)}, u32[]{:S(2)}) copy-start(bf16[768,2304]{1,0:T(8,128)(2,1)} %param.14) | copy-start | bytes 10616836
  (1 other events, 0.9 us)
where the time goes:
time: 536 us; the launch traced here: 528 us
  local copies, waits for them, and re-layouts  159 us (30%)
  waiting for transfers between devices  157 us (29%)
  other arithmetic  100 us (19%)
  matrix products  79.1 us (15%)
  starting transfers between devices  29.7 us (6%)
    all_to_all x2, waiting for transfers between devices, route_rows(): lax.all_to_all(block, ('seq', 'slide'), split_axis=0, concat_axis=0, tile...  74.8 us
    ppermute x2, waiting for transfers between devices, from_partner(): return lax.ppermute(value, axis, pairs)  65.3 us
    dot_general x48, matrix products, attend_block(): jnp.einsum('...qd,...kd->...qk', queries, keys, preferred_element_type=jn...  37 us
    dot_general x48, matrix products, attend_block(): jnp.einsum('...qk,...kd->...qd', weights.astype(jnp.bfloat16), values, pr...  35.8 us
    dynamic_slice x60, local copies, waits for them, and re-layouts, local_branches(): lax.map(per_head, (query_heads, key_heads, value_heads))  31 us
    reduce_sum x48, other arithmetic, attend_block(): total = jnp.sum(weights, axis=-1, keepdims=True)  20.5 us
    another operation x3, other arithmetic  20.1 us
    all_to_all x1, waiting for transfers between devices, far_heads(): lax.all_to_all(totals, 'seq', split_axis=0, concat_axis=0, tiled=True)  17.3 us
  transfers between devices with their start and end apart: 7, of which 4 were waited for; matrix products, arithmetic and copies ran while one was open for 43% of the time, Pallas kernels for 0%

commit v1 on v0

v1 whole, which is shorter than its diff:
```python
import functools
import math

import jax
import jax.numpy as jnp
from jax import lax
from jax.experimental import pallas as pl
from jax.experimental.pallas import tpu as pltpu
from jax.sharding import Mesh
from jax.sharding import PartitionSpec as P

HEADS = 12
HDIM = 64
SEG = 2048
CLASSES = 8
EPS = 1e-05
VMEM = 60 << 20


def layer_norm(inputs, gain):
    average = jnp.mean(inputs, axis=-1, keepdims=True)
    centred = inputs - average
    spread = jnp.mean(centred * centred, axis=-1, keepdims=True)
    return centred * lax.rsqrt(spread + EPS) * gain


def one_hot(left, right):
    return jnp.where(left == right, 1.0, 0.0).astype(jnp.bfloat16)


def dot(left, right):
    return jnp.dot(left, right, preferred_element_type=jnp.float32)


def units_of(member, members):
    owned = HEADS * CLASSES // members
    units = [divmod(member * owned + i, CLASSES) for i in range(owned)]
    return units + units[-1:] * (owned % 2)


def heads_of(member, members):
    first = units_of(member, members)[0][0]
    return first, min(first + 1, HEADS - 1)


def pack_kernel(visible, capacity, dest_ref, tiles_ref, out_ref, slot_ref):
    slots, _ = out_ref.shape
    count = dest_ref.shape[1]
    devices = slots // capacity
    target = jnp.right_shift(dest_ref[...], visible.bit_length() - 1)
    lanes = 128
    before = one_hot_lt(lanes)
    offset = jnp.zeros((devices, 1), jnp.float32)
    pieces = []
    for start in range(0, count, lanes):
        here = target[:, start : start + lanes]
        device = lax.broadcasted_iota(jnp.int32, (devices, lanes), 0)
        chosen = jnp.where(device == here, 1.0, 0.0)
        rank = dot(chosen.astype(jnp.bfloat16), before) + offset
        placed = jnp.sum(chosen * rank, axis=0, keepdims=True).astype(jnp.int32)
        pieces.append(jnp.where(here >= 0, here * capacity + placed, -1))
        offset = offset + jnp.sum(chosen, axis=1, keepdims=True)
    slot = jnp.concatenate(pieces, axis=1)
    slot_ref[...] = slot
    step = math.gcd(slots, 256)
    for start in range(0, slots, step):
        wanted = lax.broadcasted_iota(jnp.int32, (step, count), 0) + start
        rows = dot(one_hot(wanted, slot), tiles_ref[...])
        out_ref[start : start + step, :] = rows.astype(jnp.bfloat16)


def one_hot_lt(size):
    row = lax.broadcasted_iota(jnp.int32, (size, size), 0)
    column = lax.broadcasted_iota(jnp.int32, (size, size), 1)
    return jnp.where(row < column, 1.0, 0.0).astype(jnp.bfloat16)


def project_kernel(members, slot_ref, arrived_ref, gain_ref, wq_ref, wkv_ref, rows_ref, send_ref, q_ref, kv_ref):
    visible, width = rows_ref.shape
    slots = arrived_ref.shape[0]
    part = visible // CLASSES
    chosen = one_hot(lax.broadcasted_iota(jnp.int32, (visible, slots), 1), slot_ref[...])
    rows = dot(chosen, arrived_ref[...])
    rows_ref[...] = rows.astype(jnp.bfloat16)
    normed = layer_norm(rows, gain_ref[...]).astype(jnp.bfloat16)
    q_ref[...] = (dot(normed, wq_ref[...]) * HDIM ** (-0.5)).astype(jnp.bfloat16)
    kv_ref[...] = dot(normed, wkv_ref[...]).astype(jnp.bfloat16)
    low = lax.broadcasted_iota(jnp.int32, (part, 2 * HDIM), 1) < HDIM
    for member in range(members):
        for place, head in enumerate(heads_of(member, members)):
            send_ref[member, place * visible : (place + 1) * visible, :] = kv_ref[
                :, head * 2 * HDIM : (head + 1) * 2 * HDIM
            ]
        units = units_of(member, members)
        for i in range(0, len(units), 2):
            pair = [
                q_ref[cls * part : (cls + 1) * part, head * 2 * HDIM : (head + 1) * 2 * HDIM]
                for head, cls in units[i : i + 2]
            ]
            at = 2 * visible + i // 2 * part
            send_ref[member, at : at + part, :] = jnp.where(low, pair[0], pair[1])


def attend_kernel(visible, place_ref, class_ref, block_ref, out_ref):
    members = block_ref.shape[0]
    part = visible // CLASSES
    group = SEG // visible
    segments = members // group
    step = pl.program_id(0)
    rows = group * part
    low = lax.broadcasted_iota(jnp.int32, (rows, 2 * HDIM), 1) < HDIM
    counts = [1 + (t % 2 == 0) + (t % 4 == 0) + (t % 8 == 0) for t in range(CLASSES)]

    def keys_of(segment, place, cls):
        at = pl.multiple_of(place * visible + cls * part, part)
        return jnp.concatenate(
            [block_ref[segment * group + i, pl.ds(at, part), :] for i in range(group)], axis=0
        )

    for segment in range(segments):
        halves = []
        for half in range(2):
            place = place_ref[2 * step + half]
            cls = class_ref[2 * step + half]
            at = pl.multiple_of(2 * visible + step * part, part)
            query = jnp.concatenate(
                [block_ref[segment * group + i, pl.ds(at, part), :] for i in range(group)], axis=0
            )
            if half == 1:
                query = jnp.concatenate([query[:, HDIM:], query[:, :HDIM]], axis=1)
            query = jnp.where(low, query, jnp.zeros_like(query))
            keys = [(keys_of(segment, place, jnp.bitwise_and(cls + t, CLASSES - 1)), counts[t]) for t in range(CLASSES)]
            keys += [(keys_of(other, place, cls), 1) for other in range(segments) if other != segment]
            scores = [
                lax.dot_general(query, key, (((1,), (1,)), ((), ())), preferred_element_type=jnp.float32)
                for key, _ in keys
            ]
            peak = jnp.max(functools.reduce(jnp.maximum, scores), axis=-1, keepdims=True)
            mixed = jnp.zeros((rows, 2 * HDIM), jnp.float32)
            for score, (key, count) in zip(scores, keys):
                weights = jnp.exp(score - (peak - math.log(count))).astype(jnp.bfloat16)
                mixed += dot(weights, jnp.where(low, jnp.ones_like(key), key))
            turned = jnp.concatenate([mixed[:, HDIM:], mixed[:, :HDIM]], axis=1)
            halves.append(turned / mixed if half == 0 else mixed / turned)
        both = jnp.where(low, halves[0], halves[1]).astype(jnp.bfloat16)
        for i in range(group):
            out_ref[segment * group + i, :, :] = both[i * part : (i + 1) * part, :]


def finish_kernel(slot_ref, mixed_ref, rows_ref, gain_ref, w_ref, out_ref, attended_ref):
    visible, _ = rows_ref.shape
    members = mixed_ref.shape[0]
    part = visible // CLASSES
    slots = out_ref.shape[0]
    where = {}
    for member in range(members):
        owned = HEADS * CLASSES // members
        for i, unit in enumerate(units_of(member, members)[:owned]):
            where[unit] = (member, i)
    for head in range(0, HEADS, 2):
        for cls in range(CLASSES):
            pair = []
            for one in (head, head + 1):
                member, i = where[(one, cls)]
                tile = mixed_ref[member, i // 2 * part : (i // 2 + 1) * part, :]
                pair.append(tile[:, i % 2 * HDIM : (i % 2 + 1) * HDIM])
            attended_ref[cls * part : (cls + 1) * part, head * HDIM : (head + 2) * HDIM] = (
                jnp.concatenate(pair, axis=1)
            )
    hidden = rows_ref[...].astype(jnp.float32) + dot(attended_ref[...], w_ref[...])
    answer = layer_norm(hidden, gain_ref[...]).astype(jnp.bfloat16)
    step = math.gcd(slots, 256)
    for start in range(0, slots, step):
        wanted = lax.broadcasted_iota(jnp.int32, (step, visible), 0) + start
        out_ref[start : start + step, :] = dot(one_hot(wanted, slot_ref[...]), answer).astype(
            jnp.bfloat16
        )


def unpack_kernel(slot_ref, back_ref, out_ref):
    count, _ = out_ref.shape
    slots = back_ref.shape[0]
    step = math.gcd(count, 256)
    for start in range(0, count, step):
        here = lax.broadcasted_iota(jnp.int32, (step, slots), 1)
        chosen = one_hot(slot_ref[start : start + step, :], here)
        out_ref[start : start + step, :] = dot(chosen, back_ref[...]).astype(jnp.bfloat16)


def call(kernel, outs, name, scratch=()):
    return pl.pallas_call(
        kernel,
        out_shape=outs,
        scratch_shapes=list(scratch),
        compiler_params=pltpu.CompilerParams(vmem_limit_bytes=VMEM),
        name=name,
    )


def on_device(tiles, dest_table, owner_row, w_qkv, w_out, gain_attn, gain_out):
    groups = lax.axis_size("group")
    axes = ("group", "high", "low")
    inside = ("high", "low")
    members = lax.axis_size(inside)
    devices = groups * members
    count, width = tiles.shape
    visible = owner_row.shape[1]
    capacity = 2 * visible // devices
    slots = devices * capacity
    part = visible // CLASSES
    owned = HEADS * CLASSES // members
    pairs = (owned + 1) // 2
    bf16 = jnp.bfloat16

    moves = [(s * groups + g, g * members + s) for g in range(groups) for s in range(members)]
    owners = lax.ppermute(owner_row.reshape(visible // 128, 128), axes, moves).reshape(visible)
    owners = owners.reshape(part, CLASSES).T.reshape(visible)

    outgoing, send_slot = call(
        functools.partial(pack_kernel, visible, capacity),
        (jax.ShapeDtypeStruct((slots, width), bf16), jax.ShapeDtypeStruct((1, count), jnp.int32)),
        "pack",
    )(dest_table.reshape(1, count), tiles)
    arrived = lax.all_to_all(
        outgoing.reshape(devices, capacity, width), axes, split_axis=0, concat_axis=0, tiled=True
    ).reshape(slots, width)

    source = owners // count
    same = source[:, None] == source[None, :]
    earlier = owners[None, :] < owners[:, None]
    placed = jnp.sum((same & earlier).astype(jnp.int32), axis=1)
    slot = source * capacity + placed

    heads = w_qkv.reshape(width, 3, HEADS, HDIM)
    wq = jnp.stack([heads[:, 0], heads[:, 0]], axis=2).reshape(width, 2 * width)
    wkv = jnp.stack([heads[:, 1], heads[:, 2]], axis=2).reshape(width, 2 * width)

    rows, send = call(
        functools.partial(project_kernel, members),
        (
            jax.ShapeDtypeStruct((visible, width), bf16),
            jax.ShapeDtypeStruct((members, 2 * visible + pairs * part, 2 * HDIM), bf16),
        ),
        "project",
        [pltpu.VMEM((visible, 2 * width), bf16), pltpu.VMEM((visible, 2 * width), bf16)],
    )(slot[:, None], arrived, gain_attn[None, :], wq, wkv)
    blocks = lax.all_to_all(send, inside, split_axis=0, concat_axis=0, tiled=True)

    first = lax.axis_index(inside) * owned
    units = jnp.minimum(first + jnp.arange(2 * pairs), HEADS * CLASSES - 1).astype(jnp.int32)
    mixed = pl.pallas_call(
        functools.partial(attend_kernel, visible),
        out_shape=jax.ShapeDtypeStruct((members, pairs * part, 2 * HDIM), bf16),
        grid_spec=pltpu.PrefetchScalarGridSpec(
            num_scalar_prefetch=2,
            grid=(pairs,),
            in_specs=[pl.BlockSpec(blocks.shape, lambda i, *_: (0, 0, 0), pipeline_mode=pl.Buffered(1))],
            out_specs=pl.BlockSpec((members, part, 2 * HDIM), lambda i, *_: (0, i, 0)),
        ),
        compiler_params=pltpu.CompilerParams(vmem_limit_bytes=VMEM),
        name="attend",
    )(jnp.minimum(units // CLASSES - first // CLASSES, 1), units % CLASSES, blocks)
    mixed = lax.all_to_all(mixed, inside, split_axis=0, concat_axis=0, tiled=True)

    answers = call(
        finish_kernel,
        jax.ShapeDtypeStruct((slots, width), bf16),
        "finish",
        [pltpu.VMEM((visible, width), bf16)],
    )(slot[None, :], mixed, rows, gain_out[None, :], w_out)
    back = lax.all_to_all(
        answers.reshape(devices, capacity, width), axes, split_axis=0, concat_axis=0, tiled=True
    ).reshape(slots, width)
    return call(unpack_kernel, jax.ShapeDtypeStruct((count, width), bf16), "unpack")(
        send_slot.reshape(count, 1), back
    )


def solution(mesh):
    n_seq, n_slide = mesh.shape["seq"], mesh.shape["slide"]
    split = Mesh(
        mesh.devices.reshape(n_slide, n_seq // n_slide, n_slide), ("group", "high", "low")
    )
    every = ("group", "high", "low")
    in_specs = (P(every, None), P(every), P("low", ("group", "high")), P(), P(), P(), P())
    return jax.shard_map(
        on_device, mesh=split, in_specs=in_specs, out_specs=P(every, None), check_vma=False
    )
```

time: 536 us -> 197 us (0.37); the launches traced: 528 us -> 197 us
  local copies, waits for them, and re-layouts: 159 us -> 19.8 us
  other arithmetic: 100 us -> 3.94 us
  matrix products: 79.1 us -> 0 us
  waiting for transfers between devices: 157 us -> 103 us
  Pallas kernels: 0 us -> 50.1 us
  starting transfers between devices: 29.7 us -> 19.3 us
    dot_general x98 -> x0, matrix products: 79.1 us -> none  [the longest x48 37 us: attend_block(): jnp.einsum('...qd,...kd->...qk', queries, keys, preferred_element_type=jn...]
    ppermute x2 -> x1, waiting for transfers between devices: 65.3 us -> 0.01 us  [on_device(): lax.ppermute(owner_row.reshape(visible // 128, 128), axes, moves)]
    pallas_call x0 -> x5, Pallas kernels: none -> 50.1 us  [the longest x1 25.2 us: on_device(): pl.pallas_call(functools.partial(attend_kernel, visible), out_shape=jax.S...]
    reshape x128 -> x5, local copies, waits for them, and re-layouts: 53.1 us -> 9.22 us  [the longest x1 4.27 us: on_device(): wq = jnp.stack([heads[:, 0], heads[:, 0]], axis=2).reshape(width, 2 * width)]
    dynamic_slice x60 -> x0, local copies, waits for them, and re-layouts: 31 us -> none  [local_branches(): lax.map(per_head, (query_heads, key_heads, value_heads))]
    reduce_sum x55 -> x1, other arithmetic: 29 us -> 0.35 us  [on_device(): placed = jnp.sum((same & earlier).astype(jnp.int32), axis=1)]
    another operation x4 -> x1, other arithmetic: 22.7 us -> 1.62 us  [on_device(): wq = jnp.stack([heads[:, 0], heads[:, 0]], axis=2).reshape(width, 2 * width)]
    dynamic_update_slice x24 -> x0, other arithmetic: 16.6 us -> none  [local_branches(): lax.map(per_head, (query_heads, key_heads, value_heads))]
  transfers between devices with their start and end apart: 7 -> 5, of which waited for: 4 -> 4; matrix products, arithmetic and copies ran while one was open for 43% -> 10% of each run, Pallas kernels for 0% -> 0%
where the time goes in v1:
time: 197 us
  waiting for transfers between devices  103 us (52%)
  Pallas kernels  50.1 us (25%)
  local copies, waits for them, and re-layouts  19.8 us (10%)
  starting transfers between devices  19.3 us (10%)
  other arithmetic  3.94 us (2%)
    all_to_all x1, waiting for transfers between devices, on_device(): lax.all_to_all(answers.reshape(devices, capacity, width), axes, split_axi...  36.7 us
    all_to_all x1, waiting for transfers between devices, on_device(): lax.all_to_all(send, inside, split_axis=0, concat_axis=0, tiled=True)  34.4 us
    pallas_call x1, Pallas kernels, on_device(): pl.pallas_call(functools.partial(attend_kernel, visible), out_shape=jax.S...  25.2 us
    all_to_all x1, waiting for transfers between devices, on_device(): lax.all_to_all(outgoing.reshape(devices, capacity, width), axes, split_ax...  21.1 us
    all_to_all x1, waiting for transfers between devices, on_device(): lax.all_to_all(mixed, inside, split_axis=0, concat_axis=0, tiled=True)  11 us
    pallas_call x1, Pallas kernels, on_device(): call(functools.partial(project_kernel, members), (jax.ShapeDtypeStruct((v...  9.52 us
    unnamed x15, local copies, waits for them, and re-layouts  8.18 us
    all_to_all x1, starting transfers between devices, on_device(): lax.all_to_all(outgoing.reshape(devices, capacity, width), axes, split_ax...  7.44 us
  transfers between devices with their start and end apart: 5, of which 4 were waited for; matrix products, arithmetic and copies ran while one was open for 10% of the time, Pallas kernels for 0%

profile of v1, /device:TPU:0, one launch (start us, length us, event | category | flops | bytes accessed | tf_op | source)
XLA Modules:
  0.0 196.6 jit_solution(7205765063859453519)
XLA Ops:
  0.0 1.3 reshape.175.dest_ref
  1.3 5.0 %pack.1 = (bf16[1024,768]{1,0:T(8,128)(2,1)}, s32[1,1280]{1,0:T(1,128)}) custom-call(s32[1,1280]{1,0:T(1,128)} %reshape.175.dest_ref, bf16[1280,768]{1,0:T(8,128)(2,1)} %tiles_ref.1), custom_call_target="tpu_custom_call" | custom-call | tf_op jit(solution)/shard_map/pack/pallas_call | solution.py:219
  6.3 7.4 %all-to-all-start = ((bf16[32,32,768]{2,1,0:T(8,128)(2,1)}), bf16[32,32,768]{2,1,0:T(8,128)(2,1)}, u32[]{:S(2)}, u32[]{:S(2)}) async-start(bf16[32,32,768]{2,1,0:T(8,128)(2,1)} %bitcast.25), calls=%async_computation | async-start | bytes 3145728 | tf_op jit(solution)/shard_map/all_to_all | solution.py:224
  13.8 0.7 collective-permute-start
  14.5 4.5 %copy.55 = bf16[768,2304]{0,1:T(8,128)(2,1)S(1)} copy(bf16[768,2304]{1,0:T(8,128)(2,1)} %param.10) | data formatting | bytes 7077888 | tf_op args[3]
  19.0 0.4 slice_bitcast_fusion.1
  19.4 1.6 pad_maximum_fusion
  21.0 4.3 %copy.56.wq_ref = bf16[768,1536]{1,0:T(8,128)(2,1)} copy(bf16[768,1536]{0,1:T(8,128)(2,1)} %bitcast.22) | data formatting | bytes 4718592 | tf_op jit(solution)/shard_map/reshape | solution.py:235
  25.3 2.5 %copy.57.wkv_ref = bf16[768,1536]{1,0:T(8,128)(2,1)} copy(bf16[768,1536]{0,1:T(8,128)(2,1)S(1)} %bitcast.21) | data formatting | bytes 4718592 | tf_op jit(solution)/shard_map/reshape | solution.py:236
  27.8 0.6 broadcast_in_dim.4.gain_ref
  28.6 0.3 convert_reduce_fusion
  29.1 0.2 div.65
  29.3 0.3 and.60
  29.6 0.7 fusion.1.slot_ref
  30.3 21.1 %all-to-all-done = bf16[32,32,768]{2,1,0:T(8,128)(2,1)} async-done(((bf16[32,32,768]{2,1,0:T(8,128)(2,1)}), bf16[32,32,768]{2,1,0:T(8,128)(2,1)}, u32[]{:S(2)}, u32[]{:S(2)}) %all-to-all-start) | async-done | bytes 1572896 | tf_op jit(solution)/shard_map/all_to_all | solution.py:224
  51.5 9.5 %project.1 = (bf16[512,768]{1,0:T(8,128)(2,1)}, bf16[8,1408,128]{2,1,0:T(8,128)(2,1)}) custom-call(s32[512,1]{1,0:T(8,128)} %fusion.1.slot_ref, bf16[1024,768]{1,0:T(8,128)(2,1)} %bitcast.6.arrived_ref, f32[1,768]{1,0:T(1,128)} %broadcast_in_dim.4.gain_ref, bf16[768,1536]{1,0:T(8,128)(2,1)} %copy.56.wq_ref, bf16[768,1536]{1,0:T(8,128)(2,1)} %copy.57.wkv_ref), custom_call_target="tpu_custom_call" | custom-call | tf_op jit(solution)/shard_map/project/pallas_call | solution.py:238
  61.0 4.7 %all-to-all-start.1 = ((bf16[8,1408,128]{2,1,0:T(8,128)(2,1)}), bf16[8,1408,128]{2,1,0:T(8,128)(2,1)S(1)}, u32[]{:S(2)}, u32[]{:S(2)}) async-start(bf16[8,1408,128]{2,1,0:T(8,128)(2,1)} %get-tuple-element.11), calls=%async_computation.1 | async-start | bytes 5767168 | tf_op jit(solution)/shard_map/all_to_all | solution.py:247
  65.7 0.6 and_select_fusion
  66.3 34.4 %all-to-all-done.1.block_ref = bf16[8,1408,128]{2,1,0:T(8,128)(2,1)S(1)} async-done(((bf16[8,1408,128]{2,1,0:T(8,128)(2,1)}), bf16[8,1408,128]{2,1,0:T(8,128)(2,1)S(1)}, u32[]{:S(2)}, u32[]{:S(2)}) %all-to-all-start.1) | async-done | bytes 2883616 | tf_op jit(solution)/shard_map/all_to_all | solution.py:247
  100.7 1.6 copy-done
  102.3 25.2 %attend.1 = bf16[8,384,128]{2,1,0:T(8,128)(2,1)} custom-call(s32[12]{0:T(128)} %get-tuple-element.17.place_ref, s32[12]{0:T(128)} %get-tuple-element.16.class_ref, bf16[8,1408,128]{2,1,0:T(8,128)(2,1)} %copy-done), custom_call_target="tpu_custom_call" | custom-call | tf_op jit(solution)/shard_map/attend/pallas_call | solution.py:251
  127.4 3.7 %all-to-all-start.2 = ((bf16[8,384,128]{2,1,0:T(8,128)(2,1)}), bf16[8,384,128]{2,1,0:T(8,128)(2,1)S(1)}, u32[]{:S(2)}, u32[]{:S(2)}) async-start(bf16[8,384,128]{2,1,0:T(8,128)(2,1)} %attend.1), calls=%async_computation.2 | async-start | bytes 1572864 | tf_op jit(solution)/shard_map/all_to_all | solution.py:263
  131.2 0.6 broadcast_in_dim.5.gain_ref
  131.9 0.6 fusion.4.slot_ref
  132.5 11.0 %all-to-all-done.2.mixed_ref = bf16[8,384,128]{2,1,0:T(8,128)(2,1)S(1)} async-done(((bf16[8,384,128]{2,1,0:T(8,128)(2,1)}), bf16[8,384,128]{2,1,0:T(8,128)(2,1)S(1)}, u32[]{:S(2)}, u32[]{:S(2)}) %all-to-all-start.2) | async-done | bytes 786464 | tf_op jit(solution)/shard_map/all_to_all | solution.py:263
  143.5 0.9 copy-done.2
  144.4 5.3 %finish.1 = bf16[1024,768]{1,0:T(8,128)(2,1)} custom-call(s32[1,512]{1,0:T(1,128)} %fusion.4.slot_ref, bf16[8,384,128]{2,1,0:T(8,128)(2,1)} %copy-done.2, bf16[512,768]{1,0:T(8,128)(2,1)} %get-tuple-element.12.rows_ref, f32[1,768]{1,0:T(1,128)} %broadcast_in_dim.5.gain_ref, bf16[768,768]{1,0:T(8,128)(2,1)} %w_ref.1), custom_call_target="tpu_custom_call" | custom-call | tf_op jit(solution)/shard_map/finish/pallas_call | solution.py:265
  149.7 2.8 %all-to-all-start.3 = ((bf16[32,32,768]{2,1,0:T(8,128)(2,1)}), bf16[32,32,768]{2,1,0:T(8,128)(2,1)S(1)}, u32[]{:S(2)}, u32[]{:S(2)}) async-start(bf16[32,32,768]{2,1,0:T(8,128)(2,1)} %bitcast.24), calls=%async_computation.3 | async-start | bytes 3145728 | tf_op jit(solution)/shard_map/all_to_all | solution.py:271
  152.5 1.1 copy.58.slot_ref
  153.6 36.7 %all-to-all-done.3 = bf16[32,32,768]{2,1,0:T(8,128)(2,1)S(1)} async-done(((bf16[32,32,768]{2,1,0:T(8,128)(2,1)}), bf16[32,32,768]{2,1,0:T(8,128)(2,1)S(1)}, u32[]{:S(2)}, u32[]{:S(2)}) %all-to-all-start.3) | async-done | bytes 1572896 | tf_op jit(solution)/shard_map/all_to_all | solution.py:271
  190.3 1.2 copy-done.1
  191.4 5.1 %unpack.1 = bf16[1280,768]{1,0:T(8,128)(2,1)} custom-call(s32[1280,1]{1,0:T(8,128)} %copy.58.slot_ref, bf16[1024,768]{1,0:T(8,128)(2,1)} %bitcast.23), custom_call_target="tpu_custom_call" | custom-call | tf_op jit(solution)/shard_map/unpack/pallas_call | solution.py:274
  (21 shorter events, 0.6 us)
Async XLA Ops:
  6.3 7.5 %copy-start.6 = (s32[1,512]{1,0:T(1,128)S(1)}, s32[1,512]{1,0:T(1,128)}, u32[]{:S(2)}) copy-start(s32[1,512]{1,0:T(1,128)} %param.9) | copy-start | bytes 6148
  6.3 45.1 %all-to-all-start = ((bf16[32,32,768]{2,1,0:T(8,128)(2,1)}), bf16[32,32,768]{2,1,0:T(8,128)(2,1)}, u32[]{:S(2)}, u32[]{:S(2)}) async-start(bf16[32,32,768]{2,1,0:T(8,128)(2,1)} %bitcast.25), calls=%async_computation | async-start | bytes 3145728 | tf_op jit(solution)/shard_map/all_to_all | solution.py:224
  13.8 14.5 %collective-permute-start = (s32[4,128]{1,0:T(4,128)S(1)}, s32[4,128]{1,0:T(4,128)S(1)}, u32[]{:S(2)}, u32[]{:S(2)}) collective-permute-start(s32[4,128]{1,0:T(4,128)S(1)} %bitcast.30), channel_id=1, source_target_pairs={{0,0},{4,1},{8,2},{12,3},{16,4},{20,5},{24,6},{28,7},{1,8},{5,9},{... | collective-permute-start | bytes 6152 | tf_op jit(solution)/shard_map/ppermute | solution.py:216
  25.3 2.5 %copy-start.4 = (f32[768]{0:T(1024)S(1)}, f32[768]{0:T(1024)}, u32[]{:S(2)}) copy-start(f32[768]{0:T(1024)} %param.12) | copy-start | bytes 9220
  61.0 39.7 %all-to-all-start.1 = ((bf16[8,1408,128]{2,1,0:T(8,128)(2,1)}), bf16[8,1408,128]{2,1,0:T(8,128)(2,1)S(1)}, u32[]{:S(2)}, u32[]{:S(2)}) async-start(bf16[8,1408,128]{2,1,0:T(8,128)(2,1)} %get-tuple-element.11), calls=%async_computation.1 | async-start | bytes 5767168 | tf_op jit(solution)/shard_map/all_to_all | solution.py:247
  100.7 1.6 copy-start
  102.3 28.9 %copy-start.5 = (f32[768]{0:T(1024)S(1)}, f32[768]{0:T(1024)}, u32[]{:S(2)}) copy-start(f32[768]{0:T(1024)} %param.13) | copy-start | bytes 9220
  127.4 16.1 %all-to-all-start.2 = ((bf16[8,384,128]{2,1,0:T(8,128)(2,1)}), bf16[8,384,128]{2,1,0:T(8,128)(2,1)S(1)}, u32[]{:S(2)}, u32[]{:S(2)}) async-start(bf16[8,384,128]{2,1,0:T(8,128)(2,1)} %attend.1), calls=%async_computation.2 | async-start | bytes 1572864 | tf_op jit(solution)/shard_map/all_to_all | solution.py:263
  143.5 0.9 copy-start.2
  149.7 2.8 %copy-start.3 = (s32[1,1280]{1,0:T(1,128)S(1)}, s32[1,1280]{1,0:T(1,128)}, u32[]{:S(2)}) copy-start(s32[1,1280]{1,0:T(1,128)} %get-tuple-element.9) | copy-start | bytes 15364
  149.7 40.6 %all-to-all-start.3 = ((bf16[32,32,768]{2,1,0:T(8,128)(2,1)}), bf16[32,32,768]{2,1,0:T(8,128)(2,1)S(1)}, u32[]{:S(2)}, u32[]{:S(2)}) async-start(bf16[32,32,768]{2,1,0:T(8,128)(2,1)} %bitcast.24), calls=%async_computation.3 | async-start | bytes 3145728 | tf_op jit(solution)/shard_map/all_to_all | solution.py:271
  190.3 1.2 copy-start.1

commit v2 on v1

v2 whole, which is shorter than its diff:
```python
import functools
import math

import jax
import jax.numpy as jnp
from jax import lax
from jax.experimental import pallas as pl
from jax.experimental.pallas import tpu as pltpu
from jax.sharding import Mesh
from jax.sharding import PartitionSpec as P

HEADS = 12
HDIM = 64
SEG = 2048
CLASSES = 8
EPS = 1e-05
VMEM = 24 << 20


def layer_norm(inputs, gain):
    average = jnp.mean(inputs, axis=-1, keepdims=True)
    centred = inputs - average
    spread = jnp.mean(centred * centred, axis=-1, keepdims=True)
    return centred * lax.rsqrt(spread + EPS) * gain


def one_hot(left, right):
    return jnp.where(left == right, 1.0, 0.0).astype(jnp.bfloat16)


def dot(left, right):
    return jnp.dot(left, right, preferred_element_type=jnp.float32)


def parts_of(members):
    full = HEADS // members
    every = [(0, cls) for cls in range(CLASSES)]
    parts = [
        (i * members, (i + 1) * members, [([i * members + member], every) for member in range(members)])
        for i in range(full)
    ]
    first = full * members
    owned = (HEADS - first) * CLASSES // members
    if owned:
        dealt = []
        for member in range(members):
            units = [divmod(first * CLASSES + member * owned + i, CLASSES) for i in range(owned)]
            dealt.append((sorted({head for head, _ in units}), units))
        width = max(len(heads) for heads, _ in dealt)
        part = []
        for heads, units in dealt:
            units = [(heads.index(head), cls) for head, cls in units]
            part.append((heads + heads[-1:] * (width - len(heads)), units + units[-1:] * (owned % 2)))
        parts.append((first, HEADS, part))
    return parts


def swap(tile):
    return jnp.concatenate([tile[:, HDIM:], tile[:, :HDIM]], axis=1)


def dot_nt(left, right):
    return lax.dot_general(left, right, (((1,), (1,)), ((), ())), preferred_element_type=jnp.float32)


def pack_kernel(visible, capacity, dest_ref, tiles_hbm, out_ref, slot_ref, tiles_ref, sem):
    fetch = pltpu.make_async_copy(tiles_hbm, tiles_ref, sem)
    fetch.start()
    slots, _ = out_ref.shape
    count = dest_ref.shape[1]
    devices = slots // capacity
    target = jnp.right_shift(dest_ref[...], visible.bit_length() - 1)
    lanes = 128
    before = one_hot_lt(lanes)
    offset = jnp.zeros((devices, 1), jnp.float32)
    pieces = []
    for start in range(0, count, lanes):
        here = target[:, start : start + lanes]
        device = lax.broadcasted_iota(jnp.int32, (devices, lanes), 0)
        chosen = jnp.where(device == here, 1.0, 0.0)
        rank = dot(chosen.astype(jnp.bfloat16), before) + offset
        placed = jnp.sum(chosen * rank, axis=0, keepdims=True).astype(jnp.int32)
        pieces.append(jnp.where(here >= 0, here * capacity + placed, -1))
        offset = offset + jnp.sum(chosen, axis=1, keepdims=True)
    slot = jnp.concatenate(pieces, axis=1)
    slot_ref[...] = slot
    fetch.wait()
    step = math.gcd(slots, 256)
    for start in range(0, slots, step):
        wanted = lax.broadcasted_iota(jnp.int32, (step, count), 0) + start
        rows = dot(one_hot(wanted, slot), tiles_ref[...])
        out_ref[start : start + step, :] = rows.astype(jnp.bfloat16)


def one_hot_lt(size):
    row = lax.broadcasted_iota(jnp.int32, (size, size), 0)
    column = lax.broadcasted_iota(jnp.int32, (size, size), 1)
    return jnp.where(row < column, 1.0, 0.0).astype(jnp.bfloat16)


def gather_rows(slot_ref, arrived_ref, gain_ref, rows_ref, normed_ref):
    visible, slots = rows_ref.shape[0], arrived_ref.shape[0]
    chosen = one_hot(lax.broadcasted_iota(jnp.int32, (visible, slots), 1), slot_ref[...])
    rows = dot(chosen, arrived_ref[...])
    rows_ref[...] = rows.astype(jnp.bfloat16)
    normed_ref[...] = layer_norm(rows, gain_ref[...]).astype(jnp.bfloat16)


def project_part(part, normed_ref, w_ref, wvt_ref, send_ref, q_ref, k_ref, vt_ref):
    first, last, members = part
    visible, width = normed_ref.shape
    rows, middle = visible // CLASSES, visible // 2
    low, high = first * HDIM, last * HDIM
    normed = normed_ref[...]
    q_ref[...] = (dot(normed, w_ref[:, low:high]) * HDIM ** (-0.5)).astype(jnp.bfloat16)
    k_ref[...] = dot(normed, w_ref[:, width + low : width + high]).astype(jnp.bfloat16)
    vt_ref[...] = dot_nt(wvt_ref[low:high, :], normed).astype(jnp.bfloat16)
    wide = 2 * HDIM

    def place_pair(left, left_odd, right, right_odd):
        left = swap(left) if left_odd else left
        right = right if right_odd else swap(right)
        lanes = lax.broadcasted_iota(jnp.int32, left.shape, 1)
        return jnp.where(lanes < HDIM, left, right)

    for head in range(first, last):
        at, odd = (head - first) // 2 * wide, head % 2
        keys = place_pair(k_ref[:middle, at : at + wide], odd, k_ref[middle:, at : at + wide], odd)
        values = vt_ref[(head - first) * HDIM : (head - first + 1) * HDIM, :]
        for member, (heads, _) in enumerate(members):
            for place in [place for place, one in enumerate(heads) if one == head]:
                base = place * visible
                send_ref[member, base : base + middle, :] = keys
                for i in range(visible // wide):
                    top = base + middle + i * HDIM
                    send_ref[member, top : top + HDIM, :] = values[:, i * wide : (i + 1) * wide]
    for member, (heads, units) in enumerate(members):
        for i in range(0, len(units), 2):
            tiles = []
            for place, cls in units[i : i + 2]:
                at = (heads[place] - first) // 2 * wide
                tiles += [q_ref[cls * rows : (cls + 1) * rows, at : at + wide], heads[place] % 2]
            top = len(heads) * visible + i // 2 * rows
            send_ref[member, top : top + rows, :] = place_pair(*tiles)


def first_kernel(part, slot_ref, arrived_ref, gain_ref, w_ref, wvt_ref, rows_ref, normed_ref, send_ref, *scratch):
    gather_rows(slot_ref, arrived_ref, gain_ref, rows_ref, normed_ref)
    project_part(part, normed_ref, w_ref, wvt_ref, send_ref, *scratch)


def attend_kernel(visible, heads, place_ref, class_ref, block_ref, out_ref):
    members = block_ref.shape[0]
    rows, middle = visible // CLASSES, visible // 2
    group = SEG // visible
    segments = members // group
    wide = 2 * HDIM
    step = pl.program_id(0)
    top = pl.multiple_of(heads * visible + step * rows, rows)
    low = lax.broadcasted_iota(jnp.int32, (group * rows, wide), 1) < HDIM

    for segment in range(segments):
        queries = jnp.concatenate(
            [block_ref[segment * group + i, pl.ds(top, rows), :] for i in range(group)], axis=0
        )
        turned = swap(queries)
        none = jnp.zeros_like(queries)
        halves = []
        for half in range(2):
            cls = class_ref[2 * step + half]
            base = pl.multiple_of(place_ref[2 * step + half] * visible, visible)
            offsets = []
            for other in range(CLASSES):
                apart = jnp.bitwise_and(other - cls, CLASSES - 1)
                offset = jnp.where(jnp.bitwise_and(apart, 1) == 0, math.log(2.0), 0.0)
                offset = jnp.where(apart == 4, math.log(3.0), offset)
                offsets.append(jnp.where(apart == 0, math.log(4.0), offset))
            left = jnp.where(low, turned if half else queries, none)
            right = jnp.where(low, none, queries if half else turned)
            far = jnp.where(cls >= CLASSES // 2, right, left)
            odd = jnp.bitwise_and(cls, 1) == 1

            blocks = []
            for i in range(group):
                member = segment * group + i
                keys = block_ref[member, pl.ds(base, middle), :]
                for side in range(2):
                    count = visible // wide // 2
                    values = [
                        block_ref[member, pl.ds(base + middle + (side * count + j) * HDIM, HDIM), :]
                        for j in range(count)
                    ]
                    score = dot_nt(keys, right if side else left)
                    blocks.append((score, offsets[side * 4 : side * 4 + 4], jnp.concatenate(values, axis=1)))
            for other in range(segments):
                if other == segment:
                    continue
                keys, values = [], []
                for i in range(group):
                    member = other * group + i
                    at = pl.multiple_of(base + jnp.bitwise_and(cls, CLASSES // 2 - 1) * rows, rows)
                    keys.append(block_ref[member, pl.ds(at, rows), :])
                    at = pl.multiple_of(base + middle + jnp.right_shift(cls, 1) * HDIM, HDIM)
                    tile = block_ref[member, pl.ds(at, HDIM), :]
                    values.append(jnp.where(odd, swap(tile), tile)[:, :HDIM])
                score = dot_nt(jnp.concatenate(keys, axis=0), far)
                blocks.append((score, [0.0] * 4, jnp.concatenate(values, axis=1)))

            peak = jnp.max(functools.reduce(jnp.maximum, [score for score, _, _ in blocks]), axis=0, keepdims=True)
            weights = [
                jnp.exp(score[i * rows : (i + 1) * rows] - (peak - offset)).astype(jnp.bfloat16)
                for score, shifts, _ in blocks
                for i, offset in enumerate(shifts)
            ]
            values = jnp.concatenate([value for _, _, value in blocks], axis=1)
            values = jnp.concatenate([values, jnp.ones((16, values.shape[1]), jnp.bfloat16)], axis=0)
            mixed = dot(values, jnp.concatenate(weights, axis=0))
            halves.append(mixed[:HDIM] / mixed[HDIM : HDIM + 1])
        both = jnp.concatenate(halves, axis=0).T.astype(jnp.bfloat16)
        for i in range(group):
            out_ref[segment * group + i, :, :] = both[i * rows : (i + 1) * rows, :]


def finish_kernel(parts, slot_ref, *refs):
    mixed_refs, (rows_ref, gain_ref, w_ref, out_ref, attended_ref) = refs[: len(parts)], refs[len(parts) :]
    visible, _ = rows_ref.shape
    part = visible // CLASSES
    slots = out_ref.shape[0]
    where = {}
    for mixed_ref, (_, _, members) in zip(mixed_refs, parts):
        for member, (heads, units) in enumerate(members):
            for i, (place, cls) in enumerate(units):
                where.setdefault((heads[place], cls), (mixed_ref, member, i))
    for head in range(0, HEADS, 2):
        for cls in range(CLASSES):
            pair = []
            for one in (head, head + 1):
                mixed_ref, member, i = where[(one, cls)]
                tile = mixed_ref[member, i // 2 * part : (i // 2 + 1) * part, :]
                pair.append(tile[:, i % 2 * HDIM : (i % 2 + 1) * HDIM])
            attended_ref[cls * part : (cls + 1) * part, head * HDIM : (head + 2) * HDIM] = (
                jnp.concatenate(pair, axis=1)
            )
    hidden = rows_ref[...].astype(jnp.float32) + dot(attended_ref[...], w_ref[...])
    answer = layer_norm(hidden, gain_ref[...]).astype(jnp.bfloat16)
    step = math.gcd(slots, 256)
    for start in range(0, slots, step):
        wanted = lax.broadcasted_iota(jnp.int32, (step, visible), 0) + start
        out_ref[start : start + step, :] = dot(one_hot(wanted, slot_ref[...]), answer).astype(
            jnp.bfloat16
        )


def unpack_kernel(slot_ref, back_ref, out_ref):
    count, _ = out_ref.shape
    slots = back_ref.shape[0]
    step = math.gcd(count, 256)
    for start in range(0, count, step):
        here = lax.broadcasted_iota(jnp.int32, (step, slots), 1)
        chosen = one_hot(slot_ref[start : start + step, :], here)
        out_ref[start : start + step, :] = dot(chosen, back_ref[...]).astype(jnp.bfloat16)


IN_VMEM = pl.BlockSpec(memory_space=pltpu.VMEM)
WHOLE = pl.BlockSpec()


def call(kernel, outs, out_specs, name, *operands, in_specs=None, scratch=()):
    return pl.pallas_call(
        kernel,
        out_shape=outs,
        in_specs=in_specs or [IN_VMEM] * len(operands),
        out_specs=out_specs,
        scratch_shapes=list(scratch),
        compiler_params=pltpu.CompilerParams(vmem_limit_bytes=VMEM),
        name=name,
    )(*operands)


def on_device(tiles, dest_table, owner_row, w_qkv, w_out, gain_attn, gain_out):
    groups = lax.axis_size("group")
    axes = ("group", "high", "low")
    inside = ("high", "low")
    members = lax.axis_size(inside)
    devices = groups * members
    count, width = tiles.shape
    visible = owner_row.shape[1]
    capacity = 2 * visible // devices
    slots = devices * capacity
    rows = visible // CLASSES
    parts = parts_of(members)
    bf16 = jnp.bfloat16

    moves = [(s * groups + g, g * members + s) for g in range(groups) for s in range(members)]
    owners = lax.ppermute(owner_row.reshape(visible // 128, 128), axes, moves).reshape(visible)
    owners = owners.reshape(rows, CLASSES).T.reshape(visible)

    outgoing, send_slot = call(
        functools.partial(pack_kernel, visible, capacity),
        (jax.ShapeDtypeStruct((slots, width), bf16), jax.ShapeDtypeStruct((1, count), jnp.int32)),
        (WHOLE, IN_VMEM),
        "pack",
        dest_table.reshape(1, count),
        tiles,
        in_specs=[IN_VMEM, pl.BlockSpec(memory_space=pl.ANY)],
        scratch=[pltpu.VMEM((count, width), bf16), pltpu.SemaphoreType.DMA],
    )
    arrived = lax.all_to_all(
        outgoing.reshape(devices, capacity, width), axes, split_axis=0, concat_axis=0, tiled=True
    ).reshape(slots, width)

    source = owners // count
    same = source[:, None] == source[None, :]
    earlier = owners[None, :] < owners[:, None]
    placed = jnp.sum((same & earlier).astype(jnp.int32), axis=1)
    slot = source * capacity + placed

    weights = (w_qkv, w_qkv[:, 2 * width :].T)
    blocks = []
    for i, part in enumerate(parts):
        first, last, dealt = part
        heads, units = len(dealt[0][0]), len(dealt[0][1])
        shape = jax.ShapeDtypeStruct((members, heads * visible + units // 2 * rows, 2 * HDIM), bf16)
        size = (last - first) * HDIM
        scratch = [pltpu.VMEM((visible, size), bf16)] * 2 + [pltpu.VMEM((size, visible), bf16)]
        if i == 0:
            student, normed, send = call(
                functools.partial(first_kernel, part),
                (jax.ShapeDtypeStruct((visible, width), bf16),) * 2 + (shape,),
                (WHOLE, IN_VMEM, WHOLE),
                "project_first",
                slot[:, None],
                arrived,
                gain_attn[None, :],
                *weights,
                scratch=scratch,
            )
        else:
            kernel = functools.partial(project_part, part)
            send = call(kernel, shape, WHOLE, "project_next", normed, *weights, scratch=scratch)
        if blocks:
            blocks[-1], send = lax.optimization_barrier((blocks[-1], send))
        blocks.append(lax.all_to_all(send, inside, split_axis=0, concat_axis=0, tiled=True))

    mixed = []
    for (_, _, part), block in zip(parts, blocks):
        heads, units = len(part[0][0]), len(part[0][1])
        table = jnp.array([list(zip(*units)) for _, units in part], jnp.int32)[lax.axis_index(inside)]
        result = pl.pallas_call(
            functools.partial(attend_kernel, visible, heads),
            out_shape=jax.ShapeDtypeStruct((members, units // 2 * rows, 2 * HDIM), bf16),
            grid_spec=pltpu.PrefetchScalarGridSpec(
                num_scalar_prefetch=2,
                grid=(units // 2,),
                in_specs=[IN_VMEM],
                out_specs=pl.BlockSpec((members, rows, 2 * HDIM), lambda i, *_: (0, i, 0)),
            ),
            compiler_params=pltpu.CompilerParams(vmem_limit_bytes=VMEM),
            name="attend",
        )(table[0], table[1], block)
        mixed.append(lax.all_to_all(result, inside, split_axis=0, concat_axis=0, tiled=True))

    answers = call(
        functools.partial(finish_kernel, parts),
        jax.ShapeDtypeStruct((slots, width), bf16),
        WHOLE,
        "finish",
        slot[None, :],
        *mixed,
        student,
        gain_out[None, :],
        w_out,
        scratch=[pltpu.VMEM((visible, width), bf16)],
    )
    back = lax.all_to_all(
        answers.reshape(devices, capacity, width), axes, split_axis=0, concat_axis=0, tiled=True
    ).reshape(slots, width)
    shape = jax.ShapeDtypeStruct((count, width), bf16)
    return call(unpack_kernel, shape, WHOLE, "unpack", send_slot.reshape(count, 1), back)


def solution(mesh):
    n_seq, n_slide = mesh.shape["seq"], mesh.shape["slide"]
    split = Mesh(
        mesh.devices.reshape(n_slide, n_seq // n_slide, n_slide), ("group", "high", "low")
    )
    every = ("group", "high", "low")
    in_specs = (P(every, None), P(every), P("low", ("group", "high")), P(), P(), P(), P())
    return jax.shard_map(
        on_device, mesh=split, in_specs=in_specs, out_specs=P(every, None), check_vma=False
    )
```

time: 197 us -> 190 us (0.964)
  waiting for transfers between devices: 103 us -> 93.7 us
  starting transfers between devices: 19.3 us -> 27.8 us
  Pallas kernels: 50.1 us -> 43.8 us
  other arithmetic: 3.94 us -> 1.15 us
  local copies, waits for them, and re-layouts: 19.8 us -> 22.4 us
    all_to_all x1 -> x2, waiting for transfers between devices: 34.4 us -> 16.8 us  [on_device(): lax.all_to_all(send, inside, split_axis=0, concat_axis=0, tiled=True)]
    all_to_all x1, waiting for transfers between devices: 21.1 us -> 32.7 us  [on_device(): lax.all_to_all(outgoing.reshape(devices, capacity, width), axes, split_ax...]
    unnamed x15 -> x47, local copies, waits for them, and re-layouts: 8.18 us -> 18.6 us
    reshape x3 -> x1, local copies, waits for them, and re-layouts: 6.83 us -> 0.08 us  [on_device(): owners = owners.reshape(rows, CLASSES).T.reshape(visible)]
    pallas_call x5 -> x7, Pallas kernels: 50.1 us -> 43.8 us  [the longest x2 29.7 us: on_device(): pl.pallas_call(functools.partial(attend_kernel, visible, heads), out_shap...]
    all_to_all x1 -> x2, starting transfers between devices: 3.73 us -> 8.45 us  [on_device(): lax.all_to_all(result, inside, split_axis=0, concat_axis=0, tiled=True)]
    all_to_all x1 -> x2, waiting for transfers between devices: 11 us -> 6.71 us  [on_device(): lax.all_to_all(result, inside, split_axis=0, concat_axis=0, tiled=True)]
    all_to_all x1 -> x2, starting transfers between devices: 4.67 us -> 8.55 us  [on_device(): lax.all_to_all(send, inside, split_axis=0, concat_axis=0, tiled=True)]
  transfers between devices with their start and end apart: 5 -> 7, of which waited for: 4 -> 4; matrix products, arithmetic and copies ran while one was open for 10% -> 3% of each run, Pallas kernels for 0% -> 16%
where the time goes in v2:
time: 190 us; the launch traced here: 189 us
  waiting for transfers between devices  93.7 us (49%)
  Pallas kernels  43.8 us (23%)
  starting transfers between devices  27.8 us (15%)
  local copies, waits for them, and re-layouts  22.4 us (12%)
    all_to_all x1, waiting for transfers between devices, on_device(): lax.all_to_all(answers.reshape(devices, capacity, width), axes, split_axi...  37.5 us
    all_to_all x1, waiting for transfers between devices, on_device(): lax.all_to_all(outgoing.reshape(devices, capacity, width), axes, split_ax...  32.7 us
    pallas_call x2, Pallas kernels, on_device(): pl.pallas_call(functools.partial(attend_kernel, visible, heads), out_shap...  29.7 us
    unnamed x47, local copies, waits for them, and re-layouts  18.6 us
    all_to_all x2, waiting for transfers between devices, on_device(): lax.all_to_all(send, inside, split_axis=0, concat_axis=0, tiled=True)  16.8 us
    pallas_call x5, Pallas kernels, call(): pl.pallas_call(kernel, out_shape=outs, in_specs=in_specs or [IN_VMEM] * l...  14.1 us
    all_to_all x2, starting transfers between devices, on_device(): lax.all_to_all(send, inside, split_axis=0, concat_axis=0, tiled=True)  8.55 us
    all_to_all x2, starting transfers between devices, on_device(): lax.all_to_all(result, inside, split_axis=0, concat_axis=0, tiled=True)  8.45 us
  transfers between devices with their start and end apart: 7, of which 4 were waited for; matrix products, arithmetic and copies ran while one was open for 3% of the time, Pallas kernels for 16%

profile of v2, /device:TPU:0, one launch (start us, length us, event | category | flops | bytes accessed | tf_op | source)
XLA Modules:
  0.0 189.1 jit_solution(17533886268986137700)
XLA Ops:
  0.7 1.5 copy-done.7
  2.2 2.7 %pack.1 = (bf16[1024,768]{1,0:T(8,128)(2,1)S(1)}, s32[1,1280]{1,0:T(1,128)S(1)}) custom-call(s32[1,1280]{1,0:T(1,128)S(1)} %reshape.174.dest_ref, bf16[1280,768]{1,0:T(8,128)(2,1)S(1)} %copy-done.7), custom_call_target="tpu_custom_call" | custom-call | tf_op jit(solution)/shard_map/pack/pallas_call | solution.py:269
  5.0 1.1 copy-done.8
  6.1 7.3 %all-to-all-start = ((bf16[32,32,768]{2,1,0:T(8,128)(2,1)}), bf16[32,32,768]{2,1,0:T(8,128)(2,1)S(1)}, u32[]{:S(2)}, u32[]{:S(2)}) async-start(bf16[32,32,768]{2,1,0:T(8,128)(2,1)} %bitcast.24), calls=%async_computation | async-start | bytes 3145728 | tf_op jit(solution)/shard_map/all_to_all | solution.py:308
  14.7 1.5 copy.51
  18.4 32.7 %all-to-all-done = bf16[32,32,768]{2,1,0:T(8,128)(2,1)S(1)} async-done(((bf16[32,32,768]{2,1,0:T(8,128)(2,1)}), bf16[32,32,768]{2,1,0:T(8,128)(2,1)S(1)}, u32[]{:S(2)}, u32[]{:S(2)}) %all-to-all-start) | async-done | bytes 1572896 | tf_op jit(solution)/shard_map/all_to_all | solution.py:308
  51.2 1.1 copy-done.4
  52.3 2.0 %copy-done = bf16[768,2304]{1,0:T(8,128)(2,1)S(1)} copy-done((bf16[768,2304]{1,0:T(8,128)(2,1)S(1)}, bf16[768,2304]{1,0:T(8,128)(2,1)}, u32[]{:S(2)}) %copy-start) | copy-done | bytes 3538968
  54.3 1.3 copy-done.2
  55.6 1.4 copy-done.5
  57.0 0.9 copy-done.11
  57.9 3.5 %project_first.1 = (bf16[512,768]{1,0:T(8,128)(2,1)S(1)}, bf16[512,768]{1,0:T(8,128)(2,1)S(1)}, bf16[8,768,128]{2,1,0:T(8,128)(2,1)S(1)}) custom-call(s32[512,1]{1,0:T(8,128)S(1)} %copy-done.11, bf16[1024,768]{1,0:T(8,128)(2,1)S(1)} %bitcast.22, f32[1,768]{1,0:T(1,128)S(1)} %broadcast_in_dim.4.gain_ref, bf16[768,2304]{1,0:T(8,128)(2,1)S(1)} %copy-done, ...), custom_call_target="tpu_custom_call" | custom-call | tf_op jit(solution)/shard_map/project_first/pallas_call | solution.py:269
  61.5 1.1 copy-done.9
  62.6 0.9 copy-done.12
  63.5 0.9 copy-done.14
  64.4 5.0 %all-to-all-start.1 = ((bf16[8,768,128]{2,1,0:T(8,128)(2,1)}), bf16[8,768,128]{2,1,0:T(8,128)(2,1)}, u32[]{:S(2)}, u32[]{:S(2)}) async-start(bf16[8,768,128]{2,1,0:T(8,128)(2,1)} %copy-done.9), calls=%async_computation.1 | async-start | bytes 3145728 | tf_op jit(solution)/shard_map/all_to_all | solution.py:343
  69.4 1.3 copy-done.3
  70.7 1.1 copy-done.15
  71.8 0.8 project_next.1
  72.6 1.0 copy-done.6
  73.7 16.8 %all-to-all-done.1.block_ref = bf16[8,768,128]{2,1,0:T(8,128)(2,1)} async-done(((bf16[8,768,128]{2,1,0:T(8,128)(2,1)}), bf16[8,768,128]{2,1,0:T(8,128)(2,1)}, u32[]{:S(2)}, u32[]{:S(2)}) %all-to-all-start.1) | async-done | bytes 1572896 | tf_op jit(solution)/shard_map/all_to_all | solution.py:343
  90.5 3.6 %all-to-all-start.3 = ((bf16[8,640,128]{2,1,0:T(8,128)(2,1)}), bf16[8,640,128]{2,1,0:T(8,128)(2,1)S(1)}, u32[]{:S(2)}, u32[]{:S(2)}) async-start(bf16[8,640,128]{2,1,0:T(8,128)(2,1)} %copy-done.6), calls=%async_computation.3 | async-start | bytes 2621440 | tf_op jit(solution)/shard_map/all_to_all | solution.py:343
  94.8 19.8 %attend.2 = bf16[8,256,128]{2,1,0:T(8,128)(2,1)} custom-call(s32[8]{0:T(128)S(1)} %get-tuple-element.22.place_ref, s32[8]{0:T(128)S(1)} %get-tuple-element.21.class_ref, bf16[8,768,128]{2,1,0:T(8,128)(2,1)} %all-to-all-done.1.block_ref), custom_call_target="tpu_custom_call" | custom-call | tf_op jit(solution)/shard_map/attend/pallas_call | solution.py:349
  114.6 4.3 %all-to-all-start.2 = ((bf16[8,256,128]{2,1,0:T(8,128)(2,1)}), bf16[8,256,128]{2,1,0:T(8,128)(2,1)S(1)}, u32[]{:S(2)}, u32[]{:S(2)}) async-start(bf16[8,256,128]{2,1,0:T(8,128)(2,1)} %attend.2), calls=%async_computation.2 | async-start | bytes 1048576 | tf_op jit(solution)/shard_map/all_to_all | solution.py:361
  119.6 9.8 %attend.3 = bf16[8,128,128]{2,1,0:T(8,128)(2,1)} custom-call(s32[4]{0:T(128)S(1)} %get-tuple-element.20.place_ref, s32[4]{0:T(128)S(1)} %get-tuple-element.19.class_ref, bf16[8,640,128]{2,1,0:T(8,128)(2,1)S(1)} %all-to-all-done.3.block_ref), custom_call_target="tpu_custom_call" | custom-call | tf_op jit(solution)/shard_map/attend/pallas_call | solution.py:349
  129.4 4.2 %all-to-all-start.4 = ((bf16[8,128,128]{2,1,0:T(8,128)(2,1)}), bf16[8,128,128]{2,1,0:T(8,128)(2,1)S(1)}, u32[]{:S(2)}, u32[]{:S(2)}) async-start(bf16[8,128,128]{2,1,0:T(8,128)(2,1)} %attend.3), calls=%async_computation.4 | async-start | bytes 524288 | tf_op jit(solution)/shard_map/all_to_all | solution.py:361
  133.8 6.7 %all-to-all-done.4.refs_1_ = bf16[8,128,128]{2,1,0:T(8,128)(2,1)S(1)} async-done(((bf16[8,128,128]{2,1,0:T(8,128)(2,1)}), bf16[8,128,128]{2,1,0:T(8,128)(2,1)S(1)}, u32[]{:S(2)}, u32[]{:S(2)}) %all-to-all-start.4) | async-done | bytes 262176 | tf_op jit(solution)/shard_map/all_to_all | solution.py:361
  140.5 1.1 copy-done.13
  141.7 3.5 %finish.1 = bf16[1024,768]{1,0:T(8,128)(2,1)} custom-call(s32[1,512]{1,0:T(1,128)S(1)} %fusion.4.slot_ref, bf16[8,256,128]{2,1,0:T(8,128)(2,1)S(1)} %all-to-all-done.2.refs_0_, bf16[8,128,128]{2,1,0:T(8,128)(2,1)S(1)} %all-to-all-done.4.refs_1_, bf16[512,768]{1,0:T(8,128)(2,1)S(1)} %copy-done.13, f32[1,768]{1,0:T(1,128)S(1)} %broadcast_in_dim.5.refs_3_, ...), custom_call_target="tpu_custom_call" | custom-call | tf_op jit(solution)/shard_map/finish/pallas_call | solution.py:269
  145.2 2.7 %all-to-all-start.5 = ((bf16[32,32,768]{2,1,0:T(8,128)(2,1)}), bf16[32,32,768]{2,1,0:T(8,128)(2,1)S(1)}, u32[]{:S(2)}, u32[]{:S(2)}) async-start(bf16[32,32,768]{2,1,0:T(8,128)(2,1)} %bitcast.12), calls=%async_computation.5 | async-start | bytes 3145728 | tf_op jit(solution)/shard_map/all_to_all | solution.py:375
  148.1 37.5 %all-to-all-done.5 = bf16[32,32,768]{2,1,0:T(8,128)(2,1)S(1)} async-done(((bf16[32,32,768]{2,1,0:T(8,128)(2,1)}), bf16[32,32,768]{2,1,0:T(8,128)(2,1)S(1)}, u32[]{:S(2)}, u32[]{:S(2)}) %all-to-all-start.5) | async-done | bytes 1572896 | tf_op jit(solution)/shard_map/all_to_all | solution.py:375
  185.6 3.5 %unpack.1 = bf16[1280,768]{1,0:T(8,128)(2,1)} custom-call(s32[1280,1]{1,0:T(8,128)S(1)} %copy.50.slot_ref, bf16[1024,768]{1,0:T(8,128)(2,1)S(1)} %bitcast.23), custom_call_target="tpu_custom_call" | custom-call | tf_op jit(solution)/shard_map/unpack/pallas_call | solution.py:269
  (60 shorter events, 6.0 us)
Async XLA Ops:
  0.7 1.5 copy-start.7
  5.0 1.1 copy-start.8
  6.1 7.3 %copy-start.22 = (s32[1,512]{1,0:T(1,128)S(1)}, s32[1,512]{1,0:T(1,128)}, u32[]{:S(2)}) copy-start(s32[1,512]{1,0:T(1,128)} %param.11) | copy-start | bytes 6148
  6.1 45.0 %all-to-all-start = ((bf16[32,32,768]{2,1,0:T(8,128)(2,1)}), bf16[32,32,768]{2,1,0:T(8,128)(2,1)S(1)}, u32[]{:S(2)}, u32[]{:S(2)}) async-start(bf16[32,32,768]{2,1,0:T(8,128)(2,1)} %bitcast.24), calls=%async_computation | async-start | bytes 3145728 | tf_op jit(solution)/shard_map/all_to_all | solution.py:308
  13.5 1.3 slice-start
  13.5 2.7 %collective-permute-start = (s32[4,128]{1,0:T(4,128)S(1)}, s32[4,128]{1,0:T(4,128)S(1)}, u32[]{:S(2)}, u32[]{:S(2)}) collective-permute-start(s32[4,128]{1,0:T(4,128)S(1)} %bitcast.29), channel_id=1, source_target_pairs={{0,0},{4,1},{8,2},{12,3},{16,4},{20,5},{24,6},{28,7},{1,8},{5,9},{... | collective-permute-start | bytes 6152 | tf_op jit(solution)/shard_map/ppermute | solution.py:295
  14.7 1.5 copy-start.20
  16.8 0.6 copy-start.16
  17.4 34.9 %copy-start.18 = (pred[8,64]{1,0:T(8,128)(4,1)}, pred[8,64]{1,0:T(8,128)(4,1)S(1)}, u32[]{:S(2)}) copy-start(pred[8,64]{1,0:T(8,128)(4,1)S(1)} %fusion.2) | copy-start | bytes 1540
  51.2 1.1 copy-start.4
  52.3 2.0 %copy-start = (bf16[768,2304]{1,0:T(8,128)(2,1)S(1)}, bf16[768,2304]{1,0:T(8,128)(2,1)}, u32[]{:S(2)}) copy-start(bf16[768,2304]{1,0:T(8,128)(2,1)} %w_ref.3) | copy-start | bytes 10616836
  54.3 1.3 copy-start.2
  55.6 1.4 copy-start.5
  57.0 0.9 copy-start.11
  57.9 11.4 %copy-start.1 = (bf16[768,2304]{1,0:T(8,128)(2,1)S(1)}, bf16[768,2304]{1,0:T(8,128)(2,1)}, u32[]{:S(2)}) copy-start(bf16[768,2304]{1,0:T(8,128)(2,1)} %w_ref.3) | copy-start | bytes 10616836
  61.5 1.1 copy-start.9
  62.6 0.9 copy-start.12
  63.5 0.9 copy-start.14
  64.4 26.1 %all-to-all-start.1 = ((bf16[8,768,128]{2,1,0:T(8,128)(2,1)}), bf16[8,768,128]{2,1,0:T(8,128)(2,1)}, u32[]{:S(2)}, u32[]{:S(2)}) async-start(bf16[8,768,128]{2,1,0:T(8,128)(2,1)} %copy-done.9), calls=%async_computation.1 | async-start | bytes 3145728 | tf_op jit(solution)/shard_map/all_to_all | solution.py:343
  69.4 1.3 copy-start.3
  70.7 1.1 copy-start.15
  72.6 1.1 copy-start.6
  90.5 24.1 %all-to-all-start.3 = ((bf16[8,640,128]{2,1,0:T(8,128)(2,1)}), bf16[8,640,128]{2,1,0:T(8,128)(2,1)S(1)}, u32[]{:S(2)}, u32[]{:S(2)}) async-start(bf16[8,640,128]{2,1,0:T(8,128)(2,1)} %copy-done.6), calls=%async_computation.3 | async-start | bytes 2621440 | tf_op jit(solution)/shard_map/all_to_all | solution.py:343
  114.6 19.0 %copy-start.21 = (f32[768]{0:T(1024)S(1)}, f32[768]{0:T(1024)}, u32[]{:S(2)}) copy-start(f32[768]{0:T(1024)} %param.15) | copy-start | bytes 9220
  114.6 19.1 %copy-start.19 = (pred[8,64]{1,0:T(8,128)(4,1)S(1)}, pred[8,64]{1,0:T(8,128)(4,1)}, u32[]{:S(2)}) copy-start(pred[8,64]{1,0:T(8,128)(4,1)} %copy-done.18) | copy-start | bytes 1540
  114.6 19.2 %copy-start.17 = (s32[512]{0:T(512)S(1)}, s32[512]{0:T(512)}, u32[]{:S(2)}) copy-start(s32[512]{0:T(512)} %copy-done.16) | copy-start | bytes 6148
  114.6 25.9 %copy-start.10 = (bf16[768,768]{1,0:T(8,128)(2,1)S(1)}, bf16[768,768]{1,0:T(8,128)(2,1)}, u32[]{:S(2)}) copy-start(bf16[768,768]{1,0:T(8,128)(2,1)} %refs_4_.1) | copy-start | bytes 3538948
  114.6 14.8 %all-to-all-start.2 = ((bf16[8,256,128]{2,1,0:T(8,128)(2,1)}), bf16[8,256,128]{2,1,0:T(8,128)(2,1)S(1)}, u32[]{:S(2)}, u32[]{:S(2)}) async-start(bf16[8,256,128]{2,1,0:T(8,128)(2,1)} %attend.2), calls=%async_computation.2 | async-start | bytes 1048576 | tf_op jit(solution)/shard_map/all_to_all | solution.py:361
  129.4 11.1 %all-to-all-start.4 = ((bf16[8,128,128]{2,1,0:T(8,128)(2,1)}), bf16[8,128,128]{2,1,0:T(8,128)(2,1)S(1)}, u32[]{:S(2)}, u32[]{:S(2)}) async-start(bf16[8,128,128]{2,1,0:T(8,128)(2,1)} %attend.3), calls=%async_computation.4 | async-start | bytes 524288 | tf_op jit(solution)/shard_map/all_to_all | solution.py:361
  140.5 1.1 copy-start.13
  145.2 40.5 %all-to-all-start.5 = ((bf16[32,32,768]{2,1,0:T(8,128)(2,1)}), bf16[32,32,768]{2,1,0:T(8,128)(2,1)S(1)}, u32[]{:S(2)}, u32[]{:S(2)}) async-start(bf16[32,32,768]{2,1,0:T(8,128)(2,1)} %bitcast.12), calls=%async_computation.5 | async-start | bytes 3145728 | tf_op jit(solution)/shard_map/all_to_all | solution.py:375

commit v3 on v2

v3 whole, which is shorter than its diff:
```python
import functools
import itertools
import math

import jax
import jax.numpy as jnp
from jax import lax
from jax.experimental import pallas as pl
from jax.experimental.pallas import tpu as pltpu
from jax.sharding import Mesh
from jax.sharding import PartitionSpec as P

HEADS = 12
HDIM = 64
SEG = 2048
CLASSES = 8
EPS = 1e-05
VMEM = 24 << 20


def layer_norm(inputs, gain):
    average = jnp.mean(inputs, axis=-1, keepdims=True)
    centred = inputs - average
    spread = jnp.mean(centred * centred, axis=-1, keepdims=True)
    return centred * lax.rsqrt(spread + EPS) * gain


def one_hot(left, right):
    return jnp.where(left == right, 1.0, 0.0).astype(jnp.bfloat16)


def dot(left, right):
    return jnp.dot(left, right, preferred_element_type=jnp.float32)


def parts_of(members):
    full = HEADS // members
    every = [(0, cls) for cls in range(CLASSES)]
    parts = [
        (i * members, (i + 1) * members, [([i * members + member], every) for member in range(members)])
        for i in range(full)
    ]
    first = full * members
    owned = (HEADS - first) * CLASSES // members
    if owned:
        dealt = []
        for member in range(members):
            units = [divmod(first * CLASSES + member * owned + i, CLASSES) for i in range(owned)]
            dealt.append((sorted({head for head, _ in units}), units))
        width = max(len(heads) for heads, _ in dealt)
        part = []
        for heads, units in dealt:
            units = [(heads.index(head), cls) for head, cls in units]
            part.append((heads + heads[-1:] * (width - len(heads)), units + units[-1:] * (owned % 2)))
        parts.append((first, HEADS, part))
    return parts


def swap(tile):
    return jnp.concatenate([tile[:, HDIM:], tile[:, :HDIM]], axis=1)


def dot_nt(left, right):
    return lax.dot_general(left, right, (((1,), (1,)), ((), ())), preferred_element_type=jnp.float32)


def pack_kernel(visible, capacity, dest_ref, tiles_hbm, out_hbm, slot_ref, tiles_ref, out_ref, sem, sems):
    fetch = pltpu.make_async_copy(tiles_hbm, tiles_ref, sem)
    fetch.start()
    slots, _ = out_ref.shape
    count = dest_ref.shape[1]
    devices = slots // capacity
    target = jnp.right_shift(dest_ref[...], visible.bit_length() - 1)
    lanes = 128
    before = one_hot_lt(lanes)
    offset = jnp.zeros((devices, 1), jnp.float32)
    pieces = []
    for start in range(0, count, lanes):
        here = target[:, start : start + lanes]
        device = lax.broadcasted_iota(jnp.int32, (devices, lanes), 0)
        chosen = jnp.where(device == here, 1.0, 0.0)
        rank = dot(chosen.astype(jnp.bfloat16), before) + offset
        placed = jnp.sum(chosen * rank, axis=0, keepdims=True).astype(jnp.int32)
        pieces.append(jnp.where(here >= 0, here * capacity + placed, -1))
        offset = offset + jnp.sum(chosen, axis=1, keepdims=True)
    slot = jnp.concatenate(pieces, axis=1)
    slot_ref[...] = slot
    fetch.wait()
    step = math.gcd(slots, 256)
    copies = []
    for start in range(0, slots, step):
        wanted = lax.broadcasted_iota(jnp.int32, (step, count), 0) + start
        rows = dot(one_hot(wanted, slot), tiles_ref[...])
        out_ref[start : start + step, :] = rows.astype(jnp.bfloat16)
        copies.append(write(out_ref, out_hbm, start, step, sems))
    for copy in copies:
        copy.wait()


def write(source, target, start, step, sems):
    at = pl.ds(start, step)
    copy = pltpu.make_async_copy(source.at[at], target.at[at], sems.at[start // step])
    copy.start()
    return copy


def one_hot_lt(size):
    row = lax.broadcasted_iota(jnp.int32, (size, size), 0)
    column = lax.broadcasted_iota(jnp.int32, (size, size), 1)
    return jnp.where(row < column, 1.0, 0.0).astype(jnp.bfloat16)


def project_part(part, normed, w_ref, wvt_ref, send_hbm, send_ref, q_ref, k_ref, vt_ref, sems):
    first, last, members = part
    visible, width = normed.shape
    rows, middle = visible // CLASSES, visible // 2
    low, high = 0, (last - first) * HDIM
    q_ref[...] = (dot(normed, w_ref[0]) * HDIM ** (-0.5)).astype(jnp.bfloat16)
    k_ref[...] = dot(normed, w_ref[1]).astype(jnp.bfloat16)
    vt_ref[...] = dot_nt(wvt_ref[...], normed).astype(jnp.bfloat16)
    wide = 2 * HDIM

    def place_pair(left, left_odd, right, right_odd):
        left = swap(left) if left_odd else left
        right = right if right_odd else swap(right)
        lanes = lax.broadcasted_iota(jnp.int32, left.shape, 1)
        return jnp.where(lanes < HDIM, left, right)

    for head in range(first, last):
        at, odd = (head - first) // 2 * wide, head % 2
        keys = place_pair(k_ref[:middle, at : at + wide], odd, k_ref[middle:, at : at + wide], odd)
        values = vt_ref[(head - first) * HDIM : (head - first + 1) * HDIM, :]
        for member, (heads, _) in enumerate(members):
            for place in [place for place, one in enumerate(heads) if one == head]:
                base = place * visible
                send_ref[member, base : base + middle, :] = keys
                for i in range(visible // wide):
                    top = base + middle + i * HDIM
                    send_ref[member, top : top + HDIM, :] = values[:, i * wide : (i + 1) * wide]
    copies = []
    for member, (heads, units) in enumerate(members):
        for i in range(0, len(units), 2):
            tiles = []
            for place, cls in units[i : i + 2]:
                at = (heads[place] - first) // 2 * wide
                tiles += [q_ref[cls * rows : (cls + 1) * rows, at : at + wide], heads[place] % 2]
            top = len(heads) * visible + i // 2 * rows
            send_ref[member, top : top + rows, :] = place_pair(*tiles)
        copies.append(write(send_ref, send_hbm, member, 1, sems))
    return copies


def fetch_weights(part, w_hbm, wvt_hbm, w_ref, wvt_ref, sems):
    width = w_hbm.shape[0]
    at, size = part[0] * HDIM, (part[1] - part[0]) * HDIM
    copies = [
        pltpu.make_async_copy(w_hbm.at[:, pl.ds(i * width + at, size)], w_ref.at[i], sems.at[i])
        for i in range(2)
    ]
    copies.append(pltpu.make_async_copy(wvt_hbm.at[pl.ds(at, size)], wvt_ref, sems.at[2]))
    for copy in copies:
        copy.start()
    return copies


def first_kernel(part, slot_ref, arrived_ref, gain_ref, w_hbm, wvt_hbm, rows_hbm, normed_hbm, send_hbm,
                 w_ref, wvt_ref, send_ref, q_ref, k_ref, vt_ref, sems, rows_ref, normed_ref, more):
    weights = fetch_weights(part, w_hbm, wvt_hbm, w_ref, wvt_ref, more)
    visible, slots = rows_ref.shape[0], arrived_ref.shape[0]
    chosen = one_hot(lax.broadcasted_iota(jnp.int32, (visible, slots), 1), slot_ref[...])
    rows = dot(chosen, arrived_ref[...])
    rows_ref[...] = rows.astype(jnp.bfloat16)
    normed = layer_norm(rows, gain_ref[...]).astype(jnp.bfloat16)
    normed_ref[...] = normed
    copies = [
        pltpu.make_async_copy(rows_ref, rows_hbm, more.at[3]),
        pltpu.make_async_copy(normed_ref, normed_hbm, more.at[4]),
    ]
    for copy in copies:
        copy.start()
    for copy in weights:
        copy.wait()
    copies += project_part(part, normed, w_ref, wvt_ref, send_hbm, send_ref, q_ref, k_ref, vt_ref, sems)
    for copy in copies:
        copy.wait()


def next_kernel(part, normed_ref, w_hbm, wvt_hbm, send_hbm, w_ref, wvt_ref, send_ref, q_ref, k_ref, vt_ref, sems, more):
    for copy in fetch_weights(part, w_hbm, wvt_hbm, w_ref, wvt_ref, more):
        copy.wait()
    for copy in project_part(part, normed_ref[...], w_ref, wvt_ref, send_hbm, send_ref, q_ref, k_ref, vt_ref, sems):
        copy.wait()


def attend_kernel(visible, heads, place_ref, class_ref, block_ref, out_ref, score_ref, peak_ref):
    members = block_ref.shape[0]
    rows, middle = visible // CLASSES, visible // 2
    group = SEG // visible
    segments = members // group
    wide = 2 * HDIM
    size = group * rows
    turns = out_ref.shape[1] // rows * segments
    low = lax.broadcasted_iota(jnp.int32, (size, wide), 1) < HDIM

    def tile_of(turn, half):
        step, segment = turn // segments, turn % segments
        cls = class_ref[2 * step + half]
        base = pl.multiple_of(place_ref[2 * step + half] * visible, visible)
        return step, segment, cls, base

    def member_of(segment, i, apart):
        return lax.rem(segment + apart, segments) * group + i

    def blocks_of(segment):
        near = [(member_of(segment, i, 0), side) for i in range(group) for side in range(2)]
        return near + [(apart, None) for apart in range(1, segments)]

    def score_steps(turn, half):
        step, segment, cls, base = tile_of(turn, half)
        top = pl.multiple_of(heads * visible + step * rows, rows)
        queries = jnp.concatenate(
            [block_ref[member_of(segment, i, 0), pl.ds(top, rows), :] for i in range(group)], axis=0
        )
        turned = swap(queries)
        none = jnp.zeros_like(queries)
        left = jnp.where(low, turned if half else queries, none)
        right = jnp.where(low, none, queries if half else turned)
        far = jnp.where(cls >= CLASSES // 2, right, left)
        peak = None
        for j, (member, side) in enumerate(blocks_of(segment)):
            if side is None:
                at = pl.multiple_of(base + jnp.bitwise_and(cls, CLASSES // 2 - 1) * rows, rows)
                keys = [block_ref[member_of(segment, i, member), pl.ds(at, rows), :] for i in range(group)]
                score = dot_nt(jnp.concatenate(keys, axis=0), far)
            else:
                score = dot_nt(block_ref[member, pl.ds(base, middle), :], right if side else left)
            score_ref[half, j * size : (j + 1) * size, :] = score
            highest = jnp.max(score.reshape(size // 8, 8, size), axis=0)
            peak = highest if peak is None else jnp.maximum(peak, highest)
            yield
        peak_ref[half] = jnp.broadcast_to(jnp.max(peak, axis=0, keepdims=True), peak.shape)
        yield

    def weight_steps(turn, half, results):
        step, segment, cls, base = tile_of(turn, half)
        peak = peak_ref[half]
        odd = jnp.bitwise_and(cls, 1) == 1
        mixed = jnp.zeros((HDIM + 16, size), jnp.float32)
        for j, (member, side) in enumerate(blocks_of(segment)):
            values = []
            if side is None:
                at = pl.multiple_of(base + middle + jnp.right_shift(cls, 1) * HDIM, HDIM)
                for i in range(group):
                    tile = block_ref[member_of(segment, i, member), pl.ds(at, HDIM), :]
                    values.append(jnp.where(odd, swap(tile), tile)[:, :HDIM])
                shifted = [peak] * group
            else:
                count = visible // wide // 2
                for i in range(count):
                    at = pl.multiple_of(base + middle + (side * count + i) * HDIM, HDIM)
                    values.append(block_ref[member, pl.ds(at, HDIM), :])
                shifted = []
                for other in range(side * 4, side * 4 + 4):
                    apart = jnp.bitwise_and(other - cls, CLASSES - 1)
                    offset = jnp.where(jnp.bitwise_and(apart, 1) == 0, math.log(2.0), 0.0)
                    offset = jnp.where(apart == 4, math.log(3.0), offset)
                    shifted.append(peak - jnp.where(apart == 0, math.log(4.0), offset))
            weights = []
            for i, one in enumerate(shifted):
                at = j * size + i * rows
                score = score_ref[half, at : at + rows, :].reshape(rows // 8, 8, size)
                weights.append(jnp.exp(score - one[None]).reshape(rows, size).astype(jnp.bfloat16))
            values = jnp.concatenate(values, axis=1)
            values = jnp.concatenate([values, jnp.ones((16, size), jnp.bfloat16)], axis=0)
            mixed += dot(values, jnp.concatenate(weights, axis=0))
            yield
        results.append(mixed[:HDIM] / mixed[HDIM : HDIM + 1])
        yield

    def run(*streams):
        for _ in itertools.zip_longest(*streams):
            pass

    def body(turn, carry):
        results = []
        run(weight_steps(turn, 0, results), score_steps(turn, 1))
        after = jnp.minimum(turn + 1, turns - 1)
        run(weight_steps(turn, 1, results), score_steps(after, 0))
        both = jnp.concatenate(results, axis=0).T.astype(jnp.bfloat16)
        step, segment = turn // segments, turn % segments
        for i in range(group):
            at = pl.multiple_of(step * rows, rows)
            out_ref[segment * group + i, pl.ds(at, rows), :] = both[i * rows : (i + 1) * rows, :]
        return carry

    run(score_steps(0, 0))
    lax.fori_loop(0, turns, body, 0)


def finish_kernel(parts, slot_ref, *refs):
    mixed_refs = refs[: len(parts)]
    rows_hbm, gain_ref, w_hbm, out_hbm, attended_ref, rows_ref, w_ref, out_ref, more, sems = refs[len(parts) :]
    fetches = [
        pltpu.make_async_copy(w_hbm, w_ref, more.at[0]),
        pltpu.make_async_copy(rows_hbm, rows_ref, more.at[1]),
    ]
    for copy in fetches:
        copy.start()
    visible, _ = rows_ref.shape
    part = visible // CLASSES
    slots = out_ref.shape[0]
    where = {}
    for mixed_ref, (_, _, members) in zip(mixed_refs, parts):
        for member, (heads, units) in enumerate(members):
            for i, (place, cls) in enumerate(units):
                where.setdefault((heads[place], cls), (mixed_ref, member, i))
    for head in range(0, HEADS, 2):
        for cls in range(CLASSES):
            pair = []
            for one in (head, head + 1):
                mixed_ref, member, i = where[(one, cls)]
                tile = mixed_ref[member, i // 2 * part : (i // 2 + 1) * part, :]
                pair.append(tile[:, i % 2 * HDIM : (i % 2 + 1) * HDIM])
            attended_ref[cls * part : (cls + 1) * part, head * HDIM : (head + 2) * HDIM] = (
                jnp.concatenate(pair, axis=1)
            )
    for copy in fetches:
        copy.wait()
    hidden = rows_ref[...].astype(jnp.float32) + dot(attended_ref[...], w_ref[...])
    answer = layer_norm(hidden, gain_ref[...]).astype(jnp.bfloat16)
    step = math.gcd(slots, 256)
    copies = []
    for start in range(0, slots, step):
        wanted = lax.broadcasted_iota(jnp.int32, (step, visible), 0) + start
        out_ref[start : start + step, :] = dot(one_hot(wanted, slot_ref[...]), answer).astype(
            jnp.bfloat16
        )
        copies.append(write(out_ref, out_hbm, start, step, sems))
    for copy in copies:
        copy.wait()


def unpack_kernel(slot_ref, back_ref, out_hbm, out_ref, sems):
    count = out_ref.shape[0]
    slots = back_ref.shape[0]
    step = math.gcd(count, 256)
    copies = []
    for start in range(0, count, step):
        here = lax.broadcasted_iota(jnp.int32, (step, slots), 1)
        chosen = one_hot(slot_ref[start : start + step, :], here)
        out_ref[start : start + step, :] = dot(chosen, back_ref[...]).astype(jnp.bfloat16)
        copies.append(write(out_ref, out_hbm, start, step, sems))
    for copy in copies:
        copy.wait()


IN_VMEM = pl.BlockSpec(memory_space=pltpu.VMEM)
IN_HBM = pl.BlockSpec(memory_space=pltpu.HBM)
COPIES = pltpu.SemaphoreType.DMA


def call(kernel, outs, out_specs, name, *operands, in_specs=None, scratch=()):
    in_specs = in_specs or [IN_VMEM] * len(operands)
    operands = [
        pltpu.with_memory_space_constraint(operand, pltpu.HBM) if spec is IN_HBM else operand
        for operand, spec in zip(operands, in_specs)
    ]
    outs = jax.tree.map(
        lambda out, spec: pltpu.HBM(out.shape, out.dtype) if spec is IN_HBM else out, outs, out_specs
    )
    return pl.pallas_call(
        kernel,
        out_shape=outs,
        in_specs=in_specs,
        out_specs=out_specs,
        scratch_shapes=list(scratch),
        compiler_params=pltpu.CompilerParams(vmem_limit_bytes=VMEM),
        name=name,
    )(*operands)


def on_device(tiles, dest_table, owner_row, w_qkv, w_out, gain_attn, gain_out):
    groups = lax.axis_size("group")
    axes = ("group", "high", "low")
    inside = ("high", "low")
    members = lax.axis_size(inside)
    devices = groups * members
    count, width = tiles.shape
    visible = owner_row.shape[1]
    capacity = 2 * visible // devices
    slots = devices * capacity
    rows = visible // CLASSES
    parts = parts_of(members)
    bf16 = jnp.bfloat16

    moves = [(s * groups + g, g * members + s) for g in range(groups) for s in range(members)]
    owners = lax.ppermute(owner_row.reshape(visible // 128, 128), axes, moves).reshape(visible)
    owners = owners.reshape(rows, CLASSES).T.reshape(visible)

    outgoing, send_slot = call(
        functools.partial(pack_kernel, visible, capacity),
        (jax.ShapeDtypeStruct((slots, width), bf16), jax.ShapeDtypeStruct((1, count), jnp.int32)),
        (IN_HBM, IN_VMEM),
        "pack",
        dest_table.reshape(1, count),
        tiles,
        in_specs=[IN_VMEM, IN_HBM],
        scratch=[
            pltpu.VMEM((count, width), bf16),
            pltpu.VMEM((slots, width), bf16),
            COPIES,
            COPIES((slots // math.gcd(slots, 256),)),
        ],
    )
    arrived = lax.all_to_all(
        outgoing.reshape(devices, capacity, width), axes, split_axis=0, concat_axis=0, tiled=True
    ).reshape(slots, width)

    source = owners // count
    same = source[:, None] == source[None, :]
    earlier = owners[None, :] < owners[:, None]
    placed = jnp.sum((same & earlier).astype(jnp.int32), axis=1)
    slot = source * capacity + placed

    weights = (w_qkv, w_qkv[:, 2 * width :].T)
    blocks = []
    for i, part in enumerate(parts):
        first, last, dealt = part
        heads, units = len(dealt[0][0]), len(dealt[0][1])
        shape = jax.ShapeDtypeStruct((members, heads * visible + units // 2 * rows, 2 * HDIM), bf16)
        size = (last - first) * HDIM
        scratch = [
            pltpu.VMEM((2, width, size), bf16),
            pltpu.VMEM((size, width), bf16),
            pltpu.VMEM(shape.shape, bf16),
            pltpu.VMEM((visible, size), bf16),
            pltpu.VMEM((visible, size), bf16),
            pltpu.VMEM((size, visible), bf16),
            COPIES((members,)),
        ]
        if i == 0:
            student, normed, send = call(
                functools.partial(first_kernel, part),
                (jax.ShapeDtypeStruct((visible, width), bf16),) * 2 + (shape,),
                (IN_HBM,) * 3,
                "project_first",
                slot[:, None],
                arrived,
                gain_attn[None, :],
                *weights,
                in_specs=[IN_VMEM] * 3 + [IN_HBM] * 2,
                scratch=scratch + [pltpu.VMEM((visible, width), bf16)] * 2 + [COPIES((5,))],
            )
        else:
            send = call(
                functools.partial(next_kernel, part),
                shape,
                IN_HBM,
                "project_next",
                normed,
                *weights,
                in_specs=[IN_VMEM] + [IN_HBM] * 2,
                scratch=scratch + [COPIES((3,))],
            )
        if blocks:
            blocks[-1], send = lax.optimization_barrier((blocks[-1], send))
        blocks.append(lax.all_to_all(send, inside, split_axis=0, concat_axis=0, tiled=True))

    mixed = []
    for (_, _, part), block in zip(parts, blocks):
        heads, units = len(part[0][0]), len(part[0][1])
        table = jnp.array([list(zip(*units)) for _, units in part], jnp.int32)[lax.axis_index(inside)]
        depth = SEG + (members * visible // SEG - 1) * SEG // CLASSES
        across = SEG // CLASSES
        result = pl.pallas_call(
            functools.partial(attend_kernel, visible, heads),
            out_shape=jax.ShapeDtypeStruct((members, units // 2 * rows, 2 * HDIM), bf16),
            grid_spec=pltpu.PrefetchScalarGridSpec(
                num_scalar_prefetch=2,
                grid=(1,),
                in_specs=[IN_VMEM],
                out_specs=pl.BlockSpec((members, units // 2 * rows, 2 * HDIM), lambda i, *_: (0, 0, 0)),
                scratch_shapes=[
                    pltpu.VMEM((2, depth, across), jnp.float32),
                    pltpu.VMEM((2, 8, across), jnp.float32),
                ],
            ),
            compiler_params=pltpu.CompilerParams(vmem_limit_bytes=VMEM),
            name="attend",
        )(table[0], table[1], block)
        mixed.append(lax.all_to_all(result, inside, split_axis=0, concat_axis=0, tiled=True))

    answers = call(
        functools.partial(finish_kernel, parts),
        jax.ShapeDtypeStruct((slots, width), bf16),
        IN_HBM,
        "finish",
        slot[None, :],
        *mixed,
        student,
        gain_out[None, :],
        w_out,
        in_specs=[IN_VMEM] * (1 + len(parts)) + [IN_HBM, IN_VMEM, IN_HBM],
        scratch=[
            pltpu.VMEM((visible, width), bf16),
            pltpu.VMEM((visible, width), bf16),
            pltpu.VMEM((width, width), bf16),
            pltpu.VMEM((slots, width), bf16),
            COPIES((2,)),
            COPIES((slots // math.gcd(slots, 256),)),
        ],
    )
    back = lax.all_to_all(
        answers.reshape(devices, capacity, width), axes, split_axis=0, concat_axis=0, tiled=True
    ).reshape(slots, width)
    shape = jax.ShapeDtypeStruct((count, width), bf16)
    return call(
        unpack_kernel,
        shape,
        IN_HBM,
        "unpack",
        send_slot.reshape(count, 1),
        back,
        scratch=[pltpu.VMEM((count, width), bf16), COPIES((count // math.gcd(count, 256),))],
    )


def solution(mesh):
    n_seq, n_slide = mesh.shape["seq"], mesh.shape["slide"]
    split = Mesh(
        mesh.devices.reshape(n_slide, n_seq // n_slide, n_slide), ("group", "high", "low")
    )
    every = ("group", "high", "low")
    in_specs = (P(every, None), P(every), P("low", ("group", "high")), P(), P(), P(), P())
    return jax.shard_map(
        on_device, mesh=split, in_specs=in_specs, out_specs=P(every, None), check_vma=False
    )
```

time: 190 us -> 176 us (0.926)
  local copies, waits for them, and re-layouts: 22.4 us -> 5.27 us
  waiting for transfers between devices: 93.7 us -> 101 us
  starting transfers between devices: 27.8 us -> 25.7 us
    unnamed x47 -> x9, local copies, waits for them, and re-layouts: 18.6 us -> 1.47 us
    pallas_call x2, Pallas kernels: 29.7 us -> 21.2 us  [on_device(): pl.pallas_call(functools.partial(attend_kernel, visible, heads), out_shap...]
    pallas_call x5, Pallas kernels: 14.1 us -> 21.9 us  [call(): pl.pallas_call(kernel, out_shape=outs, in_specs=in_specs, out_specs=out_s...]
    all_to_all x2, waiting for transfers between devices: 16.8 us -> 21.6 us  [on_device(): lax.all_to_all(send, inside, split_axis=0, concat_axis=0, tiled=True)]
  transfers between devices with their start and end apart: 7 -> 7, of which waited for: 4 -> 6; matrix products, arithmetic and copies ran while one was open for 3% -> 3% of each run, Pallas kernels for 16% -> 14%
where the time goes in v3:
time: 176 us; the launch traced here: 175 us
  waiting for transfers between devices  101 us (57%)
  Pallas kernels  43.1 us (24%)
  starting transfers between devices  25.7 us (15%)
  local copies, waits for them, and re-layouts  5.27 us (3%)
    all_to_all x1, waiting for transfers between devices, on_device(): lax.all_to_all(answers.reshape(devices, capacity, width), axes, split_axi...  37.5 us
    all_to_all x1, waiting for transfers between devices, on_device(): lax.all_to_all(outgoing.reshape(devices, capacity, width), axes, split_ax...  33.6 us
    pallas_call x5, Pallas kernels, call(): pl.pallas_call(kernel, out_shape=outs, in_specs=in_specs, out_specs=out_s...  21.9 us
    all_to_all x2, waiting for transfers between devices, on_device(): lax.all_to_all(send, inside, split_axis=0, concat_axis=0, tiled=True)  21.6 us
    pallas_call x2, Pallas kernels, on_device(): pl.pallas_call(functools.partial(attend_kernel, visible, heads), out_shap...  21.2 us
    all_to_all x2, starting transfers between devices, on_device(): lax.all_to_all(send, inside, split_axis=0, concat_axis=0, tiled=True)  7.82 us
    all_to_all x2, waiting for transfers between devices, on_device(): lax.all_to_all(result, inside, split_axis=0, concat_axis=0, tiled=True)  7.81 us
    all_to_all x1, starting transfers between devices, on_device(): lax.all_to_all(outgoing.reshape(devices, capacity, width), axes, split_ax...  7.34 us
  transfers between devices with their start and end apart: 7, of which 6 were waited for; matrix products, arithmetic and copies ran while one was open for 3% of the time, Pallas kernels for 14%

profile of v3, /device:TPU:0, one launch (start us, length us, event | category | flops | bytes accessed | tf_op | source)
XLA Modules:
  0.0 175.5 jit_solution(2470653851841533439)
XLA Ops:
  0.0 0.7 reshape.174.dest_ref
  0.7 4.5 %pack.1 = (bf16[1024,768]{1,0:T(8,128)(2,1)}, s32[1,1280]{1,0:T(1,128)S(1)}) custom-call(s32[1,1280]{1,0:T(1,128)S(1)} %reshape.174.dest_ref, bf16[1280,768]{1,0:T(8,128)(2,1)} %tiles_hbm.1), custom_call_target="tpu_custom_call" | custom-call | tf_op jit(solution)/shard_map/pack/pallas_call | solution.py:371
  5.3 7.3 %all-to-all-start = ((bf16[32,32,768]{2,1,0:T(8,128)(2,1)}), bf16[32,32,768]{2,1,0:T(8,128)(2,1)S(1)}, u32[]{:S(2)}, u32[]{:S(2)}) async-start(bf16[32,32,768]{2,1,0:T(8,128)(2,1)} %bitcast.26), calls=%async_computation | async-start | bytes 3145728 | tf_op jit(solution)/shard_map/all_to_all | solution.py:415
  12.6 0.8 collective-permute-start
  13.4 0.5 slice-done
  13.9 1.5 copy.51
  15.4 0.1 reshape_reshape.3
  15.6 0.3 convert_reduce_fusion
  16.0 0.2 copy.48
  16.1 0.2 div.38
  16.4 0.3 and.42
  16.7 33.6 %all-to-all-done = bf16[32,32,768]{2,1,0:T(8,128)(2,1)S(1)} async-done(((bf16[32,32,768]{2,1,0:T(8,128)(2,1)}), bf16[32,32,768]{2,1,0:T(8,128)(2,1)S(1)}, u32[]{:S(2)}, u32[]{:S(2)}) %all-to-all-start) | async-done | bytes 1572896 | tf_op jit(solution)/shard_map/all_to_all | solution.py:415
  50.3 6.5 %project_first.1 = (bf16[512,768]{1,0:T(8,128)(2,1)}, bf16[512,768]{1,0:T(8,128)(2,1)}, bf16[8,768,128]{2,1,0:T(8,128)(2,1)}) custom-call(s32[512,1]{1,0:T(8,128)S(1)} %fusion.1.slot_ref, bf16[1024,768]{1,0:T(8,128)(2,1)S(1)} %bitcast.20, f32[1,768]{1,0:T(1,128)S(1)} %broadcast_in_dim.4.gain_ref, bf16[768,2304]{1,0:T(8,128)(2,1)} %w_hbm.3, ...), custom_call_target="tpu_custom_call" | custom-call | tf_op jit(solution)/shard_map/project_first/pallas_call | solution.py:371
  56.8 4.3 %all-to-all-start.1 = ((bf16[8,768,128]{2,1,0:T(8,128)(2,1)}), bf16[8,768,128]{2,1,0:T(8,128)(2,1)S(1)}, u32[]{:S(2)}, u32[]{:S(2)}) async-start(bf16[8,768,128]{2,1,0:T(8,128)(2,1)} %get-tuple-element.14), calls=%async_computation.1 | async-start | bytes 3145728 | tf_op jit(solution)/shard_map/all_to_all | solution.py:467
  61.1 3.3 %project_next.1 = bf16[8,640,128]{2,1,0:T(8,128)(2,1)} custom-call(bf16[512,768]{1,0:T(8,128)(2,1)S(1)} %copy-done, bf16[768,2304]{1,0:T(8,128)(2,1)} %w_hbm.3, bf16[768,768]{1,0:T(8,128)(2,1)} %bitcast.24), custom_call_target="tpu_custom_call" | custom-call | tf_op jit(solution)/shard_map/project_next/pallas_call | solution.py:371
  64.3 17.7 %all-to-all-done.1.block_ref = bf16[8,768,128]{2,1,0:T(8,128)(2,1)S(1)} async-done(((bf16[8,768,128]{2,1,0:T(8,128)(2,1)}), bf16[8,768,128]{2,1,0:T(8,128)(2,1)S(1)}, u32[]{:S(2)}, u32[]{:S(2)}) %all-to-all-start.1) | async-done | bytes 1572896 | tf_op jit(solution)/shard_map/all_to_all | solution.py:467
  82.0 3.6 %all-to-all-start.3 = ((bf16[8,640,128]{2,1,0:T(8,128)(2,1)}), bf16[8,640,128]{2,1,0:T(8,128)(2,1)S(1)}, u32[]{:S(2)}, u32[]{:S(2)}) async-start(bf16[8,640,128]{2,1,0:T(8,128)(2,1)} %project_next.1), calls=%async_computation.3 | async-start | bytes 2621440 | tf_op jit(solution)/shard_map/all_to_all | solution.py:467
  85.6 0.7 constant_dynamic-slice_fusion.1
  86.3 13.6 %attend.2 = bf16[8,256,128]{2,1,0:T(8,128)(2,1)} custom-call(s32[8]{0:T(128)S(1)} %get-tuple-element.22.place_ref, s32[8]{0:T(128)S(1)} %get-tuple-element.21.class_ref, bf16[8,768,128]{2,1,0:T(8,128)(2,1)S(1)} %all-to-all-done.1.block_ref), custom_call_target="tpu_custom_call" | custom-call | tf_op jit(solution)/shard_map/attend/pallas_call | solution.py:475
  99.9 3.9 %all-to-all-done.3.block_ref = bf16[8,640,128]{2,1,0:T(8,128)(2,1)S(1)} async-done(((bf16[8,640,128]{2,1,0:T(8,128)(2,1)}), bf16[8,640,128]{2,1,0:T(8,128)(2,1)S(1)}, u32[]{:S(2)}, u32[]{:S(2)}) %all-to-all-start.3) | async-done | bytes 1310752 | tf_op jit(solution)/shard_map/all_to_all | solution.py:467
  103.7 3.5 %all-to-all-start.2 = ((bf16[8,256,128]{2,1,0:T(8,128)(2,1)}), bf16[8,256,128]{2,1,0:T(8,128)(2,1)S(1)}, u32[]{:S(2)}, u32[]{:S(2)}) async-start(bf16[8,256,128]{2,1,0:T(8,128)(2,1)} %attend.2), calls=%async_computation.2 | async-start | bytes 1048576 | tf_op jit(solution)/shard_map/all_to_all | solution.py:491
  107.2 0.7 constant_dynamic-slice_fusion
  107.9 7.6 %attend.3 = bf16[8,128,128]{2,1,0:T(8,128)(2,1)} custom-call(s32[4]{0:T(128)S(1)} %get-tuple-element.20.place_ref, s32[4]{0:T(128)S(1)} %get-tuple-element.19.class_ref, bf16[8,640,128]{2,1,0:T(8,128)(2,1)S(1)} %all-to-all-done.3.block_ref), custom_call_target="tpu_custom_call" | custom-call | tf_op jit(solution)/shard_map/attend/pallas_call | solution.py:475
  115.5 1.3 all-to-all-done.2.refs_0_
  116.9 3.6 %all-to-all-start.4 = ((bf16[8,128,128]{2,1,0:T(8,128)(2,1)}), bf16[8,128,128]{2,1,0:T(8,128)(2,1)S(1)}, u32[]{:S(2)}, u32[]{:S(2)}) async-start(bf16[8,128,128]{2,1,0:T(8,128)(2,1)} %attend.3), calls=%async_computation.4 | async-start | bytes 524288 | tf_op jit(solution)/shard_map/all_to_all | solution.py:491
  120.6 0.1 and.38
  120.7 6.5 %all-to-all-done.4.refs_1_ = bf16[8,128,128]{2,1,0:T(8,128)(2,1)S(1)} async-done(((bf16[8,128,128]{2,1,0:T(8,128)(2,1)}), bf16[8,128,128]{2,1,0:T(8,128)(2,1)S(1)}, u32[]{:S(2)}, u32[]{:S(2)}) %all-to-all-start.4) | async-done | bytes 262176 | tf_op jit(solution)/shard_map/all_to_all | solution.py:491
  127.2 4.6 %finish.1 = bf16[1024,768]{1,0:T(8,128)(2,1)} custom-call(s32[1,512]{1,0:T(1,128)S(1)} %fusion.4.slot_ref, bf16[8,256,128]{2,1,0:T(8,128)(2,1)S(1)} %all-to-all-done.2.refs_0_, bf16[8,128,128]{2,1,0:T(8,128)(2,1)S(1)} %all-to-all-done.4.refs_1_, bf16[512,768]{1,0:T(8,128)(2,1)} %get-tuple-element.18.refs_2_, f32[1,768]{1,0:T(1,128)S(1)} %broadcast_in_dim.5.refs_3_, ...), custom_call_target="tpu_custom_call" | custom-call | tf_op jit(solution)/shard_map/finish/pallas_call | solution.py:371
  131.8 2.7 %all-to-all-start.5 = ((bf16[32,32,768]{2,1,0:T(8,128)(2,1)}), bf16[32,32,768]{2,1,0:T(8,128)(2,1)S(1)}, u32[]{:S(2)}, u32[]{:S(2)}) async-start(bf16[32,32,768]{2,1,0:T(8,128)(2,1)} %bitcast.25), calls=%async_computation.5 | async-start | bytes 3145728 | tf_op jit(solution)/shard_map/all_to_all | solution.py:513
  134.5 0.3 copy.50.slot_ref
  134.8 37.5 %all-to-all-done.5 = bf16[32,32,768]{2,1,0:T(8,128)(2,1)S(1)} async-done(((bf16[32,32,768]{2,1,0:T(8,128)(2,1)}), bf16[32,32,768]{2,1,0:T(8,128)(2,1)S(1)}, u32[]{:S(2)}, u32[]{:S(2)}) %all-to-all-start.5) | async-done | bytes 1572896 | tf_op jit(solution)/shard_map/all_to_all | solution.py:513
  172.3 3.0 %unpack.1 = bf16[1280,768]{1,0:T(8,128)(2,1)} custom-call(s32[1280,1]{1,0:T(8,128)S(1)} %copy.50.slot_ref, bf16[1024,768]{1,0:T(8,128)(2,1)S(1)} %bitcast.21), custom_call_target="tpu_custom_call" | custom-call | tf_op jit(solution)/shard_map/unpack/pallas_call | solution.py:371
  (22 shorter events, 0.4 us)
Async XLA Ops:
  5.3 7.4 %copy-start.3 = (s32[1,512]{1,0:T(1,128)S(1)}, s32[1,512]{1,0:T(1,128)}, u32[]{:S(2)}) copy-start(s32[1,512]{1,0:T(1,128)} %param.11) | copy-start | bytes 6148
  5.3 45.1 %all-to-all-start = ((bf16[32,32,768]{2,1,0:T(8,128)(2,1)}), bf16[32,32,768]{2,1,0:T(8,128)(2,1)S(1)}, u32[]{:S(2)}, u32[]{:S(2)}) async-start(bf16[32,32,768]{2,1,0:T(8,128)(2,1)} %bitcast.26), calls=%async_computation | async-start | bytes 3145728 | tf_op jit(solution)/shard_map/all_to_all | solution.py:415
  12.6 1.3 slice-start
  12.6 2.7 %collective-permute-start = (s32[4,128]{1,0:T(4,128)S(1)}, s32[4,128]{1,0:T(4,128)S(1)}, u32[]{:S(2)}, u32[]{:S(2)}) collective-permute-start(s32[4,128]{1,0:T(4,128)S(1)} %bitcast.30), channel_id=1, source_target_pairs={{0,0},{4,1},{8,2},{12,3},{16,4},{20,5},{24,6},{28,7},{1,8},{5,9},{... | collective-permute-start | bytes 6152 | tf_op jit(solution)/shard_map/ppermute | solution.py:397
  13.9 1.5 copy-start.1
  56.8 4.3 %copy-start = (bf16[512,768]{1,0:T(8,128)(2,1)S(1)}, bf16[512,768]{1,0:T(8,128)(2,1)}, u32[]{:S(2)}) copy-start(bf16[512,768]{1,0:T(8,128)(2,1)} %get-tuple-element.15.normed_ref) | copy-start | bytes 2359300
  56.8 25.2 %all-to-all-start.1 = ((bf16[8,768,128]{2,1,0:T(8,128)(2,1)}), bf16[8,768,128]{2,1,0:T(8,128)(2,1)S(1)}, u32[]{:S(2)}, u32[]{:S(2)}) async-start(bf16[8,768,128]{2,1,0:T(8,128)(2,1)} %get-tuple-element.14), calls=%async_computation.1 | async-start | bytes 3145728 | tf_op jit(solution)/shard_map/all_to_all | solution.py:467
  82.0 21.7 %all-to-all-start.3 = ((bf16[8,640,128]{2,1,0:T(8,128)(2,1)}), bf16[8,640,128]{2,1,0:T(8,128)(2,1)S(1)}, u32[]{:S(2)}, u32[]{:S(2)}) async-start(bf16[8,640,128]{2,1,0:T(8,128)(2,1)} %project_next.1), calls=%async_computation.3 | async-start | bytes 2621440 | tf_op jit(solution)/shard_map/all_to_all | solution.py:467
  99.9 20.6 %copy-start.2 = (f32[768]{0:T(1024)S(1)}, f32[768]{0:T(1024)}, u32[]{:S(2)}) copy-start(f32[768]{0:T(1024)} %param.15) | copy-start | bytes 9220
  103.7 13.2 %all-to-all-start.2 = ((bf16[8,256,128]{2,1,0:T(8,128)(2,1)}), bf16[8,256,128]{2,1,0:T(8,128)(2,1)S(1)}, u32[]{:S(2)}, u32[]{:S(2)}) async-start(bf16[8,256,128]{2,1,0:T(8,128)(2,1)} %attend.2), calls=%async_computation.2 | async-start | bytes 1048576 | tf_op jit(solution)/shard_map/all_to_all | solution.py:491
  116.9 10.3 %all-to-all-start.4 = ((bf16[8,128,128]{2,1,0:T(8,128)(2,1)}), bf16[8,128,128]{2,1,0:T(8,128)(2,1)S(1)}, u32[]{:S(2)}, u32[]{:S(2)}) async-start(bf16[8,128,128]{2,1,0:T(8,128)(2,1)} %attend.3), calls=%async_computation.4 | async-start | bytes 524288 | tf_op jit(solution)/shard_map/all_to_all | solution.py:491
  131.8 40.5 %all-to-all-start.5 = ((bf16[32,32,768]{2,1,0:T(8,128)(2,1)}), bf16[32,32,768]{2,1,0:T(8,128)(2,1)S(1)}, u32[]{:S(2)}, u32[]{:S(2)}) async-start(bf16[32,32,768]{2,1,0:T(8,128)(2,1)} %bitcast.25), calls=%async_computation.5 | async-start | bytes 3145728 | tf_op jit(solution)/shard_map/all_to_all | solution.py:513

commit v4 on v3

--- a/solution.py
+++ b/solution.py
@@ -33,27 +33,34 @@
     return jnp.dot(left, right, preferred_element_type=jnp.float32)
 
 
-def parts_of(members):
+def parts_of(members, segments):
     full = HEADS // members
-    every = [(0, cls) for cls in range(CLASSES)]
+    every = [(0, segment) for segment in range(segments)]
     parts = [
         (i * members, (i + 1) * members, [([i * members + member], every) for member in range(members)])
         for i in range(full)
     ]
     first = full * members
-    owned = (HEADS - first) * CLASSES // members
+    owned = (HEADS - first) * segments // members
     if owned:
         dealt = []
         for member in range(members):
-            units = [divmod(first * CLASSES + member * owned + i, CLASSES) for i in range(owned)]
+            units = [divmod(first * segments + member * owned + i, segments) for i in range(owned)]
             dealt.append((sorted({head for head, _ in units}), units))
         width = max(len(heads) for heads, _ in dealt)
         part = []
         for heads, units in dealt:
-            units = [(heads.index(head), cls) for head, cls in units]
-            part.append((heads + heads[-1:] * (width - len(heads)), units + units[-1:] * (owned % 2)))
+            units = [(heads.index(head), segment) for head, segment in units]
+            part.append((heads + heads[-1:] * (width - len(heads)), units))
         parts.append((first, HEADS, part))
     return parts
+
+
+def place_pair(left, left_odd, right, right_odd):
+    left = swap(left) if left_odd else left
+    right = right if right_odd else swap(right)
+    lanes = lax.broadcasted_iota(jnp.int32, left.shape, 1)
+    return jnp.where(lanes < HDIM, left, right)
 
 
 def swap(tile):
@@ -110,21 +117,19 @@
     return jnp.where(row < column, 1.0, 0.0).astype(jnp.bfloat16)
 
 
-def project_part(part, normed, w_ref, wvt_ref, send_hbm, send_ref, q_ref, k_ref, vt_ref, sems):
+def project_part(part, segment, normed, extra, w_ref, wvt_ref, send_hbm, send_ref, q_ref, k_ref, vt_ref, sems):
     first, last, members = part
     visible, width = normed.shape
     rows, middle = visible // CLASSES, visible // 2
-    low, high = 0, (last - first) * HDIM
+    wide = 2 * HDIM
     q_ref[...] = (dot(normed, w_ref[0]) * HDIM ** (-0.5)).astype(jnp.bfloat16)
     k_ref[...] = dot(normed, w_ref[1]).astype(jnp.bfloat16)
     vt_ref[...] = dot_nt(wvt_ref[...], normed).astype(jnp.bfloat16)
-    wide = 2 * HDIM
-
-    def place_pair(left, left_odd, right, right_odd):
-        left = swap(left) if left_odd else left
-        right = right if right_odd else swap(right)
-        lanes = lax.broadcasted_iota(jnp.int32, left.shape, 1)
-        return jnp.where(lanes < HDIM, left, right)
+
+    def queries_of(head, cls):
+        at = (head - first) // 2 * wide
+        pair = [q_ref[(cls + i) * rows : (cls + i + 1) * rows, at : at + wide] for i in range(2)]
+        return place_pair(pair[0], head % 2, pair[1], head % 2)
 
     for head in range(first, last):
         at, odd = (head - first) // 2 * wide, head % 2
@@ -139,13 +144,18 @@
                     send_ref[member, top : top + HDIM, :] = values[:, i * wide : (i + 1) * wide]
     copies = []
     for member, (heads, units) in enumerate(members):
-        for i in range(0, len(units), 2):
-            tiles = []
-            for place, cls in units[i : i + 2]:
-                at = (heads[place] - first) // 2 * wide
-                tiles += [q_ref[cls * rows : (cls + 1) * rows, at : at + wide], heads[place] % 2]
-            top = len(heads) * visible + i // 2 * rows
-            send_ref[member, top : top + rows, :] = place_pair(*tiles)
+        base = len(heads) * visible
+        for i in range(CLASSES // 2):
+            tile = queries_of(heads[0], 2 * i)
+            for place, head in enumerate(heads[1:], 1):
+                mine = functools.reduce(
+                    jnp.logical_or, [segment[0] == one for at, one in units if at == place], False
+                )
+                if head != heads[0]:
+                    tile = jnp.where(mine, queries_of(head, 2 * i), tile)
+            send_ref[member, base + i * rows : base + (i + 1) * rows, :] = tile
+        if extra is not None:
+            send_ref[member, base + middle :, :] = extra
         copies.append(write(send_ref, send_hbm, member, 1, sems))
     return copies
 
@@ -163,50 +173,51 @@
     return copies
 
 
-def first_kernel(part, slot_ref, arrived_ref, gain_ref, w_hbm, wvt_hbm, rows_hbm, normed_hbm, send_hbm,
-                 w_ref, wvt_ref, send_ref, q_ref, k_ref, vt_ref, sems, rows_ref, normed_ref, more):
+def first_kernel(part, segment, slot_ref, extra_ref, arrived_ref, gain_ref, w_hbm, wvt_hbm, normed_hbm, send_hbm,
+                 w_ref, wvt_ref, send_ref, q_ref, k_ref, vt_ref, sems, normed_ref, more):
     weights = fetch_weights(part, w_hbm, wvt_hbm, w_ref, wvt_ref, more)
-    visible, slots = rows_ref.shape[0], arrived_ref.shape[0]
+    visible, slots = normed_ref.shape[0], arrived_ref.shape[0]
     chosen = one_hot(lax.broadcasted_iota(jnp.int32, (visible, slots), 1), slot_ref[...])
     rows = dot(chosen, arrived_ref[...])
-    rows_ref[...] = rows.astype(jnp.bfloat16)
     normed = layer_norm(rows, gain_ref[...]).astype(jnp.bfloat16)
     normed_ref[...] = normed
-    copies = [
-        pltpu.make_async_copy(rows_ref, rows_hbm, more.at[3]),
-        pltpu.make_async_copy(normed_ref, normed_hbm, more.at[4]),
-    ]
+    copies = [pltpu.make_async_copy(normed_ref, normed_hbm, more.at[3])]
     for copy in copies:
         copy.start()
     for copy in weights:
         copy.wait()
-    copies += project_part(part, normed, w_ref, wvt_ref, send_hbm, send_ref, q_ref, k_ref, vt_ref, sems)
+    copies += project_part(
+        part, segment, normed, extra_ref[...], w_ref, wvt_ref, send_hbm, send_ref, q_ref, k_ref, vt_ref, sems
+    )
     for copy in copies:
         copy.wait()
 
 
-def next_kernel(part, normed_ref, w_hbm, wvt_hbm, send_hbm, w_ref, wvt_ref, send_ref, q_ref, k_ref, vt_ref, sems, more):
+def next_kernel(part, segment, normed_ref, w_hbm, wvt_hbm, send_hbm, w_ref, wvt_ref, send_ref, q_ref, k_ref, vt_ref, sems, more):
     for copy in fetch_weights(part, w_hbm, wvt_hbm, w_ref, wvt_ref, more):
         copy.wait()
-    for copy in project_part(part, normed_ref[...], w_ref, wvt_ref, send_hbm, send_ref, q_ref, k_ref, vt_ref, sems):
+    copies = project_part(
+        part, segment, normed_ref[...], None, w_ref, wvt_ref, send_hbm, send_ref, q_ref, k_ref, vt_ref, sems
+    )
+    for copy in copies:
         copy.wait()
 
 
-def attend_kernel(visible, heads, place_ref, class_ref, block_ref, out_ref, score_ref, peak_ref):
+def attend_kernel(visible, heads, place_ref, segment_ref, block_ref, out_ref, score_ref, peak_ref):
     members = block_ref.shape[0]
     rows, middle = visible // CLASSES, visible // 2
     group = SEG // visible
     segments = members // group
     wide = 2 * HDIM
     size = group * rows
-    turns = out_ref.shape[1] // rows * segments
+    pairs = CLASSES // 2
+    turns = out_ref.shape[0] // group * pairs
     low = lax.broadcasted_iota(jnp.int32, (size, wide), 1) < HDIM
 
     def tile_of(turn, half):
-        step, segment = turn // segments, turn % segments
-        cls = class_ref[2 * step + half]
-        base = pl.multiple_of(place_ref[2 * step + half] * visible, visible)
-        return step, segment, cls, base
+        unit, step = turn // pairs, turn % pairs
+        base = pl.multiple_of(place_ref[unit] * visible, visible)
+        return step, segment_ref[unit], 2 * step + half, base
 
     def member_of(segment, i, apart):
         return lax.rem(segment + apart, segments) * group + i
@@ -286,69 +297,111 @@
         run(weight_steps(turn, 0, results), score_steps(turn, 1))
         after = jnp.minimum(turn + 1, turns - 1)
         run(weight_steps(turn, 1, results), score_steps(after, 0))
-        both = jnp.concatenate(results, axis=0).T.astype(jnp.bfloat16)
-        step, segment = turn // segments, turn % segments
-        for i in range(group):
-            at = pl.multiple_of(step * rows, rows)
-            out_ref[segment * group + i, pl.ds(at, rows), :] = both[i * rows : (i + 1) * rows, :]
+        unit, step = turn // pairs, turn % pairs
+        for half, result in enumerate(results):
+            twice = jnp.concatenate([result, result], axis=0).T.astype(jnp.bfloat16)
+            at = pl.multiple_of((2 * step + half) * rows, rows)
+            for i in range(group):
+                out_ref[unit * group + i, pl.ds(at, rows), :] = twice[i * rows : (i + 1) * rows, :]
         return carry
 
     run(score_steps(0, 0))
     lax.fori_loop(0, turns, body, 0)
 
 
-def finish_kernel(parts, slot_ref, *refs):
-    mixed_refs = refs[: len(parts)]
-    rows_hbm, gain_ref, w_hbm, out_hbm, attended_ref, rows_ref, w_ref, out_ref, more, sems = refs[len(parts) :]
+def spread_kernel(heads, capacity, segment_ref, block_ref, *refs):
+    mixed_refs, (out_hbm, out_ref, sem) = refs[:-3], refs[-3:]
+    visible = mixed_refs[0].shape[1]
+    members = block_ref.shape[0]
+    devices = out_ref.shape[0]
+    group = SEG // visible
+    slots = devices * capacity
+    lines = visible // 128
+    top = heads * visible + visible // 2
+    units = [(ref, i) for ref in mixed_refs for i in range(ref.shape[0] // group)]
+    step = math.gcd(slots, 256)
+    low = lax.broadcasted_iota(jnp.int32, (step, 2 * HDIM), 1) < HDIM
+    slot_of = {}
+
+    def slot_row(u, i):
+        if (u, i) not in slot_of:
+            info = block_ref[segment_ref[u] * group + i, top : top + 16, :].astype(jnp.float32)
+            place = (info[:lines] * capacity + info[lines : 2 * lines]).astype(jnp.int32)
+            slot_of[u, i] = jnp.concatenate([place[j : j + 1] for j in range(lines)], axis=1)
+        return slot_of[u, i]
+
+    def spread(u, i, start):
+        wanted = lax.broadcasted_iota(jnp.int32, (step, visible), 0) + start
+        ref, unit = units[u]
+        return dot(one_hot(wanted, slot_row(u, i)), ref[unit * group + i])
+
+    for start in range(0, slots, step):
+        owners = slice(start // capacity, (start + step) // capacity)
+        for u in range(0, len(units), 2):
+            base = u // 2 * group * capacity
+            if u + 1 < len(units):
+                pairs = [((u, i), (u + 1, i)) for i in range(group)]
+            else:
+                pairs = [((u, i), (u, i + group // 2)) for i in range(group // 2)]
+            for i, (left, right) in enumerate(pairs):
+                both = jnp.where(low, spread(*left, start), spread(*right, start)).astype(jnp.bfloat16)
+                both = both.reshape(step // capacity, capacity, 2 * HDIM)
+                out_ref[owners, base + i * capacity : base + (i + 1) * capacity, :] = both
+    copy = pltpu.make_async_copy(out_ref, out_hbm, sem)
+    copy.start()
+    copy.wait()
+
+
+def finish_kernel(parts, capacity, slot_ref, back_ref, rows_hbm, gain_ref, w_hbm, out_hbm,
+                  attended_ref, rows_ref, w_ref, answer_ref, out_ref, more, sems):
     fetches = [
         pltpu.make_async_copy(w_hbm, w_ref, more.at[0]),
         pltpu.make_async_copy(rows_hbm, rows_ref, more.at[1]),
     ]
     for copy in fetches:
         copy.start()
-    visible, _ = rows_ref.shape
-    part = visible // CLASSES
-    slots = out_ref.shape[0]
+    slots, count = attended_ref.shape[0], out_ref.shape[0]
+    members = len(parts[0][2])
+    groups = back_ref.shape[0] // members
+    segments = 1 + max(segment for _, _, part in parts for _, units in part for _, segment in units)
+    group = members // segments
+    total = sum(len(part[0][1]) for _, _, part in parts)
     where = {}
-    for mixed_ref, (_, _, members) in zip(mixed_refs, parts):
-        for member, (heads, units) in enumerate(members):
-            for i, (place, cls) in enumerate(units):
-                where.setdefault((heads[place], cls), (mixed_ref, member, i))
-    for head in range(0, HEADS, 2):
-        for cls in range(CLASSES):
-            pair = []
-            for one in (head, head + 1):
-                mixed_ref, member, i = where[(one, cls)]
-                tile = mixed_ref[member, i // 2 * part : (i // 2 + 1) * part, :]
-                pair.append(tile[:, i % 2 * HDIM : (i % 2 + 1) * HDIM])
-            attended_ref[cls * part : (cls + 1) * part, head * HDIM : (head + 2) * HDIM] = (
-                jnp.concatenate(pair, axis=1)
-            )
+    for member in range(members):
+        u = 0
+        for _, _, part in parts:
+            heads, units = part[member]
+            for place, segment in units:
+                where[heads[place], segment] = member, u
+                u += 1
+
+    def piece(which, head, source):
+        member, u = where[head, source // group]
+        i, odd = source % group, u % 2
+        if u + 1 == total and total % 2:
+            i, odd = i % (group // 2), i // (group // 2)
+        at = u // 2 * group * capacity + i * capacity
+        return back_ref[which * members + member, at : at + capacity, :], odd
+
+    for which in range(groups):
+        for source in range(members):
+            at = (which * members + source) * capacity
+            for head in range(0, HEADS, 2):
+                pair = piece(which, head, source) + piece(which, head + 1, source)
+                attended_ref[at : at + capacity, head * HDIM : (head + 2) * HDIM] = place_pair(*pair)
     for copy in fetches:
         copy.wait()
-    hidden = rows_ref[...].astype(jnp.float32) + dot(attended_ref[...], w_ref[...])
-    answer = layer_norm(hidden, gain_ref[...]).astype(jnp.bfloat16)
     step = math.gcd(slots, 256)
-    copies = []
     for start in range(0, slots, step):
-        wanted = lax.broadcasted_iota(jnp.int32, (step, visible), 0) + start
-        out_ref[start : start + step, :] = dot(one_hot(wanted, slot_ref[...]), answer).astype(
-            jnp.bfloat16
-        )
-        copies.append(write(out_ref, out_hbm, start, step, sems))
-    for copy in copies:
-        copy.wait()
-
-
-def unpack_kernel(slot_ref, back_ref, out_hbm, out_ref, sems):
-    count = out_ref.shape[0]
-    slots = back_ref.shape[0]
+        at = slice(start, start + step)
+        hidden = rows_ref[at, :].astype(jnp.float32) + dot(attended_ref[at, :], w_ref[...])
+        answer_ref[at, :] = layer_norm(hidden, gain_ref[...]).astype(jnp.bfloat16)
     step = math.gcd(count, 256)
     copies = []
     for start in range(0, count, step):
         here = lax.broadcasted_iota(jnp.int32, (step, slots), 1)
         chosen = one_hot(slot_ref[start : start + step, :], here)
-        out_ref[start : start + step, :] = dot(chosen, back_ref[...]).astype(jnp.bfloat16)
+        out_ref[start : start + step, :] = dot(chosen, answer_ref[...]).astype(jnp.bfloat16)
         copies.append(write(out_ref, out_hbm, start, step, sems))
     for copy in copies:
         copy.wait()
@@ -356,6 +409,7 @@
 
 IN_VMEM = pl.BlockSpec(memory_space=pltpu.VMEM)
 IN_HBM = pl.BlockSpec(memory_space=pltpu.HBM)
+IN_SMEM = pl.BlockSpec(memory_space=pltpu.SMEM)
 COPIES = pltpu.SemaphoreType.DMA
 
 
@@ -390,7 +444,9 @@
     capacity = 2 * visible // devices
     slots = devices * capacity
     rows = visible // CLASSES
-    parts = parts_of(members)
+    segments = members * visible // SEG
+    group = members // segments
+    parts = parts_of(members, segments)
     bf16 = jnp.bfloat16
 
     moves = [(s * groups + g, g * members + s) for g in range(groups) for s in range(members)]
@@ -421,13 +477,26 @@
     earlier = owners[None, :] < owners[:, None]
     placed = jnp.sum((same & earlier).astype(jnp.int32), axis=1)
     slot = source * capacity + placed
+    lines = visible // 128
+    extra = jnp.concatenate([source.reshape(lines, 128), placed.reshape(lines, 128)])
+    extra = jnp.pad(extra, ((0, 16 - 2 * lines), (0, 0))).astype(bf16)
+    member = lax.axis_index(inside)
+    tables = [
+        jnp.array([list(zip(*units)) for _, units in part], jnp.int32)[member] for _, _, part in parts
+    ]
+    places = [table[0] for table in tables]
+    sought = [table[1] for table in tables]
+    every = jnp.concatenate(sought)
+    slot, extra, places, sought, every = lax.optimization_barrier((slot, extra, places, sought, every))
 
     weights = (w_qkv, w_qkv[:, 2 * width :].T)
+    mine = [member // group]
     blocks = []
     for i, part in enumerate(parts):
         first, last, dealt = part
-        heads, units = len(dealt[0][0]), len(dealt[0][1])
-        shape = jax.ShapeDtypeStruct((members, heads * visible + units // 2 * rows, 2 * HDIM), bf16)
+        heads = len(dealt[0][0])
+        depth = heads * visible + visible // 2 + (16 if i == 0 else 0)
+        shape = jax.ShapeDtypeStruct((members, depth, 2 * HDIM), bf16)
         size = (last - first) * HDIM
         scratch = [
             pltpu.VMEM((2, width, size), bf16),
@@ -438,18 +507,21 @@
             pltpu.VMEM((size, visible), bf16),
             COPIES((members,)),
         ]
+        segment = jnp.array(mine, jnp.int32)
         if i == 0:
-            student, normed, send = call(
+            normed, send = call(
                 functools.partial(first_kernel, part),
-                (jax.ShapeDtypeStruct((visible, width), bf16),) * 2 + (shape,),
-                (IN_HBM,) * 3,
+                (jax.ShapeDtypeStruct((visible, width), bf16), shape),
+                (IN_HBM,) * 2,
                 "project_first",
+                segment,
                 slot[:, None],
+                extra,
                 arrived,
                 gain_attn[None, :],
                 *weights,
-                in_specs=[IN_VMEM] * 3 + [IN_HBM] * 2,
-                scratch=scratch + [pltpu.VMEM((visible, width), bf16)] * 2 + [COPIES((5,))],
+                in_specs=[IN_SMEM] + [IN_VMEM] * 4 + [IN_HBM] * 2,
+                scratch=scratch + [pltpu.VMEM((visible, width), bf16), COPIES((4,))],
             )
         else:
             send = call(
@@ -457,9 +529,10 @@
                 shape,
                 IN_HBM,
                 "project_next",
+                segment,
                 normed,
                 *weights,
-                in_specs=[IN_VMEM] + [IN_HBM] * 2,
+                in_specs=[IN_SMEM, IN_VMEM] + [IN_HBM] * 2,
                 scratch=scratch + [COPIES((3,))],
             )
         if blocks:
@@ -467,61 +540,59 @@
         blocks.append(lax.all_to_all(send, inside, split_axis=0, concat_axis=0, tiled=True))
 
     mixed = []
-    for (_, _, part), block in zip(parts, blocks):
+    for (_, _, part), block, place, segment in zip(parts, blocks, places, sought):
         heads, units = len(part[0][0]), len(part[0][1])
-        table = jnp.array([list(zip(*units)) for _, units in part], jnp.int32)[lax.axis_index(inside)]
-        depth = SEG + (members * visible // SEG - 1) * SEG // CLASSES
-        across = SEG // CLASSES
-        result = pl.pallas_call(
+        depth = SEG + (segments - 1) * SEG // CLASSES
+        result = call(
             functools.partial(attend_kernel, visible, heads),
-            out_shape=jax.ShapeDtypeStruct((members, units // 2 * rows, 2 * HDIM), bf16),
-            grid_spec=pltpu.PrefetchScalarGridSpec(
-                num_scalar_prefetch=2,
-                grid=(1,),
-                in_specs=[IN_VMEM],
-                out_specs=pl.BlockSpec((members, units // 2 * rows, 2 * HDIM), lambda i, *_: (0, 0, 0)),
-                scratch_shapes=[
-                    pltpu.VMEM((2, depth, across), jnp.float32),
-                    pltpu.VMEM((2, 8, across), jnp.float32),
-                ],
-            ),
-            compiler_params=pltpu.CompilerParams(vmem_limit_bytes=VMEM),
-            name="attend",
-        )(table[0], table[1], block)
-        mixed.append(lax.all_to_all(result, inside, split_axis=0, concat_axis=0, tiled=True))
-
+            jax.ShapeDtypeStruct((units * group, visible, 2 * HDIM), bf16),
+            IN_VMEM,
+            "attend",
+            place,
+            segment,
+            block,
+            in_specs=[IN_SMEM, IN_SMEM, IN_VMEM],
+            scratch=[
+                pltpu.VMEM((2, depth, SEG // CLASSES), jnp.float32),
+                pltpu.VMEM((2, 8, SEG // CLASSES), jnp.float32),
+            ],
+        )
+        mixed.append(result)
+
+    heads = len(parts[0][2][0][0])
+    shape = jax.ShapeDtypeStruct((devices, every.shape[0] * group * capacity // 2, 2 * HDIM), bf16)
     answers = call(
-        functools.partial(finish_kernel, parts),
-        jax.ShapeDtypeStruct((slots, width), bf16),
+        functools.partial(spread_kernel, heads, capacity),
+        shape,
+        IN_HBM,
+        "spread",
+        every,
+        blocks[0],
+        *mixed,
+        in_specs=[IN_SMEM] + [IN_VMEM] * (1 + len(mixed)),
+        scratch=[pltpu.VMEM(shape.shape, bf16), COPIES],
+    )
+    back = lax.all_to_all(answers, axes, split_axis=0, concat_axis=0, tiled=True)
+    return call(
+        functools.partial(finish_kernel, parts, capacity),
+        jax.ShapeDtypeStruct((count, width), bf16),
         IN_HBM,
         "finish",
-        slot[None, :],
-        *mixed,
-        student,
+        send_slot.reshape(count, 1),
+        back,
+        outgoing,
         gain_out[None, :],
         w_out,
-        in_specs=[IN_VMEM] * (1 + len(parts)) + [IN_HBM, IN_VMEM, IN_HBM],
+        in_specs=[IN_VMEM, IN_VMEM, IN_HBM, IN_VMEM, IN_HBM],
         scratch=[
-            pltpu.VMEM((visible, width), bf16),
-            pltpu.VMEM((visible, width), bf16),
+            pltpu.VMEM((slots, width), bf16),
+            pltpu.VMEM((slots, width), bf16),
             pltpu.VMEM((width, width), bf16),
             pltpu.VMEM((slots, width), bf16),
+            pltpu.VMEM((count, width), bf16),
             COPIES((2,)),
-            COPIES((slots // math.gcd(slots, 256),)),
+            COPIES((count // math.gcd(count, 256),)),
         ],
-    )
-    back = lax.all_to_all(
-        answers.reshape(devices, capacity, width), axes, split_axis=0, concat_axis=0, tiled=True
-    ).reshape(slots, width)
-    shape = jax.ShapeDtypeStruct((count, width), bf16)
-    return call(
-        unpack_kernel,
-        shape,
-        IN_HBM,
-        "unpack",
-        send_slot.reshape(count, 1),
-        back,
-        scratch=[pltpu.VMEM((count, width), bf16), COPIES((count // math.gcd(count, 256),))],
     )
 
 

time: 176 us -> 167 us (0.949)
  starting transfers between devices: 25.7 us -> 18.5 us
  waiting for transfers between devices: 101 us -> 94 us
  Pallas kernels: 43.1 us -> 46.4 us
    pallas_call x5 -> x7, Pallas kernels: 21.9 us -> 46.4 us  [call(): pl.pallas_call(kernel, out_shape=outs, in_specs=in_specs, out_specs=out_s...]
    pallas_call x2 -> x0, Pallas kernels: 21.2 us -> none  [on_device(): pl.pallas_call(functools.partial(attend_kernel, visible, heads), out_shap...]
    all_to_all x3 -> x1, waiting for transfers between devices: 45.3 us -> 37.5 us  [on_device(): lax.all_to_all(answers, axes, split_axis=0, concat_axis=0, tiled=True)]
    all_to_all x3 -> x1, starting transfers between devices: 9.79 us -> 2.7 us  [on_device(): lax.all_to_all(answers, axes, split_axis=0, concat_axis=0, tiled=True)]
    all_to_all x2, waiting for transfers between devices: 21.6 us -> 24.8 us  [on_device(): lax.all_to_all(send, inside, split_axis=0, concat_axis=0, tiled=True)]
    all_to_all x1, waiting for transfers between devices: 33.6 us -> 31.8 us  [on_device(): lax.all_to_all(outgoing.reshape(devices, capacity, width), axes, split_ax...]
  transfers between devices with their start and end apart: 7 -> 5, of which waited for: 6 -> 4; matrix products, arithmetic and copies ran while one was open for 3% -> 3% of each run, Pallas kernels for 14% -> 10%
where the time goes in v4:
time: 167 us; the launch traced here: 166 us
  waiting for transfers between devices  94 us (56%)
  Pallas kernels  46.4 us (28%)
  starting transfers between devices  18.5 us (11%)
  local copies, waits for them, and re-layouts  5.88 us (4%)
    pallas_call x7, Pallas kernels, call(): pl.pallas_call(kernel, out_shape=outs, in_specs=in_specs, out_specs=out_s...  46.4 us
    all_to_all x1, waiting for transfers between devices, on_device(): lax.all_to_all(answers, axes, split_axis=0, concat_axis=0, tiled=True)  37.5 us
    all_to_all x1, waiting for transfers between devices, on_device(): lax.all_to_all(outgoing.reshape(devices, capacity, width), axes, split_ax...  31.8 us
    all_to_all x2, waiting for transfers between devices, on_device(): lax.all_to_all(send, inside, split_axis=0, concat_axis=0, tiled=True)  24.8 us
    all_to_all x2, starting transfers between devices, on_device(): lax.all_to_all(send, inside, split_axis=0, concat_axis=0, tiled=True)  7.66 us
    all_to_all x1, starting transfers between devices, on_device(): lax.all_to_all(outgoing.reshape(devices, capacity, width), axes, split_ax...  7.34 us
  transfers between devices with their start and end apart: 5, of which 4 were waited for; matrix products, arithmetic and copies ran while one was open for 3% of the time, Pallas kernels for 10%

profile of v4, /device:TPU:0, one launch (start us, length us, event | category | flops | bytes accessed | tf_op | source)
XLA Modules:
  0.0 166.4 jit_solution(13458810891569534162)
XLA Ops:
  0.0 0.7 reshape.80.dest_ref
  0.7 4.5 %pack.1 = (bf16[1024,768]{1,0:T(8,128)(2,1)}, s32[1,1280]{1,0:T(1,128)S(1)}) custom-call(s32[1,1280]{1,0:T(1,128)S(1)} %reshape.80.dest_ref, bf16[1280,768]{1,0:T(8,128)(2,1)} %tiles_hbm.1), custom_call_target="tpu_custom_call" | custom-call | tf_op jit(solution)/shard_map/pack/pallas_call | solution.py:425
  5.3 7.3 %all-to-all-start = ((bf16[32,32,768]{2,1,0:T(8,128)(2,1)}), bf16[32,32,768]{2,1,0:T(8,128)(2,1)S(1)}, u32[]{:S(2)}, u32[]{:S(2)}) async-start(bf16[32,32,768]{2,1,0:T(8,128)(2,1)} %bitcast.22), calls=%async_computation | async-start | bytes 3145728 | tf_op jit(solution)/shard_map/all_to_all | solution.py:471
  12.6 0.0 slice-start
  12.6 0.8 collective-permute-start
  13.4 0.7 constant_dynamic-slice_fusion
  14.1 0.7 constant_dynamic-slice_fusion.1
  14.8 0.6 fusion.6
  15.4 0.7 pad_add_fusion.segment_ref
  16.1 1.4 copy.32
  17.6 0.1 reshape_reshape.3
  17.7 0.1 copy.28
  17.7 0.1 reshape.83
  17.8 0.1 div.30
  17.9 0.1 and.31
  18.0 0.3 convert_reduce_fusion
  18.4 0.1 copy.30.slot_ref
  18.6 31.8 %all-to-all-done = bf16[32,32,768]{2,1,0:T(8,128)(2,1)S(1)} async-done(((bf16[32,32,768]{2,1,0:T(8,128)(2,1)}), bf16[32,32,768]{2,1,0:T(8,128)(2,1)S(1)}, u32[]{:S(2)}, u32[]{:S(2)}) %all-to-all-start) | async-done | bytes 1572896 | tf_op jit(solution)/shard_map/all_to_all | solution.py:471
  50.3 5.9 %project_first.1 = (bf16[512,768]{1,0:T(8,128)(2,1)}, bf16[8,784,128]{2,1,0:T(8,128)(2,1)}) custom-call(s32[1]{0:T(128)} %bitcast.8.segment, s32[512,1]{1,0:T(8,128)S(1)} %copy.30.slot_ref, bf16[16,128]{1,0:T(8,128)(2,1)S(1)} %fusion.2.extra_ref, bf16[1024,768]{1,0:T(8,128)(2,1)S(1)} %bitcast.18, f32[1,768]{1,0:T(1,128)S(1)} %broadcast_in_dim.17.gain_ref, ...), custom_call_target="tpu_custom_call" | custom-call | tf_op jit(solution)/shard_map/project_first/pallas_call | solution.py:425
  56.2 3.9 %all-to-all-start.1 = ((bf16[8,784,128]{2,1,0:T(8,128)(2,1)}), bf16[8,784,128]{2,1,0:T(8,128)(2,1)S(1)}, u32[]{:S(2)}, u32[]{:S(2)}) async-start(bf16[8,784,128]{2,1,0:T(8,128)(2,1)} %get-tuple-element.23), calls=%async_computation.1 | async-start | bytes 3211264 | tf_op jit(solution)/shard_map/all_to_all | solution.py:540
  60.1 3.3 %project_next.1 = bf16[8,768,128]{2,1,0:T(8,128)(2,1)} custom-call(s32[1]{0:T(128)} %bitcast.8.segment, bf16[512,768]{1,0:T(8,128)(2,1)S(1)} %copy-done.2, bf16[768,2304]{1,0:T(8,128)(2,1)} %w_hbm.4, bf16[768,768]{1,0:T(8,128)(2,1)} %bitcast.21), custom_call_target="tpu_custom_call" | custom-call | tf_op jit(solution)/shard_map/project_next/pallas_call | solution.py:425
  63.5 18.0 %all-to-all-done.1.block_ref = bf16[8,784,128]{2,1,0:T(8,128)(2,1)S(1)} async-done(((bf16[8,784,128]{2,1,0:T(8,128)(2,1)}), bf16[8,784,128]{2,1,0:T(8,128)(2,1)S(1)}, u32[]{:S(2)}, u32[]{:S(2)}) %all-to-all-start.1) | async-done | bytes 1605664 | tf_op jit(solution)/shard_map/all_to_all | solution.py:540
  81.5 3.8 %all-to-all-start.2 = ((bf16[8,768,128]{2,1,0:T(8,128)(2,1)}), bf16[8,768,128]{2,1,0:T(8,128)(2,1)S(1)}, u32[]{:S(2)}, u32[]{:S(2)}) async-start(bf16[8,768,128]{2,1,0:T(8,128)(2,1)} %project_next.1), calls=%async_computation.2 | async-start | bytes 3145728 | tf_op jit(solution)/shard_map/all_to_all | solution.py:540
  85.3 13.0 %attend.2.refs_0_ = bf16[8,512,128]{2,1,0:T(8,128)(2,1)S(1)} custom-call(s32[2]{0:T(128)S(1)} %get-tuple-element.26.place_ref, s32[2]{0:T(128)S(1)} %get-tuple-element.27.segment_ref, bf16[8,784,128]{2,1,0:T(8,128)(2,1)S(1)} %all-to-all-done.1.block_ref), custom_call_target="tpu_custom_call" | custom-call | tf_op jit(solution)/shard_map/attend/pallas_call | solution.py:425
  98.3 1.0 copy-done
  99.3 6.7 %all-to-all-done.2.block_ref = bf16[8,768,128]{2,1,0:T(8,128)(2,1)S(1)} async-done(((bf16[8,768,128]{2,1,0:T(8,128)(2,1)}), bf16[8,768,128]{2,1,0:T(8,128)(2,1)S(1)}, u32[]{:S(2)}, u32[]{:S(2)}) %all-to-all-start.2) | async-done | bytes 1572896 | tf_op jit(solution)/shard_map/all_to_all | solution.py:540
  106.0 7.8 %attend.3.refs_1_ = bf16[4,512,128]{2,1,0:T(8,128)(2,1)S(1)} custom-call(s32[1]{0:T(128)} %bitcast.5.place_ref, s32[1]{0:T(128)} %bitcast.7.segment_ref, bf16[8,768,128]{2,1,0:T(8,128)(2,1)S(1)} %all-to-all-done.2.block_ref), custom_call_target="tpu_custom_call" | custom-call | tf_op jit(solution)/shard_map/attend/pallas_call | solution.py:425
  113.9 5.1 %spread.1 = bf16[32,192,128]{2,1,0:T(8,128)(2,1)} custom-call(s32[3]{0:T(128)S(1)} %pad_add_fusion.segment_ref, bf16[8,784,128]{2,1,0:T(8,128)(2,1)S(1)} %all-to-all-done.1.block_ref, bf16[8,512,128]{2,1,0:T(8,128)(2,1)S(1)} %copy-done.1, bf16[4,512,128]{2,1,0:T(8,128)(2,1)S(1)} %attend.3.refs_1_), custom_call_target="tpu_custom_call" | custom-call | tf_op jit(solution)/shard_map/spread/pallas_call | solution.py:425
  119.0 2.7 %all-to-all-start.3 = ((bf16[32,192,128]{2,1,0:T(8,128)(2,1)}), bf16[32,192,128]{2,1,0:T(8,128)(2,1)S(1)}, u32[]{:S(2)}, u32[]{:S(2)}) async-start(bf16[32,192,128]{2,1,0:T(8,128)(2,1)} %spread.1), calls=%async_computation.3 | async-start | bytes 3145728 | tf_op jit(solution)/shard_map/all_to_all | solution.py:575
  121.7 0.3 copy.31.slot_ref
  122.0 37.5 %all-to-all-done.3.back_ref = bf16[32,192,128]{2,1,0:T(8,128)(2,1)S(1)} async-done(((bf16[32,192,128]{2,1,0:T(8,128)(2,1)}), bf16[32,192,128]{2,1,0:T(8,128)(2,1)S(1)}, u32[]{:S(2)}, u32[]{:S(2)}) %all-to-all-start.3) | async-done | bytes 1572896 | tf_op jit(solution)/shard_map/all_to_all | solution.py:575
  159.5 6.7 %finish.1 = bf16[1280,768]{1,0:T(8,128)(2,1)} custom-call(s32[1280,1]{1,0:T(8,128)S(1)} %copy.31.slot_ref, bf16[32,192,128]{2,1,0:T(8,128)(2,1)S(1)} %all-to-all-done.3.back_ref, bf16[1024,768]{1,0:T(8,128)(2,1)} %get-tuple-element.22.rows_hbm, f32[1,768]{1,0:T(1,128)S(1)} %broadcast_in_dim.18.gain_ref, bf16[768,768]{1,0:T(8,128)(2,1)} %w_hbm.5), custom_call_target="tpu_custom_call" | custom-call | tf_op jit(solution)/shard_map/finish/pallas_call | solution.py:425
  (22 shorter events, 0.1 us)
Async XLA Ops:
  5.3 7.4 %copy-start.5 = (s32[1,512]{1,0:T(1,128)S(1)}, s32[1,512]{1,0:T(1,128)}, u32[]{:S(2)}) copy-start(s32[1,512]{1,0:T(1,128)} %param.11) | copy-start | bytes 6148
  5.3 45.1 %all-to-all-start = ((bf16[32,32,768]{2,1,0:T(8,128)(2,1)}), bf16[32,32,768]{2,1,0:T(8,128)(2,1)S(1)}, u32[]{:S(2)}, u32[]{:S(2)}) async-start(bf16[32,32,768]{2,1,0:T(8,128)(2,1)} %bitcast.22), calls=%async_computation | async-start | bytes 3145728 | tf_op jit(solution)/shard_map/all_to_all | solution.py:471
  12.6 3.5 %slice-start = ((bf16[768,2304]{1,0:T(8,128)(2,1)}), bf16[768,768]{1,0:T(8,128)(2,1)S(1)}, s32[]{:S(2)}) async-start(bf16[768,2304]{1,0:T(8,128)(2,1)} %w_hbm.4), calls=%async_computation.4 | async-start | bytes 2359296 | tf_op jit(solution)/shard_map/slice | solution.py:492
  12.6 4.9 %collective-permute-start = (s32[4,128]{1,0:T(4,128)S(1)}, s32[4,128]{1,0:T(4,128)S(1)}, u32[]{:S(2)}, u32[]{:S(2)}) collective-permute-start(s32[4,128]{1,0:T(4,128)S(1)} %bitcast.25), channel_id=1, source_target_pairs={{0,0},{4,1},{8,2},{12,3},{16,4},{20,5},{24,6},{28,7},{1,8},{5,9},{... | collective-permute-start | bytes 6152 | tf_op jit(solution)/shard_map/ppermute | solution.py:453
  16.1 1.4 copy-start.3
  56.2 3.9 %copy-start.2 = (bf16[512,768]{1,0:T(8,128)(2,1)S(1)}, bf16[512,768]{1,0:T(8,128)(2,1)}, u32[]{:S(2)}) copy-start(bf16[512,768]{1,0:T(8,128)(2,1)} %get-tuple-element.24.normed_ref) | copy-start | bytes 2359300
  56.2 25.2 %all-to-all-start.1 = ((bf16[8,784,128]{2,1,0:T(8,128)(2,1)}), bf16[8,784,128]{2,1,0:T(8,128)(2,1)S(1)}, u32[]{:S(2)}, u32[]{:S(2)}) async-start(bf16[8,784,128]{2,1,0:T(8,128)(2,1)} %get-tuple-element.23), calls=%async_computation.1 | async-start | bytes 3211264 | tf_op jit(solution)/shard_map/all_to_all | solution.py:540
  81.5 24.5 %all-to-all-start.2 = ((bf16[8,768,128]{2,1,0:T(8,128)(2,1)}), bf16[8,768,128]{2,1,0:T(8,128)(2,1)S(1)}, u32[]{:S(2)}, u32[]{:S(2)}) async-start(bf16[8,768,128]{2,1,0:T(8,128)(2,1)} %project_next.1), calls=%async_computation.2 | async-start | bytes 3145728 | tf_op jit(solution)/shard_map/all_to_all | solution.py:540
  98.3 1.0 copy-start
  106.0 7.9 %copy-start.1 = (bf16[8,512,128]{2,1,0:T(8,128)(2,1)S(1)}, bf16[8,512,128]{2,1,0:T(8,128)(2,1)}, u32[]{:S(2)}) copy-start(bf16[8,512,128]{2,1,0:T(8,128)(2,1)} %copy-done) | copy-start | bytes 3145732
  119.0 3.0 %copy-start.4 = (f32[768]{0:T(1024)S(1)}, f32[768]{0:T(1024)}, u32[]{:S(2)}) copy-start(f32[768]{0:T(1024)} %param.15) | copy-start | bytes 9220
  119.0 40.5 %all-to-all-start.3 = ((bf16[32,192,128]{2,1,0:T(8,128)(2,1)}), bf16[32,192,128]{2,1,0:T(8,128)(2,1)S(1)}, u32[]{:S(2)}, u32[]{:S(2)}) async-start(bf16[32,192,128]{2,1,0:T(8,128)(2,1)} %spread.1), calls=%async_computation.3 | async-start | bytes 3145728 | tf_op jit(solution)/shard_map/all_to_all | solution.py:575

commit v5 on v4

--- a/solution.py
+++ b/solution.py
@@ -56,6 +56,16 @@
     return parts
 
 
+def shares(part):
+    held = [heads for heads, _ in part[2]]
+    return len(held[0]) == 1 and len(held) % 2 == 0 and held[::2] == held[1::2]
+
+
+def depth_of(part, visible):
+    depth = len(part[2][0][0]) * visible + visible // 2
+    return depth // 2 if shares(part) else depth
+
+
 def place_pair(left, left_odd, right, right_odd):
     left = swap(left) if left_odd else left
     right = right if right_odd else swap(right)
@@ -65,6 +75,22 @@
 
 def swap(tile):
     return jnp.concatenate([tile[:, HDIM:], tile[:, :HDIM]], axis=1)
+
+
+def column_of(row):
+    pieces = [row[:, at : at + 128].astype(jnp.float32) for at in range(0, row.shape[1], 128)]
+    pieces = [jnp.broadcast_to(piece, (8, 128)).T[:, :1] for piece in pieces]
+    return jnp.concatenate(pieces, axis=0).astype(jnp.int32)
+
+
+def member_index():
+    return lax.axis_index("high") * lax.axis_size("low") + lax.axis_index("low")
+
+
+def dealt_unit(segments, first, owned, i):
+    start = member_index() * owned
+    segment = lax.rem(start + i, segments)
+    return lax.div(start + i, segments) - lax.div(start, segments), segment
 
 
 def dot_nt(left, right):
@@ -117,7 +143,7 @@
     return jnp.where(row < column, 1.0, 0.0).astype(jnp.bfloat16)
 
 
-def project_part(part, segment, normed, extra, w_ref, wvt_ref, send_hbm, send_ref, q_ref, k_ref, vt_ref, sems):
+def project_part(part, normed, extra, w_ref, wvt_ref, send_hbm, send_ref, q_ref, k_ref, vt_ref, sems):
     first, last, members = part
     visible, width = normed.shape
     rows, middle = visible // CLASSES, visible // 2
@@ -138,24 +164,31 @@
         for member, (heads, _) in enumerate(members):
             for place in [place for place, one in enumerate(heads) if one == head]:
                 base = place * visible
-                send_ref[member, base : base + middle, :] = keys
-                for i in range(visible // wide):
-                    top = base + middle + i * HDIM
-                    send_ref[member, top : top + HDIM, :] = values[:, i * wide : (i + 1) * wide]
+                if not shares(part) or member % 2 == 0:
+                    send_ref[member, base : base + middle, :] = keys
+                if not shares(part) or member % 2 == 1:
+                    base += 0 if shares(part) else middle
+                    for i in range(visible // wide):
+                        top = base + i * HDIM
+                        send_ref[member, top : top + HDIM, :] = values[:, i * wide : (i + 1) * wide]
     copies = []
     for member, (heads, units) in enumerate(members):
-        base = len(heads) * visible
-        for i in range(CLASSES // 2):
+        base, steps = len(heads) * visible, range(CLASSES // 2)
+        if shares(part):
+            steps = steps[member % 2 * CLASSES // 4 : (member % 2 + 1) * CLASSES // 4]
+            base = middle - steps[0] * rows
+        for i in steps:
             tile = queries_of(heads[0], 2 * i)
             for place, head in enumerate(heads[1:], 1):
+                segment = lax.div(member_index(), SEG // visible)
                 mine = functools.reduce(
-                    jnp.logical_or, [segment[0] == one for at, one in units if at == place], False
+                    jnp.logical_or, [segment == one for at, one in units if at == place], False
                 )
                 if head != heads[0]:
                     tile = jnp.where(mine, queries_of(head, 2 * i), tile)
             send_ref[member, base + i * rows : base + (i + 1) * rows, :] = tile
         if extra is not None:
-            send_ref[member, base + middle :, :] = extra
+            send_ref[member, depth_of(part, visible) :, :] = extra
         copies.append(write(send_ref, send_hbm, member, 1, sems))
     return copies
 
@@ -173,11 +206,11 @@
     return copies
 
 
-def first_kernel(part, segment, slot_ref, extra_ref, arrived_ref, gain_ref, w_hbm, wvt_hbm, normed_hbm, send_hbm,
+def first_kernel(part, slot_ref, extra_ref, arrived_ref, gain_ref, w_hbm, wvt_hbm, normed_hbm, send_hbm,
                  w_ref, wvt_ref, send_ref, q_ref, k_ref, vt_ref, sems, normed_ref, more):
     weights = fetch_weights(part, w_hbm, wvt_hbm, w_ref, wvt_ref, more)
     visible, slots = normed_ref.shape[0], arrived_ref.shape[0]
-    chosen = one_hot(lax.broadcasted_iota(jnp.int32, (visible, slots), 1), slot_ref[...])
+    chosen = one_hot(lax.broadcasted_iota(jnp.int32, (visible, slots), 1), column_of(slot_ref[...]))
     rows = dot(chosen, arrived_ref[...])
     normed = layer_norm(rows, gain_ref[...]).astype(jnp.bfloat16)
     normed_ref[...] = normed
@@ -187,23 +220,48 @@
     for copy in weights:
         copy.wait()
     copies += project_part(
-        part, segment, normed, extra_ref[...], w_ref, wvt_ref, send_hbm, send_ref, q_ref, k_ref, vt_ref, sems
+        part, normed, extra_ref[...], w_ref, wvt_ref, send_hbm, send_ref, q_ref, k_ref, vt_ref, sems
     )
     for copy in copies:
         copy.wait()
 
 
-def next_kernel(part, segment, normed_ref, w_hbm, wvt_hbm, send_hbm, w_ref, wvt_ref, send_ref, q_ref, k_ref, vt_ref, sems, more):
+def next_kernel(part, normed_ref, w_hbm, wvt_hbm, send_hbm, w_ref, wvt_ref, send_ref, q_ref, k_ref, vt_ref, sems, more):
     for copy in fetch_weights(part, w_hbm, wvt_hbm, w_ref, wvt_ref, more):
         copy.wait()
     copies = project_part(
-        part, segment, normed_ref[...], None, w_ref, wvt_ref, send_hbm, send_ref, q_ref, k_ref, vt_ref, sems
+        part, normed_ref[...], None, w_ref, wvt_ref, send_hbm, send_ref, q_ref, k_ref, vt_ref, sems
     )
     for copy in copies:
         copy.wait()
 
 
-def attend_kernel(visible, heads, place_ref, segment_ref, block_ref, out_ref, score_ref, peak_ref):
+def attend_kernel(visible, part, whole, staged, *refs):
+    first, heads = part[0], len(part[2][0][0])
+    block_ref, *refs = refs
+    if shares(part):
+        other_ref, *refs = refs
+    result_ref, *refs = refs
+    full_ref, own_ref = block_ref, block_ref
+    if shares(part):
+        *refs, full_ref = refs
+    *infos, score_ref, peak_ref = refs[:-2] if staged else refs
+    out_ref, sems = refs[-2:] if staged else (result_ref, None)
+    for info_ref in infos:
+        info_ref[...] = own_ref[:, depth_of(part, visible) :, :]
+    if shares(part):
+        odd_member = lax.rem(member_index(), 2)
+        half, quarter = visible // 2, visible // 4
+        for odd, (even_ref, odd_ref) in enumerate(((own_ref, other_ref), (other_ref, own_ref))):
+
+            @pl.when(odd_member == odd)
+            def _():
+                full_ref[:, :half, :] = even_ref[:, :half, :]
+                full_ref[:, half:visible, :] = odd_ref[:, :half, :]
+                full_ref[:, visible : visible + quarter, :] = even_ref[:, half : half + quarter, :]
+                full_ref[:, visible + quarter :, :] = odd_ref[:, half : half + quarter, :]
+
+    block_ref = full_ref
     members = block_ref.shape[0]
     rows, middle = visible // CLASSES, visible // 2
     group = SEG // visible
@@ -216,8 +274,8 @@
 
     def tile_of(turn, half):
         unit, step = turn // pairs, turn % pairs
-        base = pl.multiple_of(place_ref[unit] * visible, visible)
-        return step, segment_ref[unit], 2 * step + half, base
+        place, segment = (0, unit) if whole else dealt_unit(segments, first, turns // pairs, unit)
+        return step, segment, 2 * step + half, pl.multiple_of(place * visible, visible)
 
     def member_of(segment, i, apart):
         return lax.rem(segment + apart, segments) * group + i
@@ -303,40 +361,75 @@
             at = pl.multiple_of((2 * step + half) * rows, rows)
             for i in range(group):
                 out_ref[unit * group + i, pl.ds(at, rows), :] = twice[i * rows : (i + 1) * rows, :]
+        if staged:
+
+            @pl.when(step == pairs - 1)
+            def _():
+                at = pl.ds(unit * group, group)
+                pltpu.make_async_copy(out_ref.at[at], result_ref.at[at], sems.at[unit]).start()
         return carry
 
     run(score_steps(0, 0))
     lax.fori_loop(0, turns, body, 0)
-
-
-def spread_kernel(heads, capacity, segment_ref, block_ref, *refs):
-    mixed_refs, (out_hbm, out_ref, sem) = refs[:-3], refs[-3:]
+    if staged:
+        for unit in range(turns // pairs):
+            at = pl.ds(unit * group, group)
+            pltpu.make_async_copy(out_ref.at[at], result_ref.at[at], sems.at[unit]).wait()
+
+
+def spread_kernel(capacity, fixed, info_ref, *refs):
+    mixed_refs, (out_hbm, out_ref, sems) = refs[:-3], refs[-3:]
     visible = mixed_refs[0].shape[1]
-    members = block_ref.shape[0]
+    members = info_ref.shape[0]
     devices = out_ref.shape[0]
     group = SEG // visible
+    segments = members // group
     slots = devices * capacity
     lines = visible // 128
-    top = heads * visible + visible // 2
+    wide = 2 * HDIM
     units = [(ref, i) for ref in mixed_refs for i in range(ref.shape[0] // group)]
     step = math.gcd(slots, 256)
-    low = lax.broadcasted_iota(jnp.int32, (step, 2 * HDIM), 1) < HDIM
-    slot_of = {}
-
-    def slot_row(u, i):
-        if (u, i) not in slot_of:
-            info = block_ref[segment_ref[u] * group + i, top : top + 16, :].astype(jnp.float32)
-            place = (info[:lines] * capacity + info[lines : 2 * lines]).astype(jnp.int32)
-            slot_of[u, i] = jnp.concatenate([place[j : j + 1] for j in range(lines)], axis=1)
-        return slot_of[u, i]
-
-    def spread(u, i, start):
-        wanted = lax.broadcasted_iota(jnp.int32, (step, visible), 0) + start
+    low = lax.broadcasted_iota(jnp.int32, (step, wide), 1) < HDIM
+
+    def slots_of(source):
+        info = info_ref[source].astype(jnp.float32)
+        place = (info[:lines] * capacity + info[lines : 2 * lines]).astype(jnp.int32)
+        return jnp.concatenate([place[j : j + 1] for j in range(lines)], axis=1)
+
+    def rows_of(u, i):
         ref, unit = units[u]
-        return dot(one_hot(wanted, slot_row(u, i)), ref[unit * group + i])
-
+        return ref[unit * group + i]
+
+    def segment_of(u):
+        return dealt_unit(segments, 0, len(units) - fixed, u - fixed)[1]
+
+    jobs = []
+    if fixed:
+        for segment in range(segments):
+            for i in range(group):
+                others = [u for u in range(len(units)) if u >= fixed]
+                own = [u for u in range(fixed) if u % segments == segment]
+                right = [rows_of(u, i) for u in own]
+                right += [
+                    jnp.where(segment_of(u) == segment, rows_of(u, i), jnp.zeros((visible, wide), jnp.bfloat16))
+                    for u in others
+                ]
+                jobs.append((i, own + others, slots_of(segment * group + i), jnp.concatenate(right, axis=1)))
+    else:
+        for u in range(len(units)):
+            for i in range(group):
+                jobs.append((i, [u], slots_of(segment_of(u) * group + i), rows_of(u, i)))
+
+    copies = []
     for start in range(0, slots, step):
-        owners = slice(start // capacity, (start + step) // capacity)
+        found = {}
+        for i, names, place, right in jobs:
+            wanted = lax.broadcasted_iota(jnp.int32, (step, visible), 0) + start
+            result = dot(one_hot(wanted, place), right)
+            for j, u in enumerate(names):
+                piece = result[:, j * wide : (j + 1) * wide]
+                found[u, i] = found[u, i] + piece if (u, i) in found else piece
+        first, last = start // capacity, (start + step) // capacity
         for u in range(0, len(units), 2):
             base = u // 2 * group * capacity
             if u + 1 < len(units):
@@ -344,12 +437,12 @@
             else:
                 pairs = [((u, i), (u, i + group // 2)) for i in range(group // 2)]
             for i, (left, right) in enumerate(pairs):
-                both = jnp.where(low, spread(*left, start), spread(*right, start)).astype(jnp.bfloat16)
-                both = both.reshape(step // capacity, capacity, 2 * HDIM)
-                out_ref[owners, base + i * capacity : base + (i + 1) * capacity, :] = both
-    copy = pltpu.make_async_copy(out_ref, out_hbm, sem)
-    copy.start()
-    copy.wait()
+                both = jnp.where(low, found[left], found[right]).astype(jnp.bfloat16)
+                both = both.reshape(step // capacity, capacity, wide)
+                out_ref[first:last, base + i * capacity : base + (i + 1) * capacity, :] = both
+        copies.append(write(out_ref, out_hbm, first, last - first, sems))
+    for copy in copies:
+        copy.wait()
 
 
 def finish_kernel(parts, capacity, slot_ref, back_ref, rows_hbm, gain_ref, w_hbm, out_hbm,
@@ -400,7 +493,7 @@
     copies = []
     for start in range(0, count, step):
         here = lax.broadcasted_iota(jnp.int32, (step, slots), 1)
-        chosen = one_hot(slot_ref[start : start + step, :], here)
+        chosen = one_hot(column_of(slot_ref[:, start : start + step]), here)
         out_ref[start : start + step, :] = dot(chosen, answer_ref[...]).astype(jnp.bfloat16)
         copies.append(write(out_ref, out_hbm, start, step, sems))
     for copy in copies:
@@ -410,13 +503,15 @@
 IN_VMEM = pl.BlockSpec(memory_space=pltpu.VMEM)
 IN_HBM = pl.BlockSpec(memory_space=pltpu.HBM)
 IN_SMEM = pl.BlockSpec(memory_space=pltpu.SMEM)
+PINNED = pl.BlockSpec(memory_space=pltpu.VMEM)
+SPACES = {id(IN_HBM): pltpu.HBM, id(PINNED): pltpu.VMEM}
 COPIES = pltpu.SemaphoreType.DMA
 
 
 def call(kernel, outs, out_specs, name, *operands, in_specs=None, scratch=()):
     in_specs = in_specs or [IN_VMEM] * len(operands)
     operands = [
-        pltpu.with_memory_space_constraint(operand, pltpu.HBM) if spec is IN_HBM else operand
+        pltpu.with_memory_space_constraint(operand, SPACES[id(spec)]) if id(spec) in SPACES else operand
         for operand, spec in zip(operands, in_specs)
     ]
     outs = jax.tree.map(
@@ -427,7 +522,7 @@
         out_shape=outs,
         in_specs=in_specs,
         out_specs=out_specs,
-        scratch_shapes=list(scratch),
+        scratch_shapes=[one for one in scratch if one is not None],
         compiler_params=pltpu.CompilerParams(vmem_limit_bytes=VMEM),
         name=name,
     )(*operands)
@@ -480,22 +575,13 @@
     lines = visible // 128
     extra = jnp.concatenate([source.reshape(lines, 128), placed.reshape(lines, 128)])
     extra = jnp.pad(extra, ((0, 16 - 2 * lines), (0, 0))).astype(bf16)
-    member = lax.axis_index(inside)
-    tables = [
-        jnp.array([list(zip(*units)) for _, units in part], jnp.int32)[member] for _, _, part in parts
-    ]
-    places = [table[0] for table in tables]
-    sought = [table[1] for table in tables]
-    every = jnp.concatenate(sought)
-    slot, extra, places, sought, every = lax.optimization_barrier((slot, extra, places, sought, every))
-
     weights = (w_qkv, w_qkv[:, 2 * width :].T)
-    mine = [member // group]
-    blocks = []
-    for i, part in enumerate(parts):
+    blocks = {}
+    sequence = list(range(len(parts)))[::-1]
+    for i in sequence:
+        part = parts[i]
         first, last, dealt = part
-        heads = len(dealt[0][0])
-        depth = heads * visible + visible // 2 + (16 if i == 0 else 0)
+        depth = depth_of(part, visible) + (16 if i == sequence[0] else 0)
         shape = jax.ShapeDtypeStruct((members, depth, 2 * HDIM), bf16)
         size = (last - first) * HDIM
         scratch = [
@@ -507,20 +593,18 @@
             pltpu.VMEM((size, visible), bf16),
             COPIES((members,)),
         ]
-        segment = jnp.array(mine, jnp.int32)
-        if i == 0:
+        if i == sequence[0]:
             normed, send = call(
                 functools.partial(first_kernel, part),
                 (jax.ShapeDtypeStruct((visible, width), bf16), shape),
                 (IN_HBM,) * 2,
                 "project_first",
-                segment,
-                slot[:, None],
+                slot[None, :],
                 extra,
                 arrived,
                 gain_attn[None, :],
                 *weights,
-                in_specs=[IN_SMEM] + [IN_VMEM] * 4 + [IN_HBM] * 2,
+                in_specs=[IN_VMEM] * 4 + [IN_HBM] * 2,
                 scratch=scratch + [pltpu.VMEM((visible, width), bf16), COPIES((4,))],
             )
         else:
@@ -529,48 +613,58 @@
                 shape,
                 IN_HBM,
                 "project_next",
-                segment,
                 normed,
                 *weights,
-                in_specs=[IN_SMEM, IN_VMEM] + [IN_HBM] * 2,
+                in_specs=[IN_VMEM] + [IN_HBM] * 2,
                 scratch=scratch + [COPIES((3,))],
             )
         if blocks:
-            blocks[-1], send = lax.optimization_barrier((blocks[-1], send))
-        blocks.append(lax.all_to_all(send, inside, split_axis=0, concat_axis=0, tiled=True))
-
-    mixed = []
-    for (_, _, part), block, place, segment in zip(parts, blocks, places, sought):
-        heads, units = len(part[0][0]), len(part[0][1])
+            blocks[before], send = lax.optimization_barrier((blocks[before], send))
+        blocks[i] = lax.all_to_all(send, inside, split_axis=0, concat_axis=0, tiled=True)
+        before = i
+
+    mixed, infos = {}, []
+    for i in sequence:
+        part = parts[i]
+        units = len(part[2][0][1])
         depth = SEG + (segments - 1) * SEG // CLASSES
-        result = call(
-            functools.partial(attend_kernel, visible, heads),
-            jax.ShapeDtypeStruct((units * group, visible, 2 * HDIM), bf16),
-            IN_VMEM,
+        outs = [jax.ShapeDtypeStruct((units * group, visible, 2 * HDIM), bf16)]
+        staged = i != sequence[-1]
+        if i == sequence[0]:
+            outs.append(jax.ShapeDtypeStruct((members, 16, 2 * HDIM), bf16))
+        operands = [blocks[i]]
+        if shares(part):
+            partners = [(member, member ^ 1) for member in range(members)]
+            operands.append(lax.ppermute(blocks[i], inside, partners))
+        mixed[i], *info = call(
+            functools.partial(attend_kernel, visible, part, i < HEADS // members, staged),
+            outs,
+            [IN_HBM if staged else IN_VMEM] + [IN_VMEM] * (len(outs) - 1),
             "attend",
-            place,
-            segment,
-            block,
-            in_specs=[IN_SMEM, IN_SMEM, IN_VMEM],
+            *operands,
             scratch=[
                 pltpu.VMEM((2, depth, SEG // CLASSES), jnp.float32),
                 pltpu.VMEM((2, 8, SEG // CLASSES), jnp.float32),
+                pltpu.VMEM(outs[0].shape, bf16) if staged else None,
+                COPIES((units,)) if staged else None,
+                pltpu.VMEM((members, visible + visible // 2, 2 * HDIM), bf16) if shares(part) else None,
             ],
         )
-        mixed.append(result)
-
-    heads = len(parts[0][2][0][0])
-    shape = jax.ShapeDtypeStruct((devices, every.shape[0] * group * capacity // 2, 2 * HDIM), bf16)
+        infos += info
+    mixed = [mixed[i] for i in range(len(parts))]
+
+    fixed = HEADS // members * segments
+    units_each = HEADS * segments // members
+    shape = jax.ShapeDtypeStruct((devices, units_each * group * capacity // 2, 2 * HDIM), bf16)
     answers = call(
-        functools.partial(spread_kernel, heads, capacity),
+        functools.partial(spread_kernel, capacity, fixed),
         shape,
         IN_HBM,
         "spread",
-        every,
-        blocks[0],
+        infos[0],
         *mixed,
-        in_specs=[IN_SMEM] + [IN_VMEM] * (1 + len(mixed)),
-        scratch=[pltpu.VMEM(shape.shape, bf16), COPIES],
+        in_specs=[IN_VMEM] * (1 + len(mixed)),
+        scratch=[pltpu.VMEM(shape.shape, bf16), COPIES((slots // math.gcd(slots, 256),))],
     )
     back = lax.all_to_all(answers, axes, split_axis=0, concat_axis=0, tiled=True)
     return call(
@@ -578,7 +672,7 @@
         jax.ShapeDtypeStruct((count, width), bf16),
         IN_HBM,
         "finish",
-        send_slot.reshape(count, 1),
+        send_slot,
         back,
         outgoing,
         gain_out[None, :],

time: 167 us -> 160 us (0.958)
  Pallas kernels: 46.4 us -> 43.9 us
  local copies, waits for them, and re-layouts: 5.88 us -> 4.07 us
  waiting for transfers between devices: 94 us -> 92.2 us
    all_to_all x2, waiting for transfers between devices: 24.8 us -> 19 us  [on_device(): lax.all_to_all(send, inside, split_axis=0, concat_axis=0, tiled=True)]
    pallas_call x7, Pallas kernels: 46.4 us -> 43.9 us  [call(): pl.pallas_call(kernel, out_shape=outs, in_specs=in_specs, out_specs=out_s...]
    ppermute x0 -> x1, waiting for transfers between devices: none -> 2.31 us  [on_device(): operands.append(lax.ppermute(blocks[i], inside, partners))]
  transfers between devices with their start and end apart: 5 -> 6, of which waited for: 4 -> 5; matrix products, arithmetic and copies ran while one was open for 3% -> 2% of each run, Pallas kernels for 10% -> 8%
where the time goes in v5:
time: 160 us
  waiting for transfers between devices  92.2 us (58%)
  Pallas kernels  43.9 us (27%)
  starting transfers between devices  18.6 us (12%)
  local copies, waits for them, and re-layouts  4.07 us (3%)
    pallas_call x7, Pallas kernels, call(): pl.pallas_call(kernel, out_shape=outs, in_specs=in_specs, out_specs=out_s...  43.9 us
    all_to_all x1, waiting for transfers between devices, on_device(): lax.all_to_all(answers, axes, split_axis=0, concat_axis=0, tiled=True)  37.7 us
    all_to_all x1, waiting for transfers between devices, on_device(): lax.all_to_all(outgoing.reshape(devices, capacity, width), axes, split_ax...  33.2 us
    all_to_all x2, waiting for transfers between devices, on_device(): lax.all_to_all(send, inside, split_axis=0, concat_axis=0, tiled=True)  19 us
    all_to_all x2, starting transfers between devices, on_device(): lax.all_to_all(send, inside, split_axis=0, concat_axis=0, tiled=True)  7.51 us
    all_to_all x1, starting transfers between devices, on_device(): lax.all_to_all(outgoing.reshape(devices, capacity, width), axes, split_ax...  7.34 us
  transfers between devices with their start and end apart: 6, of which 5 were waited for; matrix products, arithmetic and copies ran while one was open for 2% of the time, Pallas kernels for 8%

profile of v5, /device:TPU:0, one launch (start us, length us, event | category | flops | bytes accessed | tf_op | source)
XLA Modules:
  0.0 159.6 jit_solution(14112575280745300025)
XLA Ops:
  0.0 0.7 reshape.121.dest_ref
  0.7 4.6 %pack.1 = (bf16[1024,768]{1,0:T(8,128)(2,1)}, s32[1,1280]{1,0:T(1,128)S(1)}) custom-call(s32[1,1280]{1,0:T(1,128)S(1)} %reshape.121.dest_ref, bf16[1280,768]{1,0:T(8,128)(2,1)} %tiles_hbm.1), custom_call_target="tpu_custom_call" | custom-call | tf_op jit(solution)/shard_map/pack/pallas_call | solution.py:520
  5.3 0.0 copy-start.4
  5.3 0.0 copy-start.2
  5.3 7.3 %all-to-all-start = ((bf16[32,32,768]{2,1,0:T(8,128)(2,1)}), bf16[32,32,768]{2,1,0:T(8,128)(2,1)S(1)}, u32[]{:S(2)}, u32[]{:S(2)}) async-start(bf16[32,32,768]{2,1,0:T(8,128)(2,1)} %bitcast.13), calls=%async_computation | async-start | bytes 3145728 | tf_op jit(solution)/shard_map/all_to_all | solution.py:566
  12.7 0.7 collective-permute-start
  13.3 1.4 slice.3
  14.7 1.4 copy.28
  16.1 0.1 reshape_reshape.3
  16.2 0.1 copy.26
  16.3 0.1 and.31
  16.4 0.1 and.34
  16.5 0.1 div.30
  16.6 0.1 div.32
  16.7 0.1 reshape.123
  16.8 0.3 convert_reduce_fusion
  17.2 33.2 %all-to-all-done = bf16[32,32,768]{2,1,0:T(8,128)(2,1)S(1)} async-done(((bf16[32,32,768]{2,1,0:T(8,128)(2,1)}), bf16[32,32,768]{2,1,0:T(8,128)(2,1)S(1)}, u32[]{:S(2)}, u32[]{:S(2)}) %all-to-all-start) | async-done | bytes 1572896 | tf_op jit(solution)/shard_map/all_to_all | solution.py:566
  50.4 4.5 %project_first.1 = (bf16[512,768]{1,0:T(8,128)(2,1)}, bf16[8,400,128]{2,1,0:T(8,128)(2,1)}) custom-call(s32[1,512]{1,0:T(1,128)S(1)} %fusion.5.slot_ref, bf16[16,128]{1,0:T(8,128)(2,1)S(1)} %fusion.2.extra_ref, bf16[1024,768]{1,0:T(8,128)(2,1)S(1)} %bitcast.10, f32[1,768]{1,0:T(1,128)S(1)} %broadcast_in_dim.4.gain_ref, bf16[768,2304]{1,0:T(8,128)(2,1)} %w_hbm.4, ...), custom_call_target="tpu_custom_call" | custom-call | tf_op jit(solution)/shard_map/project_first/pallas_call | solution.py:520
  54.9 0.0 copy-start
  54.9 3.9 %all-to-all-start.1 = ((bf16[8,400,128]{2,1,0:T(8,128)(2,1)}), bf16[8,400,128]{2,1,0:T(8,128)(2,1)S(1)}, u32[]{:S(2)}, u32[]{:S(2)}) async-start(bf16[8,400,128]{2,1,0:T(8,128)(2,1)} %get-tuple-element.15), calls=%async_computation.1 | async-start | bytes 1638400 | tf_op jit(solution)/shard_map/all_to_all | solution.py:623
  58.8 4.3 %project_next.1 = bf16[8,768,128]{2,1,0:T(8,128)(2,1)} custom-call(bf16[512,768]{1,0:T(8,128)(2,1)S(1)} %copy-done, bf16[768,2304]{1,0:T(8,128)(2,1)} %w_hbm.4, bf16[768,768]{1,0:T(8,128)(2,1)} %bitcast.12), custom_call_target="tpu_custom_call" | custom-call | tf_op jit(solution)/shard_map/project_next/pallas_call | solution.py:520
  63.2 8.6 %all-to-all-done.1.refs_0_ = bf16[8,400,128]{2,1,0:T(8,128)(2,1)S(1)} async-done(((bf16[8,400,128]{2,1,0:T(8,128)(2,1)}), bf16[8,400,128]{2,1,0:T(8,128)(2,1)S(1)}, u32[]{:S(2)}, u32[]{:S(2)}) %all-to-all-start.1) | async-done | bytes 819232 | tf_op jit(solution)/shard_map/all_to_all | solution.py:623
  71.8 3.6 %all-to-all-start.2 = ((bf16[8,768,128]{2,1,0:T(8,128)(2,1)}), bf16[8,768,128]{2,1,0:T(8,128)(2,1)S(1)}, u32[]{:S(2)}, u32[]{:S(2)}) async-start(bf16[8,768,128]{2,1,0:T(8,128)(2,1)} %project_next.1), calls=%async_computation.2 | async-start | bytes 3145728 | tf_op jit(solution)/shard_map/all_to_all | solution.py:623
  75.3 0.4 collective-permute-start.1
  75.7 2.3 %collective-permute-done.1.refs_1_ = bf16[8,400,128]{2,1,0:T(8,128)(2,1)S(1)} collective-permute-done((bf16[8,400,128]{2,1,0:T(8,128)(2,1)S(1)}, bf16[8,400,128]{2,1,0:T(8,128)(2,1)S(1)}, u32[]{:S(2)}, u32[]{:S(2)}) %collective-permute-start.1) | collective-permute-done | bytes 819232 | tf_op jit(solution)/shard_map/ppermute | solution.py:638
  78.1 7.8 %attend.2 = (bf16[4,512,128]{2,1,0:T(8,128)(2,1)}, bf16[8,16,128]{2,1,0:T(8,128)(2,1)S(1)}) custom-call(bf16[8,400,128]{2,1,0:T(8,128)(2,1)S(1)} %all-to-all-done.1.refs_0_, bf16[8,400,128]{2,1,0:T(8,128)(2,1)S(1)} %collective-permute-done.1.refs_1_), custom_call_target="tpu_custom_call" | custom-call | tf_op jit(solution)/shard_map/attend/pallas_call | solution.py:520
  85.8 10.4 %all-to-all-done.2.refs_0_ = bf16[8,768,128]{2,1,0:T(8,128)(2,1)S(1)} async-done(((bf16[8,768,128]{2,1,0:T(8,128)(2,1)}), bf16[8,768,128]{2,1,0:T(8,128)(2,1)S(1)}, u32[]{:S(2)}, u32[]{:S(2)}) %all-to-all-start.2) | async-done | bytes 1572896 | tf_op jit(solution)/shard_map/all_to_all | solution.py:623
  96.3 12.7 %attend.3.refs_0_ = bf16[8,512,128]{2,1,0:T(8,128)(2,1)S(1)} custom-call(bf16[8,768,128]{2,1,0:T(8,128)(2,1)S(1)} %all-to-all-done.2.refs_0_), custom_call_target="tpu_custom_call" | custom-call | tf_op jit(solution)/shard_map/attend/pallas_call | solution.py:520
  109.0 3.2 %spread.1 = bf16[32,192,128]{2,1,0:T(8,128)(2,1)} custom-call(bf16[8,16,128]{2,1,0:T(8,128)(2,1)S(1)} %get-tuple-element.18.info_ref, bf16[8,512,128]{2,1,0:T(8,128)(2,1)S(1)} %attend.3.refs_0_, bf16[4,512,128]{2,1,0:T(8,128)(2,1)S(1)} %copy-done.1), custom_call_target="tpu_custom_call" | custom-call | tf_op jit(solution)/shard_map/spread/pallas_call | solution.py:520
  112.2 2.7 %all-to-all-start.3 = ((bf16[32,192,128]{2,1,0:T(8,128)(2,1)}), bf16[32,192,128]{2,1,0:T(8,128)(2,1)S(1)}, u32[]{:S(2)}, u32[]{:S(2)}) async-start(bf16[32,192,128]{2,1,0:T(8,128)(2,1)} %spread.1), calls=%async_computation.3 | async-start | bytes 3145728 | tf_op jit(solution)/shard_map/all_to_all | solution.py:669
  115.0 37.7 %all-to-all-done.3.back_ref = bf16[32,192,128]{2,1,0:T(8,128)(2,1)S(1)} async-done(((bf16[32,192,128]{2,1,0:T(8,128)(2,1)}), bf16[32,192,128]{2,1,0:T(8,128)(2,1)S(1)}, u32[]{:S(2)}, u32[]{:S(2)}) %all-to-all-start.3) | async-done | bytes 1572896 | tf_op jit(solution)/shard_map/all_to_all | solution.py:669
  152.7 6.7 %finish.1 = bf16[1280,768]{1,0:T(8,128)(2,1)} custom-call(s32[1,1280]{1,0:T(1,128)S(1)} %get-tuple-element.13.slot_ref, bf16[32,192,128]{2,1,0:T(8,128)(2,1)S(1)} %all-to-all-done.3.back_ref, bf16[1024,768]{1,0:T(8,128)(2,1)} %get-tuple-element.14.rows_hbm, f32[1,768]{1,0:T(1,128)S(1)} %broadcast_in_dim.10.gain_ref, bf16[768,768]{1,0:T(8,128)(2,1)} %w_hbm.5), custom_call_target="tpu_custom_call" | custom-call | tf_op jit(solution)/shard_map/finish/pallas_call | solution.py:520
  (17 shorter events, 0.1 us)
Async XLA Ops:
  5.3 7.4 %copy-start.4 = (s32[1,512]{1,0:T(1,128)S(1)}, s32[1,512]{1,0:T(1,128)}, u32[]{:S(2)}) copy-start(s32[1,512]{1,0:T(1,128)} %param.9) | copy-start | bytes 6148
  5.3 8.0 %copy-start.2 = (f32[768]{0:T(1024)S(1)}, f32[768]{0:T(1024)}, u32[]{:S(2)}) copy-start(f32[768]{0:T(1024)} %param.12) | copy-start | bytes 9220
  5.3 45.1 %all-to-all-start = ((bf16[32,32,768]{2,1,0:T(8,128)(2,1)}), bf16[32,32,768]{2,1,0:T(8,128)(2,1)S(1)}, u32[]{:S(2)}, u32[]{:S(2)}) async-start(bf16[32,32,768]{2,1,0:T(8,128)(2,1)} %bitcast.13), calls=%async_computation | async-start | bytes 3145728 | tf_op jit(solution)/shard_map/all_to_all | solution.py:566
  12.7 3.5 %collective-permute-start = (s32[4,128]{1,0:T(4,128)S(1)}, s32[4,128]{1,0:T(4,128)S(1)}, u32[]{:S(2)}, u32[]{:S(2)}) collective-permute-start(s32[4,128]{1,0:T(4,128)S(1)} %bitcast.16), channel_id=1, source_target_pairs={{0,0},{4,1},{8,2},{12,3},{16,4},{20,5},{24,6},{28,7},{1,8},{5,9},{... | collective-permute-start | bytes 6152 | tf_op jit(solution)/shard_map/ppermute | solution.py:548
  54.9 3.9 %copy-start = (bf16[512,768]{1,0:T(8,128)(2,1)S(1)}, bf16[512,768]{1,0:T(8,128)(2,1)}, u32[]{:S(2)}) copy-start(bf16[512,768]{1,0:T(8,128)(2,1)} %get-tuple-element.16.normed_ref) | copy-start | bytes 2359300
  54.9 16.8 %all-to-all-start.1 = ((bf16[8,400,128]{2,1,0:T(8,128)(2,1)}), bf16[8,400,128]{2,1,0:T(8,128)(2,1)S(1)}, u32[]{:S(2)}, u32[]{:S(2)}) async-start(bf16[8,400,128]{2,1,0:T(8,128)(2,1)} %get-tuple-element.15), calls=%async_computation.1 | async-start | bytes 1638400 | tf_op jit(solution)/shard_map/all_to_all | solution.py:623
  71.8 24.5 %all-to-all-start.2 = ((bf16[8,768,128]{2,1,0:T(8,128)(2,1)}), bf16[8,768,128]{2,1,0:T(8,128)(2,1)S(1)}, u32[]{:S(2)}, u32[]{:S(2)}) async-start(bf16[8,768,128]{2,1,0:T(8,128)(2,1)} %project_next.1), calls=%async_computation.2 | async-start | bytes 3145728 | tf_op jit(solution)/shard_map/all_to_all | solution.py:623
  75.3 2.7 %collective-permute-start.1 = (bf16[8,400,128]{2,1,0:T(8,128)(2,1)S(1)}, bf16[8,400,128]{2,1,0:T(8,128)(2,1)S(1)}, u32[]{:S(2)}, u32[]{:S(2)}) collective-permute-start(bf16[8,400,128]{2,1,0:T(8,128)(2,1)S(1)} %all-to-all-done.1.refs_0_), channel_id=1, source_target_pairs={{0,1},{1,0},{2,3},{3,2},{4,5},{5,4},{6,7},{7,6},{8,9},{9,8},{10,11... | collective-permute-start | bytes 2457608 | tf_op jit(solution)/shard_map/ppermute | solution.py:638
  85.8 23.2 %copy-start.1 = (bf16[4,512,128]{2,1,0:T(8,128)(2,1)S(1)}, bf16[4,512,128]{2,1,0:T(8,128)(2,1)}, u32[]{:S(2)}) copy-start(bf16[4,512,128]{2,1,0:T(8,128)(2,1)} %get-tuple-element.20.refs_1_) | copy-start | bytes 1572868
  112.2 2.7 %copy-start.3 = (f32[768]{0:T(1024)S(1)}, f32[768]{0:T(1024)}, u32[]{:S(2)}) copy-start(f32[768]{0:T(1024)} %param.13) | copy-start | bytes 9220
  112.2 40.5 %all-to-all-start.3 = ((bf16[32,192,128]{2,1,0:T(8,128)(2,1)}), bf16[32,192,128]{2,1,0:T(8,128)(2,1)S(1)}, u32[]{:S(2)}, u32[]{:S(2)}) async-start(bf16[32,192,128]{2,1,0:T(8,128)(2,1)} %spread.1), calls=%async_computation.3 | async-start | bytes 3145728 | tf_op jit(solution)/shard_map/all_to_all | solution.py:669

commit v6 on v5

--- a/solution.py
+++ b/solution.py
@@ -101,7 +101,7 @@
     fetch = pltpu.make_async_copy(tiles_hbm, tiles_ref, sem)
     fetch.start()
     slots, _ = out_ref.shape
-    count = dest_ref.shape[1]
+    count = dest_ref.shape[0] * 128
     devices = slots // capacity
     target = jnp.right_shift(dest_ref[...], visible.bit_length() - 1)
     lanes = 128
@@ -109,7 +109,7 @@
     offset = jnp.zeros((devices, 1), jnp.float32)
     pieces = []
     for start in range(0, count, lanes):
-        here = target[:, start : start + lanes]
+        here = target[start // lanes : start // lanes + 1, :]
         device = lax.broadcasted_iota(jnp.int32, (devices, lanes), 0)
         chosen = jnp.where(device == here, 1.0, 0.0)
         rank = dot(chosen.astype(jnp.bfloat16), before) + offset
@@ -236,17 +236,16 @@
         copy.wait()
 
 
-def attend_kernel(visible, part, whole, staged, *refs):
+def attend_kernel(visible, part, whole, *refs):
     first, heads = part[0], len(part[2][0][0])
     block_ref, *refs = refs
     if shares(part):
         other_ref, *refs = refs
-    result_ref, *refs = refs
+    out_ref, *refs = refs
     full_ref, own_ref = block_ref, block_ref
     if shares(part):
         *refs, full_ref = refs
-    *infos, score_ref, peak_ref = refs[:-2] if staged else refs
-    out_ref, sems = refs[-2:] if staged else (result_ref, None)
+    *infos, score_ref, peak_ref = refs
     for info_ref in infos:
         info_ref[...] = own_ref[:, depth_of(part, visible) :, :]
     if shares(part):
@@ -361,25 +360,14 @@
             at = pl.multiple_of((2 * step + half) * rows, rows)
             for i in range(group):
                 out_ref[unit * group + i, pl.ds(at, rows), :] = twice[i * rows : (i + 1) * rows, :]
-        if staged:
-
-            @pl.when(step == pairs - 1)
-            def _():
-                at = pl.ds(unit * group, group)
-                pltpu.make_async_copy(out_ref.at[at], result_ref.at[at], sems.at[unit]).start()
         return carry
 
     run(score_steps(0, 0))
     lax.fori_loop(0, turns, body, 0)
-    if staged:
-        for unit in range(turns // pairs):
-            at = pl.ds(unit * group, group)
-            pltpu.make_async_copy(out_ref.at[at], result_ref.at[at], sems.at[unit]).wait()
-
-
-def spread_kernel(capacity, fixed, info_ref, *refs):
-    mixed_refs, (out_hbm, out_ref, sems) = refs[:-3], refs[-3:]
-    visible = mixed_refs[0].shape[1]
+
+
+def spread_kernel(capacity, first, whole, info_ref, mixed_ref, out_hbm, out_ref, sems):
+    visible = mixed_ref.shape[1]
     members = info_ref.shape[0]
     devices = out_ref.shape[0]
     group = SEG // visible
@@ -387,49 +375,25 @@
     slots = devices * capacity
     lines = visible // 128
     wide = 2 * HDIM
-    units = [(ref, i) for ref in mixed_refs for i in range(ref.shape[0] // group)]
+    units = range(mixed_ref.shape[0] // group)
     step = math.gcd(slots, 256)
     low = lax.broadcasted_iota(jnp.int32, (step, wide), 1) < HDIM
-
-    def slots_of(source):
-        info = info_ref[source].astype(jnp.float32)
-        place = (info[:lines] * capacity + info[lines : 2 * lines]).astype(jnp.int32)
-        return jnp.concatenate([place[j : j + 1] for j in range(lines)], axis=1)
-
-    def rows_of(u, i):
-        ref, unit = units[u]
-        return ref[unit * group + i]
-
-    def segment_of(u):
-        return dealt_unit(segments, 0, len(units) - fixed, u - fixed)[1]
-
     jobs = []
-    if fixed:
-        for segment in range(segments):
-            for i in range(group):
-                others = [u for u in range(len(units)) if u >= fixed]
-                own = [u for u in range(fixed) if u % segments == segment]
-                right = [rows_of(u, i) for u in own]
-                right += [
-                    jnp.where(segment_of(u) == segment, rows_of(u, i), jnp.zeros((visible, wide), jnp.bfloat16))
-                    for u in others
-                ]
-                jobs.append((i, own + others, slots_of(segment * group + i), jnp.concatenate(right, axis=1)))
-    else:
-        for u in range(len(units)):
-            for i in range(group):
-                jobs.append((i, [u], slots_of(segment_of(u) * group + i), rows_of(u, i)))
+    for u in units:
+        segment = u if whole else dealt_unit(segments, first, len(units), u)[1]
+        for i in range(group):
+            info = info_ref[segment * group + i].astype(jnp.float32)
+            place = (info[:lines] * capacity + info[lines : 2 * lines]).astype(jnp.int32)
+            place = jnp.concatenate([place[j : j + 1] for j in range(lines)], axis=1)
+            jobs.append((u, i, place, mixed_ref[u * group + i]))
 
     copies = []
     for start in range(0, slots, step):
         found = {}
-        for i, names, place, right in jobs:
+        for u, i, place, right in jobs:
             wanted = lax.broadcasted_iota(jnp.int32, (step, visible), 0) + start
-            result = dot(one_hot(wanted, place), right)
-            for j, u in enumerate(names):
-                piece = result[:, j * wide : (j + 1) * wide]
-                found[u, i] = found[u, i] + piece if (u, i) in found else piece
-        first, last = start // capacity, (start + step) // capacity
+            found[u, i] = dot(one_hot(wanted, place), right)
+        at, last = start // capacity, (start + step) // capacity
         for u in range(0, len(units), 2):
             base = u // 2 * group * capacity
             if u + 1 < len(units):
@@ -439,14 +403,15 @@
             for i, (left, right) in enumerate(pairs):
                 both = jnp.where(low, found[left], found[right]).astype(jnp.bfloat16)
                 both = both.reshape(step // capacity, capacity, wide)
-                out_ref[first:last, base + i * capacity : base + (i + 1) * capacity, :] = both
-        copies.append(write(out_ref, out_hbm, first, last - first, sems))
+                out_ref[at:last, base + i * capacity : base + (i + 1) * capacity, :] = both
+        copies.append(write(out_ref, out_hbm, at, last - at, sems))
     for copy in copies:
         copy.wait()
 
 
-def finish_kernel(parts, capacity, slot_ref, back_ref, rows_hbm, gain_ref, w_hbm, out_hbm,
-                  attended_ref, rows_ref, w_ref, answer_ref, out_ref, more, sems):
+def finish_kernel(parts, capacity, slot_ref, rows_hbm, gain_ref, w_hbm, *refs):
+    back_refs, refs = refs[: len(parts)], refs[len(parts) :]
+    out_hbm, attended_ref, rows_ref, w_ref, answer_ref, out_ref, more, sems = refs
     fetches = [
         pltpu.make_async_copy(w_hbm, w_ref, more.at[0]),
         pltpu.make_async_copy(rows_hbm, rows_ref, more.at[1]),
@@ -455,23 +420,20 @@
         copy.start()
     slots, count = attended_ref.shape[0], out_ref.shape[0]
     members = len(parts[0][2])
-    groups = back_ref.shape[0] // members
+    groups = back_refs[0].shape[0] // members
     segments = 1 + max(segment for _, _, part in parts for _, units in part for _, segment in units)
     group = members // segments
-    total = sum(len(part[0][1]) for _, _, part in parts)
     where = {}
-    for member in range(members):
-        u = 0
-        for _, _, part in parts:
-            heads, units = part[member]
-            for place, segment in units:
-                where[heads[place], segment] = member, u
-                u += 1
+    for back_ref, (_, _, part) in zip(back_refs, parts):
+        for member, (heads, units) in enumerate(part):
+            for u, (place, segment) in enumerate(units):
+                alone = u + 1 == len(units) and u % 2 == 0
+                where[heads[place], segment] = back_ref, member, u, alone
 
     def piece(which, head, source):
-        member, u = where[head, source // group]
+        back_ref, member, u, alone = where[head, source // group]
         i, odd = source % group, u % 2
-        if u + 1 == total and total % 2:
+        if alone:
             i, odd = i % (group // 2), i // (group // 2)
         at = u // 2 * group * capacity + i * capacity
         return back_ref[which * members + member, at : at + capacity, :], odd
@@ -553,7 +515,7 @@
         (jax.ShapeDtypeStruct((slots, width), bf16), jax.ShapeDtypeStruct((1, count), jnp.int32)),
         (IN_HBM, IN_VMEM),
         "pack",
-        dest_table.reshape(1, count),
+        dest_table.reshape(count // 128, 128),
         tiles,
         in_specs=[IN_VMEM, IN_HBM],
         scratch=[
@@ -623,7 +585,7 @@
         blocks[i] = lax.all_to_all(send, inside, split_axis=0, concat_axis=0, tiled=True)
         before = i
 
-    mixed, infos = {}, []
+    backs, infos = {}, []
     for i in sequence:
         part = parts[i]
         units = len(part[2][0][1])
@@ -636,48 +598,46 @@
         if shares(part):
             partners = [(member, member ^ 1) for member in range(members)]
             operands.append(lax.ppermute(blocks[i], inside, partners))
-        mixed[i], *info = call(
-            functools.partial(attend_kernel, visible, part, i < HEADS // members, staged),
+        mixed, *info = call(
+            functools.partial(attend_kernel, visible, part, i < HEADS // members),
             outs,
-            [IN_HBM if staged else IN_VMEM] + [IN_VMEM] * (len(outs) - 1),
+            [IN_VMEM] * len(outs),
             "attend",
             *operands,
             scratch=[
                 pltpu.VMEM((2, depth, SEG // CLASSES), jnp.float32),
                 pltpu.VMEM((2, 8, SEG // CLASSES), jnp.float32),
-                pltpu.VMEM(outs[0].shape, bf16) if staged else None,
-                COPIES((units,)) if staged else None,
                 pltpu.VMEM((members, visible + visible // 2, 2 * HDIM), bf16) if shares(part) else None,
             ],
         )
         infos += info
-    mixed = [mixed[i] for i in range(len(parts))]
-
-    fixed = HEADS // members * segments
-    units_each = HEADS * segments // members
-    shape = jax.ShapeDtypeStruct((devices, units_each * group * capacity // 2, 2 * HDIM), bf16)
-    answers = call(
-        functools.partial(spread_kernel, capacity, fixed),
-        shape,
-        IN_HBM,
-        "spread",
-        infos[0],
-        *mixed,
-        in_specs=[IN_VMEM] * (1 + len(mixed)),
-        scratch=[pltpu.VMEM(shape.shape, bf16), COPIES((slots // math.gcd(slots, 256),))],
-    )
-    back = lax.all_to_all(answers, axes, split_axis=0, concat_axis=0, tiled=True)
+        shape = jax.ShapeDtypeStruct((devices, units * group * capacity // 2, 2 * HDIM), bf16)
+        answers = call(
+            functools.partial(spread_kernel, capacity, part[0], i < HEADS // members),
+            shape,
+            IN_HBM,
+            "spread",
+            infos[0],
+            mixed,
+            scratch=[pltpu.VMEM(shape.shape, bf16), COPIES((slots // math.gcd(slots, 256),))],
+        )
+        if staged:
+            after = sequence[sequence.index(i) + 1]
+            blocks[after], answers, infos[0] = lax.optimization_barrier((blocks[after], answers, infos[0]))
+        backs[i] = lax.all_to_all(answers, axes, split_axis=0, concat_axis=0, tiled=True)
+    backs = [backs[i] for i in range(len(parts))]
+
     return call(
         functools.partial(finish_kernel, parts, capacity),
         jax.ShapeDtypeStruct((count, width), bf16),
         IN_HBM,
         "finish",
         send_slot,
-        back,
         outgoing,
         gain_out[None, :],
         w_out,
-        in_specs=[IN_VMEM, IN_VMEM, IN_HBM, IN_VMEM, IN_HBM],
+        *backs,
+        in_specs=[IN_VMEM, IN_HBM, IN_VMEM, IN_HBM] + [IN_VMEM] * len(backs),
         scratch=[
             pltpu.VMEM((slots, width), bf16),
             pltpu.VMEM((slots, width), bf16),

time: 160 us -> 154 us (0.963)
  waiting for transfers between devices: 92.2 us -> 79.8 us
  starting transfers between devices: 18.6 us -> 24.4 us
    all_to_all x1 -> x2, waiting for transfers between devices: 37.7 us -> 26.2 us  [on_device(): lax.all_to_all(answers, axes, split_axis=0, concat_axis=0, tiled=True)]
    all_to_all x1 -> x2, starting transfers between devices: 2.7 us -> 8.45 us  [on_device(): lax.all_to_all(answers, axes, split_axis=0, concat_axis=0, tiled=True)]
    pallas_call x7 -> x8, Pallas kernels: 43.9 us -> 44.7 us  [call(): pl.pallas_call(kernel, out_shape=outs, in_specs=in_specs, out_specs=out_s...]
  transfers between devices with their start and end apart: 6 -> 7, of which waited for: 5 -> 5; matrix products, arithmetic and copies ran while one was open for 2% -> 2% of each run, Pallas kernels for 8% -> 19%
where the time goes in v6:
time: 154 us
  waiting for transfers between devices  79.8 us (52%)
  Pallas kernels  44.7 us (29%)
  starting transfers between devices  24.4 us (16%)
  local copies, waits for them, and re-layouts  4.07 us (3%)
    pallas_call x8, Pallas kernels, call(): pl.pallas_call(kernel, out_shape=outs, in_specs=in_specs, out_specs=out_s...  44.7 us
    all_to_all x1, waiting for transfers between devices, on_device(): lax.all_to_all(outgoing.reshape(devices, capacity, width), axes, split_ax...  33.2 us
    all_to_all x2, waiting for transfers between devices, on_device(): lax.all_to_all(answers, axes, split_axis=0, concat_axis=0, tiled=True)  26.2 us
    all_to_all x2, waiting for transfers between devices, on_device(): lax.all_to_all(send, inside, split_axis=0, concat_axis=0, tiled=True)  18.1 us
    all_to_all x2, starting transfers between devices, on_device(): lax.all_to_all(answers, axes, split_axis=0, concat_axis=0, tiled=True)  8.45 us
    all_to_all x2, starting transfers between devices, on_device(): lax.all_to_all(send, inside, split_axis=0, concat_axis=0, tiled=True)  7.51 us
    all_to_all x1, starting transfers between devices, on_device(): lax.all_to_all(outgoing.reshape(devices, capacity, width), axes, split_ax...  7.33 us
  transfers between devices with their start and end apart: 7, of which 5 were waited for; matrix products, arithmetic and copies ran while one was open for 2% of the time, Pallas kernels for 19%

profile of v6, /device:TPU:0, one launch (start us, length us, event | category | flops | bytes accessed | tf_op | source)
XLA Modules:
  0.0 153.7 jit_solution(4515066149772337399)
XLA Ops:
  0.0 0.7 copy-done.1
  0.7 4.6 %pack.1 = (bf16[1024,768]{1,0:T(8,128)(2,1)}, s32[1,1280]{1,0:T(1,128)S(1)}) custom-call(s32[10,128]{1,0:T(8,128)S(1)} %bitcast.12, bf16[1280,768]{1,0:T(8,128)(2,1)} %tiles_hbm.1), custom_call_target="tpu_custom_call" | custom-call | tf_op jit(solution)/shard_map/pack/pallas_call | solution.py:482
  5.3 7.3 %all-to-all-start = ((bf16[32,32,768]{2,1,0:T(8,128)(2,1)}), bf16[32,32,768]{2,1,0:T(8,128)(2,1)S(1)}, u32[]{:S(2)}, u32[]{:S(2)}) async-start(bf16[32,32,768]{2,1,0:T(8,128)(2,1)} %bitcast.15), calls=%async_computation | async-start | bytes 3145728 | tf_op jit(solution)/shard_map/all_to_all | solution.py:528
  12.6 0.7 collective-permute-start
  13.3 1.4 slice.3
  14.6 0.0 copy-start.2
  14.7 1.4 copy.28
  16.1 0.1 reshape_reshape.3
  16.2 0.1 copy.26
  16.3 0.1 div.32
  16.4 0.1 div.30
  16.5 0.1 and.34
  16.5 0.1 and.31
  16.6 0.1 reshape.123
  16.7 0.3 convert_reduce_fusion
  17.1 33.2 %all-to-all-done = bf16[32,32,768]{2,1,0:T(8,128)(2,1)S(1)} async-done(((bf16[32,32,768]{2,1,0:T(8,128)(2,1)}), bf16[32,32,768]{2,1,0:T(8,128)(2,1)S(1)}, u32[]{:S(2)}, u32[]{:S(2)}) %all-to-all-start) | async-done | bytes 1572896 | tf_op jit(solution)/shard_map/all_to_all | solution.py:528
  50.3 4.5 %project_first.1 = (bf16[512,768]{1,0:T(8,128)(2,1)}, bf16[8,400,128]{2,1,0:T(8,128)(2,1)}) custom-call(s32[1,512]{1,0:T(1,128)S(1)} %fusion.5.slot_ref, bf16[16,128]{1,0:T(8,128)(2,1)S(1)} %fusion.2.extra_ref, bf16[1024,768]{1,0:T(8,128)(2,1)S(1)} %bitcast.11, f32[1,768]{1,0:T(1,128)S(1)} %broadcast_in_dim.10.gain_ref, bf16[768,2304]{1,0:T(8,128)(2,1)} %w_hbm.4, ...), custom_call_target="tpu_custom_call" | custom-call | tf_op jit(solution)/shard_map/project_first/pallas_call | solution.py:482
  54.9 3.9 %all-to-all-start.1 = ((bf16[8,400,128]{2,1,0:T(8,128)(2,1)}), bf16[8,400,128]{2,1,0:T(8,128)(2,1)S(1)}, u32[]{:S(2)}, u32[]{:S(2)}) async-start(bf16[8,400,128]{2,1,0:T(8,128)(2,1)} %get-tuple-element.18), calls=%async_computation.1 | async-start | bytes 1638400 | tf_op jit(solution)/shard_map/all_to_all | solution.py:585
  58.8 4.3 %project_next.1 = bf16[8,768,128]{2,1,0:T(8,128)(2,1)} custom-call(bf16[512,768]{1,0:T(8,128)(2,1)S(1)} %copy-done, bf16[768,2304]{1,0:T(8,128)(2,1)} %w_hbm.4, bf16[768,768]{1,0:T(8,128)(2,1)} %bitcast.14), custom_call_target="tpu_custom_call" | custom-call | tf_op jit(solution)/shard_map/project_next/pallas_call | solution.py:482
  63.2 8.6 %all-to-all-done.1.refs_0_ = bf16[8,400,128]{2,1,0:T(8,128)(2,1)S(1)} async-done(((bf16[8,400,128]{2,1,0:T(8,128)(2,1)}), bf16[8,400,128]{2,1,0:T(8,128)(2,1)S(1)}, u32[]{:S(2)}, u32[]{:S(2)}) %all-to-all-start.1) | async-done | bytes 819232 | tf_op jit(solution)/shard_map/all_to_all | solution.py:585
  71.7 3.6 %all-to-all-start.2 = ((bf16[8,768,128]{2,1,0:T(8,128)(2,1)}), bf16[8,768,128]{2,1,0:T(8,128)(2,1)S(1)}, u32[]{:S(2)}, u32[]{:S(2)}) async-start(bf16[8,768,128]{2,1,0:T(8,128)(2,1)} %project_next.1), calls=%async_computation.2 | async-start | bytes 3145728 | tf_op jit(solution)/shard_map/all_to_all | solution.py:585
  75.3 0.4 collective-permute-start.1
  75.7 2.3 %collective-permute-done.1.refs_1_ = bf16[8,400,128]{2,1,0:T(8,128)(2,1)S(1)} collective-permute-done((bf16[8,400,128]{2,1,0:T(8,128)(2,1)S(1)}, bf16[8,400,128]{2,1,0:T(8,128)(2,1)S(1)}, u32[]{:S(2)}, u32[]{:S(2)}) %collective-permute-start.1) | collective-permute-done | bytes 819232 | tf_op jit(solution)/shard_map/ppermute | solution.py:600
  78.0 6.8 %attend.2 = (bf16[4,512,128]{2,1,0:T(8,128)(2,1)S(1)}, bf16[8,16,128]{2,1,0:T(8,128)(2,1)S(1)}) custom-call(bf16[8,400,128]{2,1,0:T(8,128)(2,1)S(1)} %all-to-all-done.1.refs_0_, bf16[8,400,128]{2,1,0:T(8,128)(2,1)S(1)} %collective-permute-done.1.refs_1_), custom_call_target="tpu_custom_call" | custom-call | tf_op jit(solution)/shard_map/attend/pallas_call | solution.py:482
  84.8 1.9 %spread.2 = bf16[32,64,128]{2,1,0:T(8,128)(2,1)} custom-call(bf16[8,16,128]{2,1,0:T(8,128)(2,1)S(1)} %get-tuple-element.24.info_ref, bf16[4,512,128]{2,1,0:T(8,128)(2,1)S(1)} %get-tuple-element.23.mixed_ref), custom_call_target="tpu_custom_call" | custom-call | tf_op jit(solution)/shard_map/spread/pallas_call | solution.py:482
  86.7 9.5 %all-to-all-done.2.refs_0_ = bf16[8,768,128]{2,1,0:T(8,128)(2,1)S(1)} async-done(((bf16[8,768,128]{2,1,0:T(8,128)(2,1)}), bf16[8,768,128]{2,1,0:T(8,128)(2,1)S(1)}, u32[]{:S(2)}, u32[]{:S(2)}) %all-to-all-start.2) | async-done | bytes 1572896 | tf_op jit(solution)/shard_map/all_to_all | solution.py:585
  96.2 2.8 %all-to-all-start.4 = ((bf16[32,64,128]{2,1,0:T(8,128)(2,1)}), bf16[32,64,128]{2,1,0:T(8,128)(2,1)S(1)}, u32[]{:S(2)}, u32[]{:S(2)}) async-start(bf16[32,64,128]{2,1,0:T(8,128)(2,1)} %spread.2), calls=%async_computation.4 | async-start | bytes 1048576 | tf_op jit(solution)/shard_map/all_to_all | solution.py:627
  99.0 12.7 %attend.3.mixed_ref = bf16[8,512,128]{2,1,0:T(8,128)(2,1)S(1)} custom-call(bf16[8,768,128]{2,1,0:T(8,128)(2,1)S(1)} %all-to-all-done.2.refs_0_), custom_call_target="tpu_custom_call" | custom-call | tf_op jit(solution)/shard_map/attend/pallas_call | solution.py:482
  111.7 3.1 %spread.3 = bf16[32,128,128]{2,1,0:T(8,128)(2,1)} custom-call(bf16[8,16,128]{2,1,0:T(8,128)(2,1)S(1)} %get-tuple-element.24.info_ref, bf16[8,512,128]{2,1,0:T(8,128)(2,1)S(1)} %attend.3.mixed_ref), custom_call_target="tpu_custom_call" | custom-call | tf_op jit(solution)/shard_map/spread/pallas_call | solution.py:482
  114.9 5.7 %all-to-all-start.3 = ((bf16[32,128,128]{2,1,0:T(8,128)(2,1)}), bf16[32,128,128]{2,1,0:T(8,128)(2,1)S(1)}, u32[]{:S(2)}, u32[]{:S(2)}) async-start(bf16[32,128,128]{2,1,0:T(8,128)(2,1)} %spread.3), calls=%async_computation.3 | async-start | bytes 2097152 | tf_op jit(solution)/shard_map/all_to_all | solution.py:627
  120.6 26.2 %all-to-all-done.3.refs_0_ = bf16[32,128,128]{2,1,0:T(8,128)(2,1)S(1)} async-done(((bf16[32,128,128]{2,1,0:T(8,128)(2,1)}), bf16[32,128,128]{2,1,0:T(8,128)(2,1)S(1)}, u32[]{:S(2)}, u32[]{:S(2)}) %all-to-all-start.3) | async-done | bytes 1048608 | tf_op jit(solution)/shard_map/all_to_all | solution.py:627
  146.7 6.7 %finish.1 = bf16[1280,768]{1,0:T(8,128)(2,1)} custom-call(s32[1,1280]{1,0:T(1,128)S(1)} %get-tuple-element.16.slot_ref, bf16[1024,768]{1,0:T(8,128)(2,1)} %get-tuple-element.17.rows_hbm, f32[1,768]{1,0:T(1,128)S(1)} %broadcast_in_dim.4.gain_ref, bf16[768,768]{1,0:T(8,128)(2,1)} %w_hbm.5, bf16[32,128,128]{2,1,0:T(8,128)(2,1)S(1)} %all-to-all-done.3.refs_0_, ...), custom_call_target="tpu_custom_call" | custom-call | tf_op jit(solution)/shard_map/finish/pallas_call | solution.py:482
  (19 shorter events, 0.1 us)
Async XLA Ops:
  0.0 0.7 copy-start.1
  5.3 7.4 %copy-start.4 = (s32[1,512]{1,0:T(1,128)S(1)}, s32[1,512]{1,0:T(1,128)}, u32[]{:S(2)}) copy-start(s32[1,512]{1,0:T(1,128)} %param.9) | copy-start | bytes 6148
  5.3 45.0 %all-to-all-start = ((bf16[32,32,768]{2,1,0:T(8,128)(2,1)}), bf16[32,32,768]{2,1,0:T(8,128)(2,1)S(1)}, u32[]{:S(2)}, u32[]{:S(2)}) async-start(bf16[32,32,768]{2,1,0:T(8,128)(2,1)} %bitcast.15), calls=%async_computation | async-start | bytes 3145728 | tf_op jit(solution)/shard_map/all_to_all | solution.py:528
  12.6 3.5 %collective-permute-start = (s32[4,128]{1,0:T(4,128)S(1)}, s32[4,128]{1,0:T(4,128)S(1)}, u32[]{:S(2)}, u32[]{:S(2)}) collective-permute-start(s32[4,128]{1,0:T(4,128)S(1)} %bitcast.18), channel_id=1, source_target_pairs={{0,0},{4,1},{8,2},{12,3},{16,4},{20,5},{24,6},{28,7},{1,8},{5,9},{... | collective-permute-start | bytes 6152 | tf_op jit(solution)/shard_map/ppermute | solution.py:510
  14.6 1.5 copy-start.2
  54.9 3.9 %copy-start = (bf16[512,768]{1,0:T(8,128)(2,1)S(1)}, bf16[512,768]{1,0:T(8,128)(2,1)}, u32[]{:S(2)}) copy-start(bf16[512,768]{1,0:T(8,128)(2,1)} %get-tuple-element.19.normed_ref) | copy-start | bytes 2359300
  54.9 16.9 %all-to-all-start.1 = ((bf16[8,400,128]{2,1,0:T(8,128)(2,1)}), bf16[8,400,128]{2,1,0:T(8,128)(2,1)S(1)}, u32[]{:S(2)}, u32[]{:S(2)}) async-start(bf16[8,400,128]{2,1,0:T(8,128)(2,1)} %get-tuple-element.18), calls=%async_computation.1 | async-start | bytes 1638400 | tf_op jit(solution)/shard_map/all_to_all | solution.py:585
  71.7 24.5 %all-to-all-start.2 = ((bf16[8,768,128]{2,1,0:T(8,128)(2,1)}), bf16[8,768,128]{2,1,0:T(8,128)(2,1)S(1)}, u32[]{:S(2)}, u32[]{:S(2)}) async-start(bf16[8,768,128]{2,1,0:T(8,128)(2,1)} %project_next.1), calls=%async_computation.2 | async-start | bytes 3145728 | tf_op jit(solution)/shard_map/all_to_all | solution.py:585
  75.3 2.7 %collective-permute-start.1 = (bf16[8,400,128]{2,1,0:T(8,128)(2,1)S(1)}, bf16[8,400,128]{2,1,0:T(8,128)(2,1)S(1)}, u32[]{:S(2)}, u32[]{:S(2)}) collective-permute-start(bf16[8,400,128]{2,1,0:T(8,128)(2,1)S(1)} %all-to-all-done.1.refs_0_), channel_id=1, source_target_pairs={{0,1},{1,0},{2,3},{3,2},{4,5},{5,4},{6,7},{7,6},{8,9},{9,8},{10,11... | collective-permute-start | bytes 2457608 | tf_op jit(solution)/shard_map/ppermute | solution.py:600
  96.2 18.6 %all-to-all-start.4 = ((bf16[32,64,128]{2,1,0:T(8,128)(2,1)}), bf16[32,64,128]{2,1,0:T(8,128)(2,1)S(1)}, u32[]{:S(2)}, u32[]{:S(2)}) async-start(bf16[32,64,128]{2,1,0:T(8,128)(2,1)} %spread.2), calls=%async_computation.4 | async-start | bytes 1048576 | tf_op jit(solution)/shard_map/all_to_all | solution.py:627
  114.8 5.7 %copy-start.3 = (f32[768]{0:T(1024)S(1)}, f32[768]{0:T(1024)}, u32[]{:S(2)}) copy-start(f32[768]{0:T(1024)} %param.13) | copy-start | bytes 9220
  114.9 31.9 %all-to-all-start.3 = ((bf16[32,128,128]{2,1,0:T(8,128)(2,1)}), bf16[32,128,128]{2,1,0:T(8,128)(2,1)S(1)}, u32[]{:S(2)}, u32[]{:S(2)}) async-start(bf16[32,128,128]{2,1,0:T(8,128)(2,1)} %spread.3), calls=%async_computation.3 | async-start | bytes 2097152 | tf_op jit(solution)/shard_map/all_to_all | solution.py:627

commit v7 on v6

--- a/solution.py
+++ b/solution.py
@@ -97,12 +97,22 @@
     return lax.dot_general(left, right, (((1,), (1,)), ((), ())), preferred_element_type=jnp.float32)
 
 
-def pack_kernel(visible, capacity, dest_ref, tiles_hbm, out_hbm, slot_ref, tiles_ref, out_ref, sem, sems):
-    fetch = pltpu.make_async_copy(tiles_hbm, tiles_ref, sem)
-    fetch.start()
+def pack_kernel(visible, capacity, dest_hbm, tiles_hbm, out_hbm, slot_ref, dest_ref, tiles_ref, out_ref, more, sems):
+    width = tiles_ref.shape[1]
+    spans = [(0, width // 3), (width // 3, width)]
+    table = pltpu.make_async_copy(dest_hbm, dest_ref, more.at[0])
+    fetches = [
+        pltpu.make_async_copy(
+            tiles_hbm.at[:, pl.ds(low, high - low)], tiles_ref.at[:, pl.ds(low, high - low)], more.at[1 + i]
+        )
+        for i, (low, high) in enumerate(spans)
+    ]
+    for copy in [table, *fetches]:
+        copy.start()
     slots, _ = out_ref.shape
     count = dest_ref.shape[0] * 128
     devices = slots // capacity
+    table.wait()
     target = jnp.right_shift(dest_ref[...], visible.bit_length() - 1)
     lanes = 128
     before = one_hot_lt(lanes)
@@ -118,14 +128,16 @@
         offset = offset + jnp.sum(chosen, axis=1, keepdims=True)
     slot = jnp.concatenate(pieces, axis=1)
     slot_ref[...] = slot
-    fetch.wait()
     step = math.gcd(slots, 256)
     copies = []
-    for start in range(0, slots, step):
-        wanted = lax.broadcasted_iota(jnp.int32, (step, count), 0) + start
-        rows = dot(one_hot(wanted, slot), tiles_ref[...])
-        out_ref[start : start + step, :] = rows.astype(jnp.bfloat16)
-        copies.append(write(out_ref, out_hbm, start, step, sems))
+    for fetch, (low, high) in zip(fetches, spans):
+        fetch.wait()
+        for start in range(0, slots, step):
+            wanted = lax.broadcasted_iota(jnp.int32, (step, count), 0) + start
+            rows = dot(one_hot(wanted, slot), tiles_ref[:, low:high])
+            out_ref[start : start + step, low:high] = rows.astype(jnp.bfloat16)
+            if high == width:
+                copies.append(write(out_ref, out_hbm, start, step, sems))
     for copy in copies:
         copy.wait()
 
@@ -245,7 +257,7 @@
     full_ref, own_ref = block_ref, block_ref
     if shares(part):
         *refs, full_ref = refs
-    *infos, score_ref, peak_ref = refs
+    *infos, score_ref, peak_ref, mixed_ref = refs
     for info_ref in infos:
         info_ref[...] = own_ref[:, depth_of(part, visible) :, :]
     if shares(part):
@@ -309,7 +321,7 @@
         peak_ref[half] = jnp.broadcast_to(jnp.max(peak, axis=0, keepdims=True), peak.shape)
         yield
 
-    def weight_steps(turn, half, results):
+    def weight_steps(turn, half):
         step, segment, cls, base = tile_of(turn, half)
         peak = peak_ref[half]
         odd = jnp.bitwise_and(cls, 1) == 1
@@ -342,28 +354,33 @@
             values = jnp.concatenate([values, jnp.ones((16, size), jnp.bfloat16)], axis=0)
             mixed += dot(values, jnp.concatenate(weights, axis=0))
             yield
-        results.append(mixed[:HDIM] / mixed[HDIM : HDIM + 1])
+        mixed_ref[lax.rem(turn, 2), half] = mixed
         yield
 
-    def run(*streams):
-        for _ in itertools.zip_longest(*streams):
-            pass
-
-    def body(turn, carry):
-        results = []
-        run(weight_steps(turn, 0, results), score_steps(turn, 1))
-        after = jnp.minimum(turn + 1, turns - 1)
-        run(weight_steps(turn, 1, results), score_steps(after, 0))
+    def finish_steps(turn):
         unit, step = turn // pairs, turn % pairs
-        for half, result in enumerate(results):
+        for half in range(2):
+            result = mixed_ref[lax.rem(turn, 2), half, :HDIM] / mixed_ref[lax.rem(turn, 2), half, HDIM : HDIM + 1]
             twice = jnp.concatenate([result, result], axis=0).T.astype(jnp.bfloat16)
             at = pl.multiple_of((2 * step + half) * rows, rows)
             for i in range(group):
                 out_ref[unit * group + i, pl.ds(at, rows), :] = twice[i * rows : (i + 1) * rows, :]
+            yield
+
+    def run(*streams):
+        for _ in itertools.zip_longest(*streams):
+            pass
+
+    mixed_ref[...] = jnp.ones_like(mixed_ref)
+
+    def body(turn, carry):
+        run(weight_steps(turn, 0), score_steps(turn, 1), finish_steps(jnp.maximum(turn - 1, 0)))
+        run(weight_steps(turn, 1), score_steps(jnp.minimum(turn + 1, turns - 1), 0))
         return carry
 
     run(score_steps(0, 0))
     lax.fori_loop(0, turns, body, 0)
+    run(finish_steps(turns - 1))
 
 
 def spread_kernel(capacity, first, whole, info_ref, mixed_ref, out_hbm, out_ref, sems):
@@ -517,11 +534,12 @@
         "pack",
         dest_table.reshape(count // 128, 128),
         tiles,
-        in_specs=[IN_VMEM, IN_HBM],
+        in_specs=[IN_HBM, IN_HBM],
         scratch=[
+            pltpu.VMEM((count // 128, 128), jnp.int32),
             pltpu.VMEM((count, width), bf16),
             pltpu.VMEM((slots, width), bf16),
-            COPIES,
+            COPIES((3,)),
             COPIES((slots // math.gcd(slots, 256),)),
         ],
     )
@@ -607,6 +625,7 @@
             scratch=[
                 pltpu.VMEM((2, depth, SEG // CLASSES), jnp.float32),
                 pltpu.VMEM((2, 8, SEG // CLASSES), jnp.float32),
+                pltpu.VMEM((2, 2, HDIM + 16, SEG // CLASSES), jnp.float32),
                 pltpu.VMEM((members, visible + visible // 2, 2 * HDIM), bf16) if shares(part) else None,
             ],
         )

time: 154 us -> 153 us (level)
  transfers between devices with their start and end apart: 7 -> 7, of which waited for: 5 -> 6; matrix products, arithmetic and copies ran while one was open for 2% -> 2% of each run, Pallas kernels for 19% -> 18%
where the time goes in v7:
time: 153 us; the launch traced here: 152 us
  waiting for transfers between devices  80.3 us (52%)
  Pallas kernels  43.5 us (28%)
  starting transfers between devices  24.1 us (16%)
  local copies, waits for them, and re-layouts  3.38 us (2%)
    pallas_call x8, Pallas kernels, call(): pl.pallas_call(kernel, out_shape=outs, in_specs=in_specs, out_specs=out_s...  43.5 us
    all_to_all x1, waiting for transfers between devices, on_device(): lax.all_to_all(outgoing.reshape(devices, capacity, width), axes, split_ax...  33.2 us
    all_to_all x2, waiting for transfers between devices, on_device(): lax.all_to_all(answers, axes, split_axis=0, concat_axis=0, tiled=True)  26.5 us
    all_to_all x2, waiting for transfers between devices, on_device(): lax.all_to_all(send, inside, split_axis=0, concat_axis=0, tiled=True)  18.3 us
    all_to_all x2, starting transfers between devices, on_device(): lax.all_to_all(answers, axes, split_axis=0, concat_axis=0, tiled=True)  8.18 us
    all_to_all x2, starting transfers between devices, on_device(): lax.all_to_all(send, inside, split_axis=0, concat_axis=0, tiled=True)  7.51 us
    all_to_all x1, starting transfers between devices, on_device(): lax.all_to_all(outgoing.reshape(devices, capacity, width), axes, split_ax...  7.33 us
  transfers between devices with their start and end apart: 7, of which 6 were waited for; matrix products, arithmetic and copies ran while one was open for 2% of the time, Pallas kernels for 18%

profile of v7, /device:TPU:0, one launch (start us, length us, event | category | flops | bytes accessed | tf_op | source)
XLA Modules:
  0.0 152.0 jit_solution(6272915500433763900)
XLA Ops:
  0.0 4.3 %pack.1 = (bf16[1024,768]{1,0:T(8,128)(2,1)}, s32[1,1280]{1,0:T(1,128)S(1)}) custom-call(s32[10,128]{1,0:T(8,128)} %bitcast.17, bf16[1280,768]{1,0:T(8,128)(2,1)} %tiles_hbm.1), custom_call_target="tpu_custom_call" | custom-call | tf_op jit(solution)/shard_map/pack/pallas_call | solution.py:499
  4.3 0.0 copy-start.3
  4.3 7.3 %all-to-all-start = ((bf16[32,32,768]{2,1,0:T(8,128)(2,1)}), bf16[32,32,768]{2,1,0:T(8,128)(2,1)S(1)}, u32[]{:S(2)}, u32[]{:S(2)}) async-start(bf16[32,32,768]{2,1,0:T(8,128)(2,1)} %bitcast.14), calls=%async_computation | async-start | bytes 3145728 | tf_op jit(solution)/shard_map/all_to_all | solution.py:546
  11.7 0.7 collective-permute-start
  12.3 1.4 slice.3
  13.7 1.5 copy.28
  15.2 0.1 reshape_reshape.3
  15.3 0.1 copy.26
  15.3 0.1 div.32
  15.4 0.1 div.30
  15.5 0.1 and.34
  15.6 0.1 and.31
  15.7 0.1 reshape.123
  15.8 0.3 convert_reduce_fusion
  16.2 33.2 %all-to-all-done = bf16[32,32,768]{2,1,0:T(8,128)(2,1)S(1)} async-done(((bf16[32,32,768]{2,1,0:T(8,128)(2,1)}), bf16[32,32,768]{2,1,0:T(8,128)(2,1)S(1)}, u32[]{:S(2)}, u32[]{:S(2)}) %all-to-all-start) | async-done | bytes 1572896 | tf_op jit(solution)/shard_map/all_to_all | solution.py:546
  49.4 4.5 %project_first.1 = (bf16[512,768]{1,0:T(8,128)(2,1)}, bf16[8,400,128]{2,1,0:T(8,128)(2,1)}) custom-call(s32[1,512]{1,0:T(1,128)S(1)} %fusion.5.slot_ref, bf16[16,128]{1,0:T(8,128)(2,1)S(1)} %fusion.2.extra_ref, bf16[1024,768]{1,0:T(8,128)(2,1)S(1)} %bitcast.11, f32[1,768]{1,0:T(1,128)S(1)} %broadcast_in_dim.10.gain_ref, bf16[768,2304]{1,0:T(8,128)(2,1)} %w_hbm.4, ...), custom_call_target="tpu_custom_call" | custom-call | tf_op jit(solution)/shard_map/project_first/pallas_call | solution.py:499
  53.9 3.9 %all-to-all-start.1 = ((bf16[8,400,128]{2,1,0:T(8,128)(2,1)}), bf16[8,400,128]{2,1,0:T(8,128)(2,1)S(1)}, u32[]{:S(2)}, u32[]{:S(2)}) async-start(bf16[8,400,128]{2,1,0:T(8,128)(2,1)} %get-tuple-element.18), calls=%async_computation.1 | async-start | bytes 1638400 | tf_op jit(solution)/shard_map/all_to_all | solution.py:603
  57.9 4.3 %project_next.1 = bf16[8,768,128]{2,1,0:T(8,128)(2,1)} custom-call(bf16[512,768]{1,0:T(8,128)(2,1)S(1)} %copy-done, bf16[768,2304]{1,0:T(8,128)(2,1)} %w_hbm.4, bf16[768,768]{1,0:T(8,128)(2,1)} %bitcast.13), custom_call_target="tpu_custom_call" | custom-call | tf_op jit(solution)/shard_map/project_next/pallas_call | solution.py:499
  62.2 8.6 %all-to-all-done.1.refs_0_ = bf16[8,400,128]{2,1,0:T(8,128)(2,1)S(1)} async-done(((bf16[8,400,128]{2,1,0:T(8,128)(2,1)}), bf16[8,400,128]{2,1,0:T(8,128)(2,1)S(1)}, u32[]{:S(2)}, u32[]{:S(2)}) %all-to-all-start.1) | async-done | bytes 819232 | tf_op jit(solution)/shard_map/all_to_all | solution.py:603
  70.8 3.6 %all-to-all-start.2 = ((bf16[8,768,128]{2,1,0:T(8,128)(2,1)}), bf16[8,768,128]{2,1,0:T(8,128)(2,1)S(1)}, u32[]{:S(2)}, u32[]{:S(2)}) async-start(bf16[8,768,128]{2,1,0:T(8,128)(2,1)} %project_next.1), calls=%async_computation.2 | async-start | bytes 3145728 | tf_op jit(solution)/shard_map/all_to_all | solution.py:603
  74.4 0.4 collective-permute-start.1
  74.8 2.3 %collective-permute-done.1.refs_1_ = bf16[8,400,128]{2,1,0:T(8,128)(2,1)S(1)} collective-permute-done((bf16[8,400,128]{2,1,0:T(8,128)(2,1)S(1)}, bf16[8,400,128]{2,1,0:T(8,128)(2,1)S(1)}, u32[]{:S(2)}, u32[]{:S(2)}) %collective-permute-start.1) | collective-permute-done | bytes 819232 | tf_op jit(solution)/shard_map/ppermute | solution.py:618
  77.1 6.5 %attend.2 = (bf16[4,512,128]{2,1,0:T(8,128)(2,1)S(1)}, bf16[8,16,128]{2,1,0:T(8,128)(2,1)S(1)}) custom-call(bf16[8,400,128]{2,1,0:T(8,128)(2,1)S(1)} %all-to-all-done.1.refs_0_, bf16[8,400,128]{2,1,0:T(8,128)(2,1)S(1)} %collective-permute-done.1.refs_1_), custom_call_target="tpu_custom_call" | custom-call | tf_op jit(solution)/shard_map/attend/pallas_call | solution.py:499
  83.6 1.9 %spread.2 = bf16[32,64,128]{2,1,0:T(8,128)(2,1)} custom-call(bf16[8,16,128]{2,1,0:T(8,128)(2,1)S(1)} %get-tuple-element.24.info_ref, bf16[4,512,128]{2,1,0:T(8,128)(2,1)S(1)} %get-tuple-element.23.mixed_ref), custom_call_target="tpu_custom_call" | custom-call | tf_op jit(solution)/shard_map/spread/pallas_call | solution.py:499
  85.5 9.7 %all-to-all-done.2.refs_0_ = bf16[8,768,128]{2,1,0:T(8,128)(2,1)S(1)} async-done(((bf16[8,768,128]{2,1,0:T(8,128)(2,1)}), bf16[8,768,128]{2,1,0:T(8,128)(2,1)S(1)}, u32[]{:S(2)}, u32[]{:S(2)}) %all-to-all-start.2) | async-done | bytes 1572896 | tf_op jit(solution)/shard_map/all_to_all | solution.py:603
  95.3 2.8 %all-to-all-start.4 = ((bf16[32,64,128]{2,1,0:T(8,128)(2,1)}), bf16[32,64,128]{2,1,0:T(8,128)(2,1)S(1)}, u32[]{:S(2)}, u32[]{:S(2)}) async-start(bf16[32,64,128]{2,1,0:T(8,128)(2,1)} %spread.2), calls=%async_computation.4 | async-start | bytes 1048576 | tf_op jit(solution)/shard_map/all_to_all | solution.py:646
  98.1 12.0 %attend.3.mixed_ref = bf16[8,512,128]{2,1,0:T(8,128)(2,1)S(1)} custom-call(bf16[8,768,128]{2,1,0:T(8,128)(2,1)S(1)} %all-to-all-done.2.refs_0_), custom_call_target="tpu_custom_call" | custom-call | tf_op jit(solution)/shard_map/attend/pallas_call | solution.py:499
  110.1 3.1 %spread.3 = bf16[32,128,128]{2,1,0:T(8,128)(2,1)} custom-call(bf16[8,16,128]{2,1,0:T(8,128)(2,1)S(1)} %get-tuple-element.24.info_ref, bf16[8,512,128]{2,1,0:T(8,128)(2,1)S(1)} %attend.3.mixed_ref), custom_call_target="tpu_custom_call" | custom-call | tf_op jit(solution)/shard_map/spread/pallas_call | solution.py:499
  113.2 0.3 all-to-all-done.4.refs_1_
  113.5 5.4 %all-to-all-start.3 = ((bf16[32,128,128]{2,1,0:T(8,128)(2,1)}), bf16[32,128,128]{2,1,0:T(8,128)(2,1)S(1)}, u32[]{:S(2)}, u32[]{:S(2)}) async-start(bf16[32,128,128]{2,1,0:T(8,128)(2,1)} %spread.3), calls=%async_computation.3 | async-start | bytes 2097152 | tf_op jit(solution)/shard_map/all_to_all | solution.py:646
  118.9 26.2 %all-to-all-done.3.refs_0_ = bf16[32,128,128]{2,1,0:T(8,128)(2,1)S(1)} async-done(((bf16[32,128,128]{2,1,0:T(8,128)(2,1)}), bf16[32,128,128]{2,1,0:T(8,128)(2,1)S(1)}, u32[]{:S(2)}, u32[]{:S(2)}) %all-to-all-start.3) | async-done | bytes 1048608 | tf_op jit(solution)/shard_map/all_to_all | solution.py:646
  145.1 6.7 %finish.1 = bf16[1280,768]{1,0:T(8,128)(2,1)} custom-call(s32[1,1280]{1,0:T(1,128)S(1)} %get-tuple-element.16.slot_ref, bf16[1024,768]{1,0:T(8,128)(2,1)} %get-tuple-element.17.rows_hbm, f32[1,768]{1,0:T(1,128)S(1)} %broadcast_in_dim.4.gain_ref, bf16[768,768]{1,0:T(8,128)(2,1)} %w_hbm.5, bf16[32,128,128]{2,1,0:T(8,128)(2,1)S(1)} %all-to-all-done.3.refs_0_, ...), custom_call_target="tpu_custom_call" | custom-call | tf_op jit(solution)/shard_map/finish/pallas_call | solution.py:499
  (17 shorter events, 0.1 us)
Async XLA Ops:
  4.3 7.4 %copy-start.3 = (s32[1,512]{1,0:T(1,128)S(1)}, s32[1,512]{1,0:T(1,128)}, u32[]{:S(2)}) copy-start(s32[1,512]{1,0:T(1,128)} %param.9) | copy-start | bytes 6148
  4.3 45.0 %all-to-all-start = ((bf16[32,32,768]{2,1,0:T(8,128)(2,1)}), bf16[32,32,768]{2,1,0:T(8,128)(2,1)S(1)}, u32[]{:S(2)}, u32[]{:S(2)}) async-start(bf16[32,32,768]{2,1,0:T(8,128)(2,1)} %bitcast.14), calls=%async_computation | async-start | bytes 3145728 | tf_op jit(solution)/shard_map/all_to_all | solution.py:546
  11.7 3.5 %collective-permute-start = (s32[4,128]{1,0:T(4,128)S(1)}, s32[4,128]{1,0:T(4,128)S(1)}, u32[]{:S(2)}, u32[]{:S(2)}) collective-permute-start(s32[4,128]{1,0:T(4,128)S(1)} %bitcast.18), channel_id=1, source_target_pairs={{0,0},{4,1},{8,2},{12,3},{16,4},{20,5},{24,6},{28,7},{1,8},{5,9},{... | collective-permute-start | bytes 6152 | tf_op jit(solution)/shard_map/ppermute | solution.py:527
  13.7 1.5 copy-start.1
  53.9 3.9 %copy-start = (bf16[512,768]{1,0:T(8,128)(2,1)S(1)}, bf16[512,768]{1,0:T(8,128)(2,1)}, u32[]{:S(2)}) copy-start(bf16[512,768]{1,0:T(8,128)(2,1)} %get-tuple-element.19.normed_ref) | copy-start | bytes 2359300
  53.9 16.8 %all-to-all-start.1 = ((bf16[8,400,128]{2,1,0:T(8,128)(2,1)}), bf16[8,400,128]{2,1,0:T(8,128)(2,1)S(1)}, u32[]{:S(2)}, u32[]{:S(2)}) async-start(bf16[8,400,128]{2,1,0:T(8,128)(2,1)} %get-tuple-element.18), calls=%async_computation.1 | async-start | bytes 1638400 | tf_op jit(solution)/shard_map/all_to_all | solution.py:603
  70.8 24.5 %all-to-all-start.2 = ((bf16[8,768,128]{2,1,0:T(8,128)(2,1)}), bf16[8,768,128]{2,1,0:T(8,128)(2,1)S(1)}, u32[]{:S(2)}, u32[]{:S(2)}) async-start(bf16[8,768,128]{2,1,0:T(8,128)(2,1)} %project_next.1), calls=%async_computation.2 | async-start | bytes 3145728 | tf_op jit(solution)/shard_map/all_to_all | solution.py:603
  74.4 2.7 %collective-permute-start.1 = (bf16[8,400,128]{2,1,0:T(8,128)(2,1)S(1)}, bf16[8,400,128]{2,1,0:T(8,128)(2,1)S(1)}, u32[]{:S(2)}, u32[]{:S(2)}) collective-permute-start(bf16[8,400,128]{2,1,0:T(8,128)(2,1)S(1)} %all-to-all-done.1.refs_0_), channel_id=1, source_target_pairs={{0,1},{1,0},{2,3},{3,2},{4,5},{5,4},{6,7},{7,6},{8,9},{9,8},{10,11... | collective-permute-start | bytes 2457608 | tf_op jit(solution)/shard_map/ppermute | solution.py:618
  95.3 18.2 %all-to-all-start.4 = ((bf16[32,64,128]{2,1,0:T(8,128)(2,1)}), bf16[32,64,128]{2,1,0:T(8,128)(2,1)S(1)}, u32[]{:S(2)}, u32[]{:S(2)}) async-start(bf16[32,64,128]{2,1,0:T(8,128)(2,1)} %spread.2), calls=%async_computation.4 | async-start | bytes 1048576 | tf_op jit(solution)/shard_map/all_to_all | solution.py:646
  113.2 5.7 %copy-start.2 = (f32[768]{0:T(1024)S(1)}, f32[768]{0:T(1024)}, u32[]{:S(2)}) copy-start(f32[768]{0:T(1024)} %param.13) | copy-start | bytes 9220
  113.5 31.6 %all-to-all-start.3 = ((bf16[32,128,128]{2,1,0:T(8,128)(2,1)}), bf16[32,128,128]{2,1,0:T(8,128)(2,1)S(1)}, u32[]{:S(2)}, u32[]{:S(2)}) async-start(bf16[32,128,128]{2,1,0:T(8,128)(2,1)} %spread.3), calls=%async_computation.3 | async-start | bytes 2097152 | tf_op jit(solution)/shard_map/all_to_all | solution.py:646

commit v8 on v7

--- a/solution.py
+++ b/solution.py
@@ -426,12 +426,11 @@
         copy.wait()
 
 
-def finish_kernel(parts, capacity, slot_ref, rows_hbm, gain_ref, w_hbm, *refs):
+def finish_kernel(parts, capacity, slot_ref, rows_hbm, gain_ref, w_ref, *refs):
     back_refs, refs = refs[: len(parts)], refs[len(parts) :]
-    out_hbm, attended_ref, rows_ref, w_ref, answer_ref, out_ref, more, sems = refs
+    out_hbm, attended_ref, rows_ref, answer_ref, out_ref, more, sems = refs
     fetches = [
-        pltpu.make_async_copy(w_hbm, w_ref, more.at[0]),
-        pltpu.make_async_copy(rows_hbm, rows_ref, more.at[1]),
+        pltpu.make_async_copy(rows_hbm, rows_ref, more.at[0]),
     ]
     for copy in fetches:
         copy.start()
@@ -656,14 +655,13 @@
         gain_out[None, :],
         w_out,
         *backs,
-        in_specs=[IN_VMEM, IN_HBM, IN_VMEM, IN_HBM] + [IN_VMEM] * len(backs),
+        in_specs=[IN_VMEM, IN_HBM, IN_VMEM, PINNED] + [IN_VMEM] * len(backs),
         scratch=[
             pltpu.VMEM((slots, width), bf16),
             pltpu.VMEM((slots, width), bf16),
-            pltpu.VMEM((width, width), bf16),
             pltpu.VMEM((slots, width), bf16),
             pltpu.VMEM((count, width), bf16),
-            COPIES((2,)),
+            COPIES((1,)),
             COPIES((count // math.gcd(count, 256),)),
         ],
     )

time: 153 us -> 152 us (level)
  no operation moved by 1% of the time
where the time goes in v8:
time: 152 us; the launch traced here: 151 us
  waiting for transfers between devices  81.6 us (54%)
  Pallas kernels  42.4 us (28%)
  starting transfers between devices  23.9 us (16%)
  local copies, waits for them, and re-layouts  2.48 us (2%)
    pallas_call x8, Pallas kernels, call(): pl.pallas_call(kernel, out_shape=outs, in_specs=in_specs, out_specs=out_s...  42.4 us
    all_to_all x1, waiting for transfers between devices, on_device(): lax.all_to_all(outgoing.reshape(devices, capacity, width), axes, split_ax...  34 us
    all_to_all x2, waiting for transfers between devices, on_device(): lax.all_to_all(answers, axes, split_axis=0, concat_axis=0, tiled=True)  26.8 us
    all_to_all x2, waiting for transfers between devices, on_device(): lax.all_to_all(send, inside, split_axis=0, concat_axis=0, tiled=True)  18.5 us
    all_to_all x2, starting transfers between devices, on_device(): lax.all_to_all(answers, axes, split_axis=0, concat_axis=0, tiled=True)  7.84 us
    all_to_all x2, starting transfers between devices, on_device(): lax.all_to_all(send, inside, split_axis=0, concat_axis=0, tiled=True)  7.51 us
    all_to_all x1, starting transfers between devices, on_device(): lax.all_to_all(outgoing.reshape(devices, capacity, width), axes, split_ax...  7.33 us
  transfers between devices with their start and end apart: 7, of which 6 were waited for; matrix products, arithmetic and copies ran while one was open for 2% of the time, Pallas kernels for 18%

profile of v8, /device:TPU:0, one launch (start us, length us, event | category | flops | bytes accessed | tf_op | source)
XLA Modules:
  0.0 151.2 jit_solution(14548754365008319562)
XLA Ops:
  0.0 4.3 %pack.1 = (bf16[1024,768]{1,0:T(8,128)(2,1)}, s32[1,1280]{1,0:T(1,128)S(1)}) custom-call(s32[10,128]{1,0:T(8,128)} %bitcast.17, bf16[1280,768]{1,0:T(8,128)(2,1)} %tiles_hbm.1), custom_call_target="tpu_custom_call" | custom-call | tf_op jit(solution)/shard_map/pack/pallas_call | solution.py:498
  4.3 7.3 %all-to-all-start = ((bf16[32,32,768]{2,1,0:T(8,128)(2,1)}), bf16[32,32,768]{2,1,0:T(8,128)(2,1)S(1)}, u32[]{:S(2)}, u32[]{:S(2)}) async-start(bf16[32,32,768]{2,1,0:T(8,128)(2,1)} %bitcast.14), calls=%async_computation | async-start | bytes 3145728 | tf_op jit(solution)/shard_map/all_to_all | solution.py:545
  11.6 0.0 slice-start
  11.7 0.8 collective-permute-start
  12.5 0.5 slice-done
  12.9 1.4 copy.28
  14.4 0.1 reshape_reshape.3
  14.5 0.1 copy.26
  14.5 0.1 div.32
  14.6 0.1 div.30
  14.7 0.1 and.34
  14.8 0.1 and.31
  14.9 0.1 reshape.123
  15.0 0.3 convert_reduce_fusion
  15.4 34.0 %all-to-all-done = bf16[32,32,768]{2,1,0:T(8,128)(2,1)S(1)} async-done(((bf16[32,32,768]{2,1,0:T(8,128)(2,1)}), bf16[32,32,768]{2,1,0:T(8,128)(2,1)S(1)}, u32[]{:S(2)}, u32[]{:S(2)}) %all-to-all-start) | async-done | bytes 1572896 | tf_op jit(solution)/shard_map/all_to_all | solution.py:545
  49.3 4.5 %project_first.1 = (bf16[512,768]{1,0:T(8,128)(2,1)}, bf16[8,400,128]{2,1,0:T(8,128)(2,1)}) custom-call(s32[1,512]{1,0:T(1,128)S(1)} %fusion.5.slot_ref, bf16[16,128]{1,0:T(8,128)(2,1)S(1)} %fusion.2.extra_ref, bf16[1024,768]{1,0:T(8,128)(2,1)S(1)} %bitcast.11, f32[1,768]{1,0:T(1,128)S(1)} %broadcast_in_dim.10.gain_ref, bf16[768,2304]{1,0:T(8,128)(2,1)} %w_hbm.3, ...), custom_call_target="tpu_custom_call" | custom-call | tf_op jit(solution)/shard_map/project_first/pallas_call | solution.py:498
  53.9 3.9 %all-to-all-start.1 = ((bf16[8,400,128]{2,1,0:T(8,128)(2,1)}), bf16[8,400,128]{2,1,0:T(8,128)(2,1)S(1)}, u32[]{:S(2)}, u32[]{:S(2)}) async-start(bf16[8,400,128]{2,1,0:T(8,128)(2,1)} %get-tuple-element.18), calls=%async_computation.1 | async-start | bytes 1638400 | tf_op jit(solution)/shard_map/all_to_all | solution.py:602
  57.8 4.3 %project_next.1 = bf16[8,768,128]{2,1,0:T(8,128)(2,1)} custom-call(bf16[512,768]{1,0:T(8,128)(2,1)S(1)} %copy-done.1, bf16[768,2304]{1,0:T(8,128)(2,1)} %w_hbm.3, bf16[768,768]{1,0:T(8,128)(2,1)} %bitcast.13), custom_call_target="tpu_custom_call" | custom-call | tf_op jit(solution)/shard_map/project_next/pallas_call | solution.py:498
  62.2 8.6 %all-to-all-done.1.refs_0_ = bf16[8,400,128]{2,1,0:T(8,128)(2,1)S(1)} async-done(((bf16[8,400,128]{2,1,0:T(8,128)(2,1)}), bf16[8,400,128]{2,1,0:T(8,128)(2,1)S(1)}, u32[]{:S(2)}, u32[]{:S(2)}) %all-to-all-start.1) | async-done | bytes 819232 | tf_op jit(solution)/shard_map/all_to_all | solution.py:602
  70.7 3.6 %all-to-all-start.2 = ((bf16[8,768,128]{2,1,0:T(8,128)(2,1)}), bf16[8,768,128]{2,1,0:T(8,128)(2,1)S(1)}, u32[]{:S(2)}, u32[]{:S(2)}) async-start(bf16[8,768,128]{2,1,0:T(8,128)(2,1)} %project_next.1), calls=%async_computation.2 | async-start | bytes 3145728 | tf_op jit(solution)/shard_map/all_to_all | solution.py:602
  74.3 0.4 collective-permute-start.1
  74.7 2.3 %collective-permute-done.1.refs_1_ = bf16[8,400,128]{2,1,0:T(8,128)(2,1)S(1)} collective-permute-done((bf16[8,400,128]{2,1,0:T(8,128)(2,1)S(1)}, bf16[8,400,128]{2,1,0:T(8,128)(2,1)S(1)}, u32[]{:S(2)}, u32[]{:S(2)}) %collective-permute-start.1) | collective-permute-done | bytes 819232 | tf_op jit(solution)/shard_map/ppermute | solution.py:617
  77.0 6.3 %attend.2 = (bf16[4,512,128]{2,1,0:T(8,128)(2,1)S(1)}, bf16[8,16,128]{2,1,0:T(8,128)(2,1)S(1)}) custom-call(bf16[8,400,128]{2,1,0:T(8,128)(2,1)S(1)} %all-to-all-done.1.refs_0_, bf16[8,400,128]{2,1,0:T(8,128)(2,1)S(1)} %collective-permute-done.1.refs_1_), custom_call_target="tpu_custom_call" | custom-call | tf_op jit(solution)/shard_map/attend/pallas_call | solution.py:498
  83.4 1.9 %spread.2 = bf16[32,64,128]{2,1,0:T(8,128)(2,1)} custom-call(bf16[8,16,128]{2,1,0:T(8,128)(2,1)S(1)} %get-tuple-element.24.info_ref, bf16[4,512,128]{2,1,0:T(8,128)(2,1)S(1)} %get-tuple-element.23.mixed_ref), custom_call_target="tpu_custom_call" | custom-call | tf_op jit(solution)/shard_map/spread/pallas_call | solution.py:498
  85.3 9.9 %all-to-all-done.2.refs_0_ = bf16[8,768,128]{2,1,0:T(8,128)(2,1)S(1)} async-done(((bf16[8,768,128]{2,1,0:T(8,128)(2,1)}), bf16[8,768,128]{2,1,0:T(8,128)(2,1)S(1)}, u32[]{:S(2)}, u32[]{:S(2)}) %all-to-all-start.2) | async-done | bytes 1572896 | tf_op jit(solution)/shard_map/all_to_all | solution.py:602
  95.2 2.8 %all-to-all-start.4 = ((bf16[32,64,128]{2,1,0:T(8,128)(2,1)}), bf16[32,64,128]{2,1,0:T(8,128)(2,1)S(1)}, u32[]{:S(2)}, u32[]{:S(2)}) async-start(bf16[32,64,128]{2,1,0:T(8,128)(2,1)} %spread.2), calls=%async_computation.4 | async-start | bytes 1048576 | tf_op jit(solution)/shard_map/all_to_all | solution.py:645
  98.0 11.7 %attend.3.mixed_ref = bf16[8,512,128]{2,1,0:T(8,128)(2,1)S(1)} custom-call(bf16[8,768,128]{2,1,0:T(8,128)(2,1)S(1)} %all-to-all-done.2.refs_0_), custom_call_target="tpu_custom_call" | custom-call | tf_op jit(solution)/shard_map/attend/pallas_call | solution.py:498
  109.7 3.1 %spread.3 = bf16[32,128,128]{2,1,0:T(8,128)(2,1)} custom-call(bf16[8,16,128]{2,1,0:T(8,128)(2,1)S(1)} %get-tuple-element.24.info_ref, bf16[8,512,128]{2,1,0:T(8,128)(2,1)S(1)} %attend.3.mixed_ref), custom_call_target="tpu_custom_call" | custom-call | tf_op jit(solution)/shard_map/spread/pallas_call | solution.py:498
  112.9 0.6 all-to-all-done.4.refs_1_
  113.5 5.1 %all-to-all-start.3 = ((bf16[32,128,128]{2,1,0:T(8,128)(2,1)}), bf16[32,128,128]{2,1,0:T(8,128)(2,1)S(1)}, u32[]{:S(2)}, u32[]{:S(2)}) async-start(bf16[32,128,128]{2,1,0:T(8,128)(2,1)} %spread.3), calls=%async_computation.3 | async-start | bytes 2097152 | tf_op jit(solution)/shard_map/all_to_all | solution.py:645
  118.6 26.2 %all-to-all-done.3.refs_0_ = bf16[32,128,128]{2,1,0:T(8,128)(2,1)S(1)} async-done(((bf16[32,128,128]{2,1,0:T(8,128)(2,1)}), bf16[32,128,128]{2,1,0:T(8,128)(2,1)S(1)}, u32[]{:S(2)}, u32[]{:S(2)}) %all-to-all-start.3) | async-done | bytes 1048608 | tf_op jit(solution)/shard_map/all_to_all | solution.py:645
  144.7 6.3 %finish.1 = bf16[1280,768]{1,0:T(8,128)(2,1)} custom-call(s32[1,1280]{1,0:T(1,128)S(1)} %get-tuple-element.16.slot_ref, bf16[1024,768]{1,0:T(8,128)(2,1)} %get-tuple-element.17.rows_hbm, f32[1,768]{1,0:T(1,128)S(1)} %broadcast_in_dim.4.gain_ref, bf16[768,768]{1,0:T(8,128)(2,1)S(1)} %copy-done, bf16[32,128,128]{2,1,0:T(8,128)(2,1)S(1)} %all-to-all-done.3.refs_0_, ...), custom_call_target="tpu_custom_call" | custom-call | tf_op jit(solution)/shard_map/finish/pallas_call | solution.py:498
  (20 shorter events, 0.1 us)
Async XLA Ops:
  4.3 7.4 %copy-start.4 = (s32[1,512]{1,0:T(1,128)S(1)}, s32[1,512]{1,0:T(1,128)}, u32[]{:S(2)}) copy-start(s32[1,512]{1,0:T(1,128)} %param.9) | copy-start | bytes 6148
  4.3 45.0 %all-to-all-start = ((bf16[32,32,768]{2,1,0:T(8,128)(2,1)}), bf16[32,32,768]{2,1,0:T(8,128)(2,1)S(1)}, u32[]{:S(2)}, u32[]{:S(2)}) async-start(bf16[32,32,768]{2,1,0:T(8,128)(2,1)} %bitcast.14), calls=%async_computation | async-start | bytes 3145728 | tf_op jit(solution)/shard_map/all_to_all | solution.py:545
  11.6 1.3 slice-start
  11.7 2.7 %collective-permute-start = (s32[4,128]{1,0:T(4,128)S(1)}, s32[4,128]{1,0:T(4,128)S(1)}, u32[]{:S(2)}, u32[]{:S(2)}) collective-permute-start(s32[4,128]{1,0:T(4,128)S(1)} %bitcast.18), channel_id=1, source_target_pairs={{0,0},{4,1},{8,2},{12,3},{16,4},{20,5},{24,6},{28,7},{1,8},{5,9},{... | collective-permute-start | bytes 6152 | tf_op jit(solution)/shard_map/ppermute | solution.py:526
  12.9 1.5 copy-start.2
  53.9 3.9 %copy-start.1 = (bf16[512,768]{1,0:T(8,128)(2,1)S(1)}, bf16[512,768]{1,0:T(8,128)(2,1)}, u32[]{:S(2)}) copy-start(bf16[512,768]{1,0:T(8,128)(2,1)} %get-tuple-element.19.normed_ref) | copy-start | bytes 2359300
  53.9 16.8 %all-to-all-start.1 = ((bf16[8,400,128]{2,1,0:T(8,128)(2,1)}), bf16[8,400,128]{2,1,0:T(8,128)(2,1)S(1)}, u32[]{:S(2)}, u32[]{:S(2)}) async-start(bf16[8,400,128]{2,1,0:T(8,128)(2,1)} %get-tuple-element.18), calls=%async_computation.1 | async-start | bytes 1638400 | tf_op jit(solution)/shard_map/all_to_all | solution.py:602
  70.7 24.5 %all-to-all-start.2 = ((bf16[8,768,128]{2,1,0:T(8,128)(2,1)}), bf16[8,768,128]{2,1,0:T(8,128)(2,1)S(1)}, u32[]{:S(2)}, u32[]{:S(2)}) async-start(bf16[8,768,128]{2,1,0:T(8,128)(2,1)} %project_next.1), calls=%async_computation.2 | async-start | bytes 3145728 | tf_op jit(solution)/shard_map/all_to_all | solution.py:602
  74.3 2.7 %collective-permute-start.1 = (bf16[8,400,128]{2,1,0:T(8,128)(2,1)S(1)}, bf16[8,400,128]{2,1,0:T(8,128)(2,1)S(1)}, u32[]{:S(2)}, u32[]{:S(2)}) collective-permute-start(bf16[8,400,128]{2,1,0:T(8,128)(2,1)S(1)} %all-to-all-done.1.refs_0_), channel_id=1, source_target_pairs={{0,1},{1,0},{2,3},{3,2},{4,5},{5,4},{6,7},{7,6},{8,9},{9,8},{10,11... | collective-permute-start | bytes 2457608 | tf_op jit(solution)/shard_map/ppermute | solution.py:617
  95.2 18.2 %all-to-all-start.4 = ((bf16[32,64,128]{2,1,0:T(8,128)(2,1)}), bf16[32,64,128]{2,1,0:T(8,128)(2,1)S(1)}, u32[]{:S(2)}, u32[]{:S(2)}) async-start(bf16[32,64,128]{2,1,0:T(8,128)(2,1)} %spread.2), calls=%async_computation.4 | async-start | bytes 1048576 | tf_op jit(solution)/shard_map/all_to_all | solution.py:645
  112.8 5.7 %copy-start.3 = (f32[768]{0:T(1024)S(1)}, f32[768]{0:T(1024)}, u32[]{:S(2)}) copy-start(f32[768]{0:T(1024)} %param.13) | copy-start | bytes 9220
  112.8 31.9 %copy-start = (bf16[768,768]{1,0:T(8,128)(2,1)S(1)}, bf16[768,768]{1,0:T(8,128)(2,1)}, u32[]{:S(2)}) copy-start(bf16[768,768]{1,0:T(8,128)(2,1)} %w_ref.1) | copy-start | bytes 3538948
  113.5 31.3 %all-to-all-start.3 = ((bf16[32,128,128]{2,1,0:T(8,128)(2,1)}), bf16[32,128,128]{2,1,0:T(8,128)(2,1)S(1)}, u32[]{:S(2)}, u32[]{:S(2)}) async-start(bf16[32,128,128]{2,1,0:T(8,128)(2,1)} %spread.3), calls=%async_computation.3 | async-start | bytes 2097152 | tf_op jit(solution)/shard_map/all_to_all | solution.py:645
